TPU v7x, 256 devices: a whole 4x4x8 slice. The times are simulated.
256 devices in a mesh: shot: 32 (over z_hi, y, x), space: 8 (over z_lo, core).
Axes of the slice: x: 4, y: 4, z: 8 (z_hi: 2, z_lo: 4; z = z_hi * 4 + z_lo), core: 2. Of those that a mesh axis runs over, the one named last changes fastest.
Arguments:
- velocity: float32 [1024, 2048], P('space'), may hold values from 1.5 to 4.5
- encoder_weight: float32 [4, 4, 64], replicated, may hold values from -1.5 to 1.5
- encoder_bias: float32 [64], replicated, may hold values from -3 to 3
- source_amplitude: float32 [64], replicated, may hold values from -12 to 12
- source_row: int32 [128], P('shot'), may hold values from 0 to 255
- source_column: int32 [128], P('shot'), may hold values from 0 to 511
- receiver_rows: int32 [128, 16], P('shot'), may hold values from 0 to 255
- point_weight: bfloat16 [64, 64], replicated, may hold values from -0.75 to 0.75
- spectral_weight: bfloat16 [48, 24, 64, 128], P(None, 'space'), may hold values from -1.5 to 1.5
- layer_bias: float32 [64], replicated, may hold values from -3 to 3
- out_weight: float32 [64], replicated, may hold values from -0.75 to 0.75
- observed: float32 [128, 16, 512], P('shot'), may hold values from -6 to 6
Outputs:
- misfit: float32 [128], P('shot')
- velocity_gradient: float32 [1024, 2048], P('space', 'shot')
Inputs may be any that keep to these rules, and one draw needn't show every extreme that they name: `receiver_rows`: receivers of one shot may share a row.
All inputs are finite; a program needn't handle non-finite values.
Results may differ from a plain program's by a relative error of at most 0.0065.
Values may be sent and summed in bfloat16 or wider, within the bound.
No kernel may reach another device: no remote copies, remote signals or barrier semaphores. Data moves between devices by JAX's collectives and lax.ppermute only.
A program may use at most 128 MiB of HBM per device.

v0:
```python
import math

import jax
import jax.numpy as jnp
from jax import lax
from jax.sharding import PartitionSpec as P

KX = 48
KY = 24
GH = 256
GW = 512


VELOCITY_MEAN = 3.0
VELOCITY_SCALE = 1.5
BUMP_SPREAD = 32.0
EPSILON = 1e-06
HIGHEST = lax.Precision.HIGHEST


def build_tables(grid_rows, grid_columns, row_modes, column_modes):
    column_index = jnp.arange(grid_columns, dtype=jnp.int32)
    mode_index = jnp.arange(column_modes, dtype=jnp.int32)
    column_phase = (column_index[:, None] * mode_index[None, :] % grid_columns).astype(
        jnp.float32
    ) * (2.0 * math.pi / grid_columns)
    mode_weight = jnp.where(mode_index == 0, 1.0, 2.0).astype(jnp.float32)
    root_columns = 1.0 / math.sqrt(grid_columns)
    forward_plain = (
        jnp.stack([jnp.cos(column_phase), -jnp.sin(column_phase)], axis=1) * root_columns
    )
    backward_plain = (
        jnp.stack([jnp.cos(column_phase).T, -jnp.sin(column_phase).T], axis=0) * root_columns
    )
    forward_weighted = forward_plain * mode_weight[None, None, :]
    backward_weighted = backward_plain * mode_weight[None, :, None]
    row_index = jnp.arange(grid_rows, dtype=jnp.int32)
    row_mode_index = jnp.arange(row_modes, dtype=jnp.int32)
    frequency = jnp.where(
        row_mode_index < row_modes // 2, row_mode_index, row_mode_index - row_modes
    )
    row_phase = (frequency[:, None] * row_index[None, :] % grid_rows).astype(jnp.float32) * (
        2.0 * math.pi / grid_rows
    )
    root_rows = 1.0 / math.sqrt(grid_rows)
    cosine_rows = jnp.cos(row_phase) * root_rows
    sine_rows = jnp.sin(row_phase) * root_rows
    return tuple(
        (
            element.astype(jnp.bfloat16)
            for element in (
                forward_plain,
                backward_plain,
                forward_weighted,
                backward_weighted,
                cosine_rows,
                sine_rows,
            )
        )
    )


def mix_modes(spectrum, weights, adjoint, accuracy):
    channels = weights.shape[2]
    real_part = spectrum[..., :channels]
    imaginary_part = spectrum[..., channels:]
    if adjoint:
        result_real = jnp.einsum(
            "...kyq,kycq->...kyc",
            spectrum,
            weights,
            precision=accuracy,
            preferred_element_type=jnp.float32,
        )
        rotated = jnp.concatenate([imaginary_part, -real_part], axis=-1)
        result_imaginary = jnp.einsum(
            "...kyq,kycq->...kyc",
            rotated,
            weights,
            precision=accuracy,
            preferred_element_type=jnp.float32,
        )
    else:
        leading = jnp.einsum(
            "...kyc,kycq->...kyq",
            real_part,
            weights,
            precision=accuracy,
            preferred_element_type=jnp.float32,
        )
        trailing = jnp.einsum(
            "...kyc,kycq->...kyq",
            imaginary_part,
            weights,
            precision=accuracy,
            preferred_element_type=jnp.float32,
        )
        result_real = leading[..., :channels] - trailing[..., channels:]
        result_imaginary = leading[..., channels:] + trailing[..., :channels]
    return jnp.concatenate([result_real, result_imaginary], axis=-1)


def forward_spectral(values, weights, table_in, table_out, cosine_rows, sine_rows):
    shot_count, channels, rows_local, grid_columns = values.shape
    along_columns = jnp.einsum(
        "schw,wpk->shkpc", values, table_in, preferred_element_type=jnp.float32
    )
    column_modes = along_columns.shape[2]
    along_columns = along_columns.reshape(
        shot_count, rows_local, column_modes, 2 * channels
    ).astype(jnp.bfloat16)
    pencils = lax.all_to_all(along_columns, "space", split_axis=2, concat_axis=1, tiled=True)
    leading = jnp.einsum("kh,shyx->skyx", cosine_rows, pencils, preferred_element_type=jnp.float32)
    trailing = jnp.einsum("kh,shyx->skyx", sine_rows, pencils, preferred_element_type=jnp.float32)
    spectrum = jnp.concatenate(
        [
            leading[..., :channels] + trailing[..., channels:],
            leading[..., channels:] - trailing[..., :channels],
        ],
        axis=-1,
    ).astype(jnp.bfloat16)
    mixture = mix_modes(spectrum, weights, False, None).astype(jnp.bfloat16)
    leading = jnp.einsum("kh,skyx->shyx", cosine_rows, mixture, preferred_element_type=jnp.float32)
    trailing = jnp.einsum("kh,skyx->shyx", sine_rows, mixture, preferred_element_type=jnp.float32)
    rows_back = jnp.concatenate(
        [
            leading[..., :channels] - trailing[..., channels:],
            trailing[..., :channels] + leading[..., channels:],
        ],
        axis=-1,
    ).astype(jnp.bfloat16)
    returned = lax.all_to_all(rows_back, "space", split_axis=1, concat_axis=2, tiled=True)
    returned = returned.reshape(shot_count, rows_local, column_modes, 2, channels)
    return jnp.einsum("shkpo,pkw->sohw", returned, table_out, preferred_element_type=jnp.float32)


def adjoint_spectral(values, weights, table_in, table_out, cosine_rows, sine_rows):
    shot_count, channels, rows_local, grid_columns = values.shape
    weights_wide = weights.astype(jnp.float32)
    cosine_wide = cosine_rows.astype(jnp.float32)
    sine_wide = sine_rows.astype(jnp.float32)
    out_wide = table_out.astype(jnp.float32)
    along_columns = jnp.einsum(
        "schw,wpk->shkpc", values, table_in, preferred_element_type=jnp.float32
    )
    column_modes = along_columns.shape[2]
    along_columns = along_columns.reshape(shot_count, rows_local, column_modes, 2 * channels)
    combined = jnp.sum(along_columns, axis=0, keepdims=True)
    pencils = lax.all_to_all(combined, "space", split_axis=2, concat_axis=1, tiled=True)
    leading = jnp.einsum("kh,shyx->skyx", cosine_wide, pencils, precision=HIGHEST)
    trailing = jnp.einsum("kh,shyx->skyx", sine_wide, pencils, precision=HIGHEST)
    spectrum = jnp.concatenate(
        [
            leading[..., :channels] + trailing[..., channels:],
            leading[..., channels:] - trailing[..., :channels],
        ],
        axis=-1,
    )
    mixture = mix_modes(spectrum, weights_wide, True, HIGHEST)
    leading = jnp.einsum("kh,skyx->shyx", cosine_wide, mixture, precision=HIGHEST)
    trailing = jnp.einsum("kh,skyx->shyx", sine_wide, mixture, precision=HIGHEST)
    returned = lax.all_to_all(
        jnp.concatenate(
            [
                leading[..., :channels] - trailing[..., channels:],
                trailing[..., :channels] + leading[..., channels:],
            ],
            axis=-1,
        ),
        "space",
        split_axis=1,
        concat_axis=2,
        tiled=True,
    )
    returned = returned.reshape(returned.shape[0], rows_local, column_modes, 2, channels)
    return jnp.einsum("shkpo,pkw->ohw", returned, out_wide, precision=HIGHEST)


def misfit_of(predicted, recorded, taper_gain):
    weighted = predicted * taper_gain
    target = recorded * taper_gain
    predicted_scale = jnp.sqrt(jnp.mean(weighted * weighted) + EPSILON)
    target_scale = jnp.sqrt(jnp.mean(target * target) + EPSILON)
    differ = weighted / predicted_scale - target / target_scale
    return 0.5 * jnp.mean(differ * differ)


def shards(
    velocity,
    encoder_weight,
    encoder_bias,
    source_amplitude,
    source_row,
    source_column,
    receiver_rows,
    point_weight,
    spectral_weight,
    layer_bias,
    out_weight,
    observed,
):
    column_in, column_out, weighted_in, weighted_out, cosine_rows, sine_rows = build_tables(
        GH, GW, KX, KY
    )
    rows_local = velocity.shape[0] // 4
    grid_columns = velocity.shape[1] // 4
    row_start = lax.axis_index("space") * rows_local
    local_rows = row_start + jnp.arange(rows_local, dtype=jnp.int32)
    normalized = (velocity - VELOCITY_MEAN) / VELOCITY_SCALE
    patches = normalized.reshape(rows_local, 4, grid_columns, 4)
    encoded = (
        jnp.einsum("hawb,abc->chw", patches, encoder_weight, precision=HIGHEST)
        + encoder_bias[:, None, None]
    )
    row_place = local_rows.astype(jnp.float32)
    column_place = jnp.arange(grid_columns, dtype=jnp.int32).astype(jnp.float32)
    row_gap = row_place[None, :] - source_row.astype(jnp.float32)[:, None]
    column_gap = column_place[None, :] - source_column.astype(jnp.float32)[:, None]
    source_bump = jnp.exp(
        -(
            row_gap[:, :, None] * row_gap[:, :, None]
            + column_gap[:, None, :] * column_gap[:, None, :]
        )
        / BUMP_SPREAD
    )
    lifted = (encoded[None] + source_amplitude[None, :, None, None] * source_bump[:, None]).astype(
        jnp.bfloat16
    )
    pointwise = jnp.einsum(
        "co,schw->sohw", point_weight, lifted, preferred_element_type=jnp.float32
    )
    spectral_out = forward_spectral(
        lifted, spectral_weight, column_in, weighted_out, cosine_rows, sine_rows
    )
    preactivation = pointwise + spectral_out + layer_bias[None, :, None, None]
    activation, activation_back = jax.vjp(jax.nn.gelu, preactivation)
    output_field = jnp.einsum("c,schw->shw", out_weight, activation, precision=HIGHEST)
    receiver_mask = (receiver_rows[:, :, None] == local_rows[None, None, :]).astype(jnp.float32)
    partial_rows = jnp.einsum("srh,shw->srw", receiver_mask, output_field, precision=HIGHEST)
    predicted = lax.psum(partial_rows, "space")
    taper_gain = 0.5 + column_place / GW
    misfits, misfit_back = jax.vjp(
        lambda values: jax.vmap(misfit_of, in_axes=(0, 0, None))(values, observed, taper_gain),
        predicted,
    )
    data_gradient = misfit_back(jnp.full(misfits.shape, GH * GW, jnp.float32))[0]
    field_gradient = jnp.einsum("srh,srw->shw", receiver_mask, data_gradient, precision=HIGHEST)
    inner_gradient = activation_back(out_weight[None, :, None, None] * field_gradient[:, None])[
        0
    ].astype(jnp.bfloat16)
    lifted_gradient = jnp.einsum(
        "co,sohw->chw", point_weight, inner_gradient, preferred_element_type=jnp.float32
    )
    lifted_gradient = lifted_gradient + adjoint_spectral(
        inner_gradient, spectral_weight, weighted_in, column_out, cosine_rows, sine_rows
    )
    patch_gradient = (
        jnp.einsum("abc,chw->hawb", encoder_weight, lifted_gradient, precision=HIGHEST)
        / VELOCITY_SCALE
    )
    local_gradient = patch_gradient.reshape(velocity.shape)
    cell_count = velocity.shape[0] * lax.axis_size("space") * velocity.shape[1]
    own_block = lax.psum_scatter(local_gradient, "shot", scatter_dimension=1, tiled=True)
    total_squares = lax.psum(jnp.sum(own_block * own_block), ("shot", "space"))
    scaled = own_block / jnp.sqrt(total_squares / cell_count + EPSILON)
    return (misfits, scaled)


def solution(mesh):
    in_specs = (
        P("space", None),
        P(),
        P(),
        P(),
        P("shot"),
        P("shot"),
        P("shot", None),
        P(),
        P(None, "space", None, None),
        P(),
        P(),
        P("shot", None, None),
    )
    out_specs = (P("shot"), P("space", "shot"))
    return jax.shard_map(shards, mesh=mesh, in_specs=in_specs, out_specs=out_specs, check_vma=False)
```

profile of v0, /device:TPU:1, one launch (start us, length us, event | category | flops | bytes accessed | tf_op | source)
XLA Modules:
  0.0 718.6 jit_solution(5225909696756055120)
XLA Ops:
  10.8 35.9 %reshape.310 = f32[32,4,512,4]{3,2,1,0:T(8,128)} reshape(f32[128,2048]{1,0:T(8,128)S(1)} %add_multiply_fusion) | data formatting | bytes 2097152 | tf_op jit(solution)/shard_map/reshape | solution.py:210
  47.0 44.2 %fusion.32 = f32[64,32,512]{2,0,1:T(8,128)} fusion(f32[32,4,512,4]{3,2,1,0:T(8,128)} %reshape.310, f32[64]{0:T(128)S(1)} %copy-done.19, f32[4,4,64]{2,1,0:T(4,128)S(1)} %copy-done.9), kind=kOutput, calls=%fused_computation.39 | convolution fusion | flops 202375168 | bytes 5247232 | tf_op jit(solution)/shard_map/hawb,abc->chw/dot_general | solution.py:212
  91.3 6.2 fusion.41
  100.2 3.9 reshape.340
  104.1 7.4 %all-to-all-start = ((bf16[4,32,24,128]{3,1,0,2:T(8,128)(2,1)}), bf16[4,32,24,128]{3,1,0,2:T(8,128)(2,1)S(1)}, u32[]{:S(2)}, u32[]{:S(2)}) async-start(bf16[4,32,24,128]{3,1,0,2:T(8,128)(2,1)} %reshape.340), calls=%async_computation | async-start | bytes 1572864 | tf_op jit(solution)/shard_map/all_to_all | solution.py:112
  111.5 20.1 %all-to-all-done = bf16[4,32,24,128]{3,1,0,2:T(8,128)(2,1)S(1)} async-done(((bf16[4,32,24,128]{3,1,0,2:T(8,128)(2,1)}), bf16[4,32,24,128]{3,1,0,2:T(8,128)(2,1)S(1)}, u32[]{:S(2)}, u32[]{:S(2)}) %all-to-all-start) | async-done | bytes 786464 | tf_op jit(solution)/shard_map/all_to_all | solution.py:112
  137.9 4.3 all-to-all-start.1
  143.0 19.4 %all-to-all-done.1 = bf16[4,256,3,128]{3,0,2,1:T(4,128)(2,1)S(1)} async-done(((bf16[4,256,3,128]{3,0,2,1:T(4,128)(2,1)}), bf16[4,256,3,128]{3,0,2,1:T(4,128)(2,1)S(1)}, u32[]{:S(2)}, u32[]{:S(2)}) %all-to-all-start.1) | async-done | bytes 786464 | tf_op jit(solution)/shard_map/all_to_all | solution.py:132
  164.4 9.7 %fusion.39 = f32[512,4,32,64,1]{0,3,4,2,1:T(8,128)} fusion(bf16[4,32,24,2,64]{4,3,1,2,0:T(2,128)(2,1)} %reshape.311, f32[1,24,512]{2,1,0:T(8,128)S(1)} %get-tuple-element.34, f32[1,24,512]{2,1,0:T(8,128)S(1)} %get-tuple-element.35, f32[24]{0:T(128)} %fusion.132), kind=kOutput, calls=%fused_computation.42 | convolution fusion | flops 402726912 | bytes 17662048 | tf_op jit(solution)/shard_map/shkpo,pkw->sohw/dot_general | solution.py:134
  174.1 11.6 %fusion.10 = f32[4,64,32,512]{3,1,2,0:T(8,128)} fusion(f32[512,4,32,64,1]{0,3,4,2,1:T(8,128)} %fusion.39, f32[64]{0:T(128)S(1)} %copy-done.13, f32[4,32,512]{2,1,0:T(8,128)S(1)} %multiply_exponential_fusion, f32[64]{0:T(128)S(1)} %copy-done.12, f32[64,32,512]{2,0,1:T(8,128)S(1)} %copy-done.1, bf16[64,64]{1,0:T(8,128)(2,1)S(1)} %copy-done.7), kind=kOutput, calls=%fused_computation.15 | convolution fusion | flops 557842432 | bytes 38019584 | tf_op jit(solution)/shard_map/co,schw->sohw/dot_general | solution.py:229
  185.8 16.0 %fusion.11 = f32[1,4,32,512]{3,0,2,1:T(1,128)S(1)} fusion(f32[4,64,32,512]{3,1,2,0:T(8,128)} %fusion.10, f32[64]{0:T(128)S(1)} %copy-done.16), kind=kOutput, calls=%fused_computation.17 | convolution fusion | flops 83886080 | bytes 17039616 | tf_op jit(solution)/shard_map/c,schw->shw/dot_general | solution.py:237
  202.8 68.0 %all-reduce.2.cloned.1.call-done = f32[4,16,512]{2,1,0:T(8,128)} async-done(((f32[4,16,512]{2,1,0:T(8,128)}), f32[4,16,512]{2,1,0:T(8,128)}) %all-reduce.2.cloned.1.call-update) | async-done | bytes 131088 | tf_op jit(solution)/shard_map/psum | solution.py:240
  274.8 19.6 %convert_reduce_fusion = (bf16[64,32,512]{2,0,1:T(8,128)(2,1)}, bf16[4,64,32,512]{3,1,2,0:T(8,128)(2,1)S(1)}) fusion(f32[4,64,32,512]{3,1,2,0:T(8,128)} %fusion.10, f32[4,32,512]{2,1,0:T(8,128)S(1)} %fusion.64, f32[64]{0:T(128)S(1)} %copy-done.16), kind=kLoop, calls=%fused_computation.16 | loop fusion | flops 95420416 | bytes 27525376 | tf_op jit(solution)/shard_map/co,sohw->chw/reduce_sum | solution.py:251
  294.4 4.0 fusion.36
  299.5 17.4 %all_to_all.63 = f32[1,32,24,128]{3,1,0,2:T(8,128)S(1)} all-to-all(f32[1,32,24,128]{3,1,0,2:T(8,128)S(1)} %reshape.341), channel_id=1, replica_groups=mesh['shot'=32,'space'=8] {'space'}, dimensions={2} | all-to-all | bytes 786432 | tf_op jit(solution)/shard_map/all_to_all | solution.py:149
  323.2 3.8 fusion.75
  330.5 4.2 all-to-all-start.3
  335.0 4.3 fusion.123
  339.3 7.1 all-to-all-done.3
  349.8 5.0 fusion.47
  354.8 26.5 %copy.109 = f32[32,4,512,4]{1,0,3,2:T(8,128)} copy(f32[32,4,512,4]{2,3,1,0:T(4,128)S(1)} %fusion.47) | data formatting | bytes 2097152
  381.2 28.6 %reshape.344 = f32[128,2048]{0,1:T(8,128)} reshape(f32[32,4,512,4]{1,0,3,2:T(8,128)} %copy.109) | data formatting | bytes 2097152
  409.8 202.4 %reduce-scatter.4.cloned.1.call-done = f32[64,128]{1,0:T(8,128)} async-done(((f32[2048,128]{1,0:T(8,128)}), f32[64,128]{1,0:T(8,128)}) %reduce-scatter.4.cloned.1.call-update) | async-done | bytes 32784
  614.2 95.7 %psum.15 = f32[]{:T(128)} all-reduce(f32[]{:T(128)} %multiply_reduce_fusion.4), channel_id=1, replica_groups=mesh['shot'=32,'space'=8] {'shot','space'}, use_global_device_ids=true, to_apply=%region_9.10 | all-reduce | flops 1 | bytes 8 | tf_op jit(solution)/shard_map/psum | solution.py:264
  (105 shorter events, 37.5 us)
Async XLA Ops:
  7.2 125.7 %copy-start = (bf16[48,3,64,128]{3,2,1,0:T(8,128)(2,1)S(1)}, bf16[48,3,64,128]{3,2,1,0:T(8,128)(2,1)}, u32[]{:S(2)}) copy-start(bf16[48,3,64,128]{3,2,1,0:T(8,128)(2,1)} %param.20) | copy-start | bytes 7077892
  7.4 83.8 %copy-start.5 = (f32[512,1,24]{0,2,1:T(8,128)}, f32[512,1,24]{0,2,1:T(8,128)S(1)}, u32[]{:S(2)}) copy-start(f32[512,1,24]{0,2,1:T(8,128)S(1)} %get-tuple-element.33) | copy-start | bytes 147460
  10.7 36.2 %copy-start.9 = (f32[4,4,64]{2,1,0:T(4,128)S(1)}, f32[4,4,64]{2,1,0:T(4,128)}, u32[]{:S(2)}) copy-start(f32[4,4,64]{2,1,0:T(4,128)} %param.13) | copy-start | bytes 12292
  10.8 36.2 %copy-start.19 = (f32[64]{0:T(128)S(1)}, f32[64]{0:T(128)}, u32[]{:S(2)}) copy-start(f32[64]{0:T(128)} %param.14) | copy-start | bytes 772
  47.0 44.2 %copy-start.11 = (f32[64]{0:T(128)S(1)}, f32[64]{0:T(128)}, u32[]{:S(2)}) copy-start(f32[64]{0:T(128)} %param.15) | copy-start | bytes 772
  104.1 27.5 %all-to-all-start = ((bf16[4,32,24,128]{3,1,0,2:T(8,128)(2,1)}), bf16[4,32,24,128]{3,1,0,2:T(8,128)(2,1)S(1)}, u32[]{:S(2)}, u32[]{:S(2)}) async-start(bf16[4,32,24,128]{3,1,0,2:T(8,128)(2,1)} %reshape.340), calls=%async_computation | async-start | bytes 1572864 | tf_op jit(solution)/shard_map/all_to_all | solution.py:112
  111.5 30.7 %copy-start.8 = (s32[48]{0:T(128)}, s32[48]{0:T(128)S(1)}, u32[]{:S(2)}) copy-start(s32[48]{0:T(128)S(1)} %compare_select_fusion) | copy-start | bytes 580
  137.9 24.5 %all-to-all-start.1 = ((bf16[4,256,3,128]{3,0,2,1:T(4,128)(2,1)}), bf16[4,256,3,128]{3,0,2,1:T(4,128)(2,1)S(1)}, u32[]{:S(2)}, u32[]{:S(2)}) async-start(bf16[4,256,3,128]{3,0,2,1:T(4,128)(2,1)} %copy.71), calls=%async_computation.1 | async-start | bytes 1572864 | tf_op jit(solution)/shard_map/all_to_all | solution.py:132
  142.2 128.6 %all-reduce.2.cloned.1.call-start = ((), (), s32[]{:S(2)}) async-start(), calls=%async_computation.5 | async-start | bytes 262144 | tf_op jit(solution)/shard_map/psum | solution.py:240
  142.9 42.8 %copy-start.3 = (f32[1,24,512]{2,1,0:T(8,128)}, f32[1,24,512]{2,1,0:T(8,128)S(1)}, u32[]{:S(2)}) copy-start(f32[1,24,512]{2,1,0:T(8,128)S(1)} %get-tuple-element.34) | copy-start | bytes 147460
  142.9 42.8 %copy-start.4 = (f32[1,24,512]{2,1,0:T(8,128)}, f32[1,24,512]{2,1,0:T(8,128)S(1)}, u32[]{:S(2)}) copy-start(f32[1,24,512]{2,1,0:T(8,128)S(1)} %get-tuple-element.35) | copy-start | bytes 147460
  164.4 9.7 %copy-start.7 = (bf16[64,64]{1,0:T(8,128)(2,1)S(1)}, bf16[64,64]{1,0:T(8,128)(2,1)}, u32[]{:S(2)}) copy-start(bf16[64,64]{1,0:T(8,128)(2,1)} %param.19) | copy-start | bytes 24580
  164.4 9.7 %copy-start.12 = (f32[64]{0:T(128)S(1)}, f32[64]{0:T(128)}, u32[]{:S(2)}) copy-start(f32[64]{0:T(128)} %param.15) | copy-start | bytes 772
  164.4 9.7 %copy-start.13 = (f32[64]{0:T(128)S(1)}, f32[64]{0:T(128)}, u32[]{:S(2)}) copy-start(f32[64]{0:T(128)} %param.21) | copy-start | bytes 772
  174.1 11.6 %copy-start.16 = (f32[64]{0:T(128)S(1)}, f32[64]{0:T(128)}, u32[]{:S(2)}) copy-start(f32[64]{0:T(128)} %param.22) | copy-start | bytes 772
  185.7 16.1 %copy-start.15 = (s32[4,16]{1,0:T(4,128)S(1)}, s32[4,16]{1,0:T(4,128)}, u32[]{:S(2)}) copy-start(s32[4,16]{1,0:T(4,128)} %param.18) | copy-start | bytes 772
  185.7 16.1 %copy-start.17 = (s32[32]{0:T(128)S(1)}, s32[32]{0:T(128)}, u32[]{:S(2)}) copy-start(s32[32]{0:T(128)} %get-tuple-element.30) | copy-start | bytes 388
  185.8 85.1 %copy-start.2 = (f32[4,16,512]{2,1,0:T(8,128)S(1)}, f32[4,16,512]{2,1,0:T(8,128)}, u32[]{:S(2)}) copy-start(f32[4,16,512]{2,1,0:T(8,128)} %param.23) | copy-start | bytes 393220
  201.8 92.6 %copy-start.6 = (f32[512,1,24]{0,2,1:T(8,128)S(1)}, f32[512,1,24]{0,2,1:T(8,128)}, u32[]{:S(2)}) copy-start(f32[512,1,24]{0,2,1:T(8,128)} %copy-done.5) | copy-start | bytes 147460
  201.8 92.6 %copy-start.14 = (f32[24]{0:T(128)S(1)}, f32[24]{0:T(128)}, u32[]{:S(2)}) copy-start(f32[24]{0:T(128)} %fusion.132) | copy-start | bytes 292
  298.4 51.3 %copy-start.10 = (f32[4,4,64]{2,1,0:T(4,128)S(1)}, f32[4,4,64]{2,1,0:T(4,128)}, u32[]{:S(2)}) copy-start(f32[4,4,64]{2,1,0:T(4,128)} %param.13) | copy-start | bytes 12292
  330.5 15.9 %all-to-all-start.3 = ((f32[1,256,3,128]{3,0,2,1:T(1,128)}), f32[1,256,3,128]{3,0,2,1:T(1,128)S(1)}, u32[]{:S(2)}, u32[]{:S(2)}) async-start(f32[1,256,3,128]{3,0,2,1:T(1,128)} %copy.78), calls=%async_computation.3 | async-start | bytes 786432 | tf_op jit(solution)/shard_map/all_to_all | solution.py:162
  334.7 277.5 %reduce-scatter.4.cloned.1.call-start = ((), (), s32[]{:S(2)}) async-start(), calls=%async_computation.6 | async-start | bytes 1081344
  381.2 232.4 %copy-start.18 = (f32[4]{0:T(128)S(1)}, f32[4]{0:T(128)}, u32[]{:S(2)}) copy-start(f32[4]{0:T(128)} %get-tuple-element.9) | copy-start | bytes 52
  (1 other events, 9.7 us)
Sparse Core Ops, SparseCore 0:
  202.9 67.8 all-reduce.1
  409.9 202.2 reduce-scatter.3
where the time goes:
time: 727 us; the launch traced here: 719 us
  waiting for transfers between devices  317 us (44%)
  matrix products  122 us (17%)
  blocking collectives  113 us (16%)
  local copies, waits for them, and re-layouts  105 us (14%)
  other arithmetic  29.5 us (4%)
  starting transfers between devices  16.2 us (2%)
  between operations  15.7 us (2%)
    unnamed x3, waiting for transfers between devices  202 us
    psum x1, blocking collectives, shards(): total_squares = lax.psum(jnp.sum(own_block * own_block), ('shot', 'space'))  95.7 us
    psum x1, waiting for transfers between devices, shards(): predicted = lax.psum(partial_rows, 'space')  68 us
    unnamed x44, local copies, waits for them, and re-layouts  56.7 us
    dot_general x1, matrix products, shards(): jnp.einsum('hawb,abc->chw', patches, encoder_weight, precision=HIGHEST)  44.2 us
    reshape x1, local copies, waits for them, and re-layouts, shards(): patches = normalized.reshape(rows_local, 4, grid_columns, 4)  35.9 us
    all_to_all x1, waiting for transfers between devices, forward_spectral(): lax.all_to_all(along_columns, 'space', split_axis=2, concat_axis=1, tiled...  20.1 us
    reduce_sum x1, other arithmetic, shards(): jnp.einsum('co,sohw->chw', point_weight, inner_gradient, preferred_elemen...  19.6 us
  transfers between devices with their start and end apart: 5, of which 5 were waited for; matrix products, arithmetic and copies ran while one was open for 1% of the time, Pallas kernels for 0%

commit v1 on v0

v1 whole, which is shorter than its diff:
```python
import math

import jax
import jax.numpy as jnp
import ml_dtypes
import numpy as np
from jax import lax
from jax.experimental import pallas as pl
from jax.experimental.pallas import tpu as pltpu
from jax.sharding import PartitionSpec as P

C = 64
KX = 48
KY = 24
GH = 256
GW = 512
REC = 16
SPACE = 8
SHOT = 32
ROWS = GH // SPACE
KOWN = KY // SPACE
PAIRS = 64
EPSILON = 1e-06
VELOCITY_MEAN = 3.0
VELOCITY_SCALE = 1.5
HIGHEST = lax.Precision.HIGHEST
F32 = jnp.float32
BF16 = jnp.bfloat16
VMEM_LIMIT = 56 << 20


def bf(values):
    return np.asarray(values, np.float32).astype(ml_dtypes.bfloat16)


def as64(values):
    return values.astype(np.float64)


def make_tables():
    k = np.arange(KY)
    w = np.arange(GW)
    phase = (k[:, None] * w[None, :] % GW) * (2.0 * math.pi / GW)
    plain = bf(np.stack([np.cos(phase), -np.sin(phase)], 1) / math.sqrt(GW))
    f = np.where(np.arange(KX) < KX // 2, np.arange(KX), np.arange(KX) - KX)
    phase = (f[:, None] * np.arange(GH)[None, :] % GH) * (2.0 * math.pi / GH)
    cos_rows = bf(np.cos(phase) / math.sqrt(GH))
    sin_rows = bf(np.sin(phase) / math.sqrt(GH))
    return plain, cos_rows, sin_rows


PLAIN, COS_ROWS, SIN_ROWS = make_tables()
MODE_WEIGHT = np.where(np.arange(KY) == 0, 1.0, 2.0)


def columns_table():
    table = np.zeros((GW, 4, SPACE, 32), np.float32)
    plain = PLAIN.astype(np.float32).reshape(SPACE, 6, GW)
    for b in range(4):
        table[:, b, :, 6 * b : 6 * b + 6] = plain.transpose(2, 0, 1)
    return bf(table.reshape(4 * GW, 256))


def rows_table():
    table = np.zeros((SPACE, 4, KX, 2, ROWS, 4), np.float32)
    for p in range(SPACE):
        for a in range(4):
            table[p, a, :, 0, :, a] = COS_ROWS[:, ROWS * p : ROWS * p + ROWS]
            table[p, a, :, 1, :, a] = SIN_ROWS[:, ROWS * p : ROWS * p + ROWS]
    return bf(table.reshape(SPACE, 4 * KX, 256))


def ones_table():
    wsum = as64(PLAIN).sum(-1)
    c, s = as64(COS_ROWS).sum(-1), as64(SIN_ROWS).sum(-1)
    table = np.zeros((SPACE, KX, 128), np.float32)
    for q in range(SPACE):
        for k in range(KOWN):
            re, im = wsum[3 * q + k]
            table[q, :, 24 + 2 * k] = c * re + s * im
            table[q, :, 25 + 2 * k] = c * im - s * re
    return table


def select_table():
    table = np.zeros((128, 4, 4, 128), np.float32)
    for b in range(4):
        table[np.arange(128), b, b, np.arange(128)] = 1.0
    return bf(table.reshape(512, 512))


def weighted_table():
    plain = PLAIN.astype(np.float32) * MODE_WEIGHT[:, None, None]
    return bf(plain.reshape(SPACE, KOWN, 2, GW).transpose(1, 2, 0, 3).reshape(48, GW))


def gram_tables():
    full = np.concatenate([as64(COS_ROWS), as64(SIN_ROWS)], 0)
    gram_rows = full @ full.T
    e = as64(PLAIN).reshape(48, GW)
    gram = e @ e.T
    wide = np.zeros((SPACE, 4, 32, SPACE, 4, 32))
    gram = gram.reshape(SPACE, 6, SPACE, 6)
    for a in range(4):
        for b in range(4):
            wide[:, a, b * 6 : b * 6 + 6, :, a, b * 6 : b * 6 + 6] = gram
    wide = wide.reshape(1024, 1024)
    diag_rows = np.broadcast_to(np.diag(gram_rows)[:, None], (96, 128))
    off_rows = bf(gram_rows - np.diag(np.diag(gram_rows)))
    diag_wide = np.diag(wide)[None, :]
    off_wide = bf(wide - np.diag(np.diag(wide)))
    return (
        np.asarray(diag_rows, np.float32),
        off_rows,
        np.asarray(diag_wide, np.float32),
        off_wide,
    )


COLUMNS = columns_table()
ROW_SUMS = rows_table()
ONES = ones_table()
SELECT = select_table()
WEIGHTED = weighted_table()
DIAG_ROWS, OFF_ROWS, DIAG_WIDE, OFF_WIDE = gram_tables()
PAIRED_ROWS = np.zeros((2, 64, GH), np.float32)
PAIRED_ROWS[0, :KX], PAIRED_ROWS[1, :KX] = COS_ROWS, SIN_ROWS
PAIRED_ROWS = bf(PAIRED_ROWS.reshape(128, GH))
OWN_COLUMNS = np.zeros((SPACE, 8, GW), np.float32)
OWN_COLUMNS[:, :6] = PLAIN.reshape(SPACE, 6, GW)
OWN_COLUMNS = bf(OWN_COLUMNS)


def lanes_table():
    table = np.zeros((KOWN, 2, 128, 128), np.float32)
    for k in range(KOWN):
        for part in range(2):
            for ab in range(16):
                table[k, part, ab, 32 * (ab // 4) + 6 * (ab % 4) + 2 * k + part] = 1.0
    return bf(table.reshape(KOWN * 2, 128, 128))


def block_table():
    table = np.zeros((SHOT, SPACE, 4, 32, 16, 4), np.float32)
    plain = PLAIN.astype(np.float32).reshape(SPACE, 6, SHOT, 16)
    for b in range(4):
        table[:, :, :, 6 * b : 6 * b + 6, :, b] = plain.transpose(2, 0, 1, 3)[:, :, None]
    return bf(table.reshape(SHOT, 1024, 64))


LANES = lanes_table()
BLOCKS = block_table()
BOTH_ROWS = bf(np.concatenate([COS_ROWS.astype(np.float32), SIN_ROWS.astype(np.float32)], 0))
ROWS_BACK = bf(
    BOTH_ROWS.astype(np.float32).T.reshape(SPACE, ROWS, 96)
)


def split(values):
    high = values.astype(BF16)
    return high, (values - high.astype(F32)).astype(BF16)


def dot(a, b, dims=((1,), (0,))):
    return lax.dot_general(a, b, (dims, ((), ())), preferred_element_type=F32)


def dot_split(a, b):
    high, low = split(b)
    return dot(a, high) + dot(a, low)


def minus_i(x):
    lane = lax.broadcasted_iota(jnp.int32, x.shape, 1)
    swapped = pltpu.roll(x, 64, 1)
    return jnp.where(lane < 64, swapped, -swapped)


def times_i(x):
    lane = lax.broadcasted_iota(jnp.int32, x.shape, 1)
    swapped = pltpu.roll(x, 64, 1)
    return jnp.where(lane < 64, -swapped, swapped)


def full_spec(shape):
    return pl.BlockSpec(shape, lambda *_: (0,) * len(shape))


def own_spec(shape, place=0):
    return pl.BlockSpec((1,) + shape, lambda i, *own: (own[place][0],) + (0,) * len(shape))


def call(body, prefetch, out_shape, in_specs, out_specs, scratch=(), name=None):
    return pl.pallas_call(
        body,
        out_shape=out_shape,
        grid_spec=pltpu.PrefetchScalarGridSpec(
            num_scalar_prefetch=prefetch,
            grid=(1,),
            in_specs=in_specs,
            out_specs=out_specs,
            scratch_shapes=list(scratch),
        ),
        compiler_params=pltpu.CompilerParams(vmem_limit_bytes=VMEM_LIMIT),
        name=name,
    )


def shaped(shape, dtype=F32):
    return jax.ShapeDtypeStruct(shape, dtype)


def velocity_body(own, v_ref, cols_ref, rows_ref, out_ref):
    vn = (v_ref[...] - VELOCITY_MEAN) / VELOCITY_SCALE
    high, low = split(vn)
    xx = dot(high, cols_ref[...]) + dot(low, cols_ref[...])
    even = lax.broadcasted_iota(jnp.int32, xx.shape, 1) % 2 == 0
    turned = jnp.where(even, pltpu.roll(xx, 255, 1), -pltpu.roll(xx, 1, 1))
    stacked = jnp.concatenate([xx, turned], axis=0)
    yy = dot_split(rows_ref[0], stacked)
    group = lax.broadcasted_iota(jnp.int32, (KX, 128), 1) // 32
    for q in range(SPACE):
        total = jnp.zeros((KX, 128), F32)
        for a in range(4):
            piece = yy[KX * a : KX * a + KX, 128 * (q // 4) : 128 * (q // 4) + 128]
            shift = (32 * a - 32 * (q % 4)) % 128
            if shift:
                piece = pltpu.roll(piece, shift, 1)
            total = jnp.where(group == a, piece, total)
        out_ref[q] = total


def column_of(row):
    return jnp.broadcast_to(row, (128, C)).T


def planes_body(
    own, v_ref, sel_ref, enc_ref, bias_ref, amp_ref, point_ref, layer_ref, weight_ref, lanes_ref,
    out_ref, wk_ref, vec_ref, place_ref, high_ref, low_ref, tmp,
):
    for m in range(4):
        vn = (v_ref[:, 512 * m : 512 * m + 512] - VELOCITY_MEAN) / VELOCITY_SCALE
        high, low = split(vn)
        tmp[...] = dot(high, sel_ref[...]) + dot(low, sel_ref[...])
        for h in range(ROWS):
            for b in range(4):
                out_ref[h, 4 * b : 4 * b + 4, 128 * m : 128 * m + 128] = tmp[
                    4 * h : 4 * h + 4, 128 * b : 128 * b + 128
                ]
    stack = jnp.concatenate(
        [enc_ref[...], bias_ref[...], amp_ref[...], jnp.zeros((6, C), F32)], axis=0
    )
    high, low = split(stack)
    pointed = dot(high, point_ref[...]) + dot(low, point_ref[...])
    swapped = jnp.concatenate(
        [pointed[4 * a + b : 4 * a + b + 1] for b in range(4) for a in range(4)], axis=0
    )
    high, low = split(swapped)
    wk_ref[0:16] = high
    wk_ref[16:32] = high
    wk_ref[32:48] = low
    vec_ref[0] = column_of(pointed[17:18])
    vec_ref[1] = column_of(pointed[16:17] + layer_ref[...])
    vec_ref[2] = column_of(weight_ref[...])
    turned = jnp.concatenate([pointed[:16], jnp.zeros((112, C), F32)], axis=0).T
    scaled = turned * (1.0 / VELOCITY_SCALE)
    for e in range(8):
        high, low = split(pltpu.roll(scaled, 16 * e, 1) if e else scaled)
        place_ref[e, 0:C] = high
        place_ref[e, C : 2 * C] = low
    th, tl = split(scaled)
    for k in range(KOWN):
        reach = jnp.where((own[0] == 0) & (k == 0), 1.0, 0.5)
        for part in range(2):
            wide = (dot(th, lanes_ref[2 * k + part]) + dot(tl, lanes_ref[2 * k + part])) * reach
            high, low = split(wide)
            high_ref[k, C * part : C * part + C] = high
            low_ref[k, C * part : C * part + C] = low


def operator_body(
    own, enc_ref, bias_ref, amp_ref, w_ref, index_ref, rows_ref, cols_ref, out_ref, side_ref, bump_ref
):
    stack = jnp.concatenate(
        [enc_ref[...], bias_ref[...], amp_ref[...], jnp.zeros((6, C), F32)], axis=0
    )
    high, low = split(stack)
    lhs = jnp.concatenate([high.astype(F32), low.astype(F32)], axis=0).astype(BF16)

    def step(j, carry):
        for k in range(KOWN):
            both = dot(lhs, w_ref[j, k])
            out_ref[pl.ds(k * KX * 24 + j, 24, stride=KX), :] = both[:24] + both[24:]
        return carry

    lax.fori_loop(0, KX, step, 0, unroll=8)
    receiver, row, column = index_ref[:, 0:1], index_ref[:, 1:2], index_ref[:, 2:3]
    line = lax.broadcasted_iota(jnp.int32, (PAIRS, GH), 1).astype(F32)
    chosen = jnp.where(line == receiver, 1.0, 0.0).astype(BF16)
    at_rows = dot(chosen, rows_ref[...], ((1,), (1,)))
    gap = line - row
    high, low = split(jnp.exp(gap * gap * (-1.0 / 32.0)))
    row_side = dot(high, rows_ref[...], ((1,), (1,))) + dot(low, rows_ref[...], ((1,), (1,)))
    gap = lax.broadcasted_iota(jnp.int32, (PAIRS, GW), 1).astype(F32) - column
    bump = jnp.exp(gap * gap * (-1.0 / 32.0))
    high, low = split(bump)
    column_side = dot(high, cols_ref[0], ((1,), (1,))) + dot(low, cols_ref[0], ((1,), (1,)))
    gap = receiver - row
    bump_ref[...] = bump * jnp.exp(gap * gap * (-1.0 / 32.0))
    lane = lax.broadcasted_iota(jnp.int32, (PAIRS, 128), 1)
    first = at_rows * row_side
    second = at_rows * pltpu.roll(row_side, 64, 1)
    both = jnp.where(
        lane < 64, first + pltpu.roll(first, 64, 1), second - pltpu.roll(second, 64, 1)
    )
    turned = times_i(both)
    for k in range(KOWN):
        side_ref[k, :, 0:128] = at_rows.astype(BF16)
        side_ref[k, :, 128:256] = (
            both * column_side[:, 2 * k : 2 * k + 1] + turned * column_side[:, 2 * k + 1 : 2 * k + 2]
        ).astype(BF16)


def mix_body(own, v_ref, ones_ref, t_ref, l_ref, out_ref):
    spectrum = ones_ref[0]
    for q in range(SPACE):
        spectrum = spectrum + v_ref[q]
    for k in range(KOWN):
        first = jnp.zeros((KX, 128), F32)
        second = jnp.zeros((KX, 128), F32)
        for ab in range(17):
            lane = (ab // 4) * 32 + (ab % 4) * 6 + 2 * k if ab < 16 else 24 + 2 * k
            plane = t_ref[pl.ds((k * 24 + ab) * KX, KX), :]
            first = first + spectrum[:, lane : lane + 1] * plane
            second = second + spectrum[:, lane + 1 : lane + 2] * plane
        modes = first + times_i(second)
        source = t_ref[pl.ds((k * 24 + 17) * KX, KX), :]
        none = jnp.zeros((16, 128), F32)
        rhs = jnp.concatenate(
            [modes, none, times_i(modes), none, source, none, times_i(source), none], axis=0
        )
        values = dot(l_ref[k], rhs.astype(BF16)).astype(BF16)
        for z in range(SPACE // 2):
            out_ref[z, :, 128 * k : 128 * k + 128] = values


def gain_row():
    return 0.5 + lax.broadcasted_iota(jnp.int32, (1, GW), 1).astype(F32) * (1.0 / GW)


def forward_body(
    own, rows_ref, d_ref, other_ref, planes_ref, table_ref, wk_ref, col_ref, vec_ref, obs_ref,
    pred_ref, slope_ref, stats_ref, dd, acc,
):
    p = own[0]
    gain = gain_row()
    for m in range(3):
        for z in range(SPACE // 2):
            for source, core in ((d_ref, p % 2), (other_ref, 1 - p % 2)):
                start = pl.multiple_of(PAIRS * (SPACE * m + 2 * z + core), PAIRS)
                dd[pl.ds(start, PAIRS), :] = source[z, :, 128 * m : 128 * m + 128].astype(F32)
    acc[...] = jnp.zeros_like(acc)
    root = math.sqrt(2.0 / math.pi)

    def step(r, carry):
        row = rows_ref[r] - p * ROWS

        @pl.when((row >= 0) & (row < ROWS))
        def _():
            s = r // REC
            pieces = []
            for m in range(3):
                block = dd[pl.ds(SPACE * PAIRS * m + r, SPACE, stride=PAIRS), :]
                pieces.append(block[:, :64])
                pieces.append(pltpu.roll(block, 64, 1)[:, :64])
            lhs = jnp.concatenate(pieces, axis=0).astype(BF16)
            lhs = jnp.concatenate([lhs, wk_ref[...]], axis=0)
            high, low = split(planes_ref[row])
            rhs = jnp.concatenate([table_ref[...], high, low, high], axis=0)
            x = dot(lhs, rhs, ((0,), (0,)))
            amp, const, weight = vec_ref[0], vec_ref[1], vec_ref[2]
            col = col_ref[pl.ds(r, 1), :]
            total = []
            for m in range(4):
                lanes = slice(128 * m, 128 * m + 128)
                xm = x[:, lanes] + const + amp * col[:, lanes]
                square = xm * xm
                t = jnp.tanh(root * (xm + 0.044715 * (square * xm)))
                cdf = 0.5 * (1.0 + t)
                slope = cdf + xm * (
                    (0.5 * root) * (1.0 - t * t) * (1.0 + 3.0 * 0.044715 * square)
                )
                slope_ref[pl.ds(pl.multiple_of(r * C, C), C), lanes] = (slope * weight).astype(BF16)
                total.append(jnp.sum(weight * (xm * cdf), axis=0, keepdims=True))
            predicted = jnp.concatenate(total, axis=1)
            pred_ref[pl.ds(r, 1), :] = predicted
            weighted = predicted * gain
            target = obs_ref[pl.ds(r, 1), :] * gain
            acc[pl.ds(s, 1), :] += weighted * weighted
            acc[pl.ds(s + 4, 1), :] += weighted * target

        return carry

    lax.fori_loop(0, PAIRS, step, 0)
    stats = acc[:, :128] + acc[:, 128:256] + acc[:, 256:384] + acc[:, 384:]
    for q in range(SPACE):
        stats_ref[q] = stats


def backward_body(
    own, rows_ref, shot, stats_ref, obs_ref, pred_ref, slope_ref, table_ref, place_ref,
    cols_ref, near_ref, next_ref, far_ref, last_ref, misfit_ref, coef, acc, planes,
):
    p = own[0]
    count = float(REC * GW)
    stats = stats_ref[0]
    for q in range(1, SPACE):
        stats = stats + stats_ref[q]
    stats = jnp.sum(stats, axis=1, keepdims=True)
    gain = gain_row()
    for s in range(4):
        target = obs_ref[REC * s : REC * s + REC, :] * gain
        tt = jnp.sum(jnp.sum(target * target, axis=0, keepdims=True), axis=1, keepdims=True) / count
        ww = stats[s : s + 1] / count
        wt = stats[s + 4 : s + 5] / count
        sp2 = ww + EPSILON
        isp = 1.0 / jnp.sqrt(sp2)
        isq = 1.0 / jnp.sqrt(tt + EPSILON)
        kappa = ww / sp2 - wt * isp * isq
        coef[s : s + 1, :] = jnp.broadcast_to(isp, (1, GW))
        coef[s + 4 : s + 5, :] = jnp.broadcast_to(isq, (1, GW))
        coef[s + 8 : s + 9, :] = jnp.broadcast_to(kappa, (1, GW))
        coef[s + 12 : s + 13, :] = jnp.zeros((1, GW), F32)
    acc[...] = jnp.zeros_like(acc)
    planes[...] = jnp.zeros_like(planes)

    def step(r, carry):
        row = rows_ref[r] - p * ROWS

        @pl.when((row >= 0) & (row < ROWS))
        def _():
            s = r // REC
            isp = coef[pl.ds(s, 1), :]
            isq = coef[pl.ds(s + 4, 1), :]
            kappa = coef[pl.ds(s + 8, 1), :]
            weighted = pred_ref[pl.ds(r, 1), :] * gain * isp
            target = obs_ref[pl.ds(r, 1), :] * gain * isq
            differ = weighted - target
            coef[pl.ds(s + 12, 1), :] += differ * differ
            data = (GH * GW / count) * gain * isp * (differ - kappa * weighted)
            slope = slope_ref[pl.ds(pl.multiple_of(r * C, C), C), :].astype(F32)
            inner = (slope * data).astype(BF16)
            spectra = dot(table_ref[...], inner, ((1,), (1,)))
            acc[pl.ds(pl.multiple_of(row * 48, 8), 48), 0:64] += spectra
            eighth = row % 8
            two = jnp.concatenate([inner, inner], axis=0)
            planes[row // 8] += dot(two, place_ref[eighth], ((0,), (0,)))

        return carry

    lax.fori_loop(0, PAIRS, step, 0)
    lane = lax.broadcasted_iota(jnp.int32, (ROWS, 128), 1)
    for q in range(SPACE):
        for m in range(3):
            even = acc[pl.ds(16 * m + q, ROWS, stride=48), :]
            odd = acc[pl.ds(16 * m + 8 + q, ROWS, stride=48), :]
            joined = jnp.where(lane < 64, even, pltpu.roll(odd, 64, 1))
            cols_ref[q, :, 128 * m : 128 * m + 128] = joined.astype(BF16)
    x = shot[0] % 4
    for by, grad_ref in enumerate((near_ref, next_ref, far_ref, last_ref)):
        column = (x + by) % 4
        for zy in range(8):
            for g in range(4):
                start = pl.multiple_of(64 * zy + 16 * column, 16)
                grad_ref[64 * zy + 16 * g : 64 * zy + 16 * g + 16, :] = planes[
                    g, pl.ds(start, 16), :
                ].astype(BF16)
    for s in range(4):
        row = coef[s + 12 : s + 13, :]
        misfit_ref[s : s + 1, :] = (
            row[:, :128] + row[:, 128:256] + row[:, 256:384] + row[:, 384:]
        )
    misfit_ref[4:8, :] = jnp.zeros((4, 128), F32)


def adjoint_body(a_ref, rows_ref, out_ref):
    values = jnp.concatenate([a_ref[q] for q in range(SPACE)], axis=0)
    y = dot(rows_ref[...], values)
    for k in range(KOWN):
        lanes = slice(128 * k, 128 * k + 128)
        out_ref[KX * k : KX * k + KX, :] = y[:KX, lanes] + minus_i(y[KX:, lanes])


MODES = KOWN * KX


def along_x_body(shot, a_ref, b_ref, c_ref, d_ref, near_ref, next_ref, far_ref, last_ref, tmp):
    tmp[...] = (a_ref[...].astype(F32) + b_ref[...].astype(F32)) + (
        c_ref[...].astype(F32) + d_ref[...].astype(F32)
    )
    y = shot[0] // 4 % 4
    for by, out_ref in enumerate((near_ref, next_ref, far_ref, last_ref)):
        for z in range(2):
            start = pl.multiple_of(64 * (4 * z + (y + by) % 4), 64)
            out_ref[64 * z : 64 * z + 64, :] = tmp[pl.ds(start, 64), :]


def along_y_body(a_ref, b_ref, c_ref, d_ref, modes_ref, out_ref):
    out_ref[0:MODES, :] = modes_ref[...]
    out_ref[MODES:, :] = (a_ref[...] + b_ref[...]) + (c_ref[...] + d_ref[...])


def along_z_body(shot, a_ref, b_ref, local_ref, out_ref, tmp):
    out_ref[0:MODES, :] = a_ref[0:MODES, :] + b_ref[0:MODES, :]
    total = a_ref[MODES:, :] + b_ref[MODES:, :]
    tmp[...] = total
    local_ref[...] = tmp[pl.ds(pl.multiple_of(64 * (shot[0] // 16), 64), 64), :]
    out_ref[MODES : MODES + 8, :] = jnp.broadcast_to(
        jnp.sum(total * total, axis=0, keepdims=True), (8, 128)
    )


def adjoint_mix_body(
    near_ref, next_ref, far_ref, last_ref, t_ref, high_ref, low_ref, extra_ref, out_ref
):
    lane = lax.broadcasted_iota(jnp.int32, (KX, 128), 1)
    total = jnp.zeros((KX, 128), F32)
    cross = jnp.zeros((KX, 128), F32)
    for k in range(KOWN):
        own = slice(KX * k, KX * k + KX)
        spectrum = (near_ref[own, :] + next_ref[own, :]) + (far_ref[own, :] + last_ref[own, :])
        turned = minus_i(spectrum)
        for ab in range(16):
            base = (ab // 4) * 32 + (ab % 4) * 6 + 2 * k
            plane = t_ref[pl.ds((k * 24 + ab) * KX, KX), :]
            re = jnp.sum(spectrum * plane, axis=1, keepdims=True)
            im = jnp.sum(turned * plane, axis=1, keepdims=True)
            total = jnp.where(lane == base, re, total)
            total = jnp.where(lane == base + 1, im, total)
        sh, sl = split(spectrum)
        cross = cross + dot(sh, high_ref[k]) + dot(sl, high_ref[k]) + dot(sh, low_ref[k])
    total = total * (1.0 / VELOCITY_SCALE)
    product = jnp.sum(total * cross, axis=0, keepdims=True)
    own = slice(MODES, MODES + 1)
    squares = (near_ref[own, :] + next_ref[own, :]) + (far_ref[own, :] + last_ref[own, :])
    for z in range(SPACE // 2):
        out_ref[z, :KX, :] = total
        out_ref[z, KX : KX + 1, :] = product
        out_ref[z, KX + 1 : KX + 5, :] = extra_ref[0:4, :]
        out_ref[z, KX + 5 : KX + 6, :] = squares
        out_ref[z, KX + 6 : KX + 8, :] = jnp.zeros((2, 128), F32)


def output_body(
    own, shot, m_ref, other_ref, back_ref, block_ref, local_ref, diag_rows_ref, off_rows_ref, diag_ref, off_ref,
    out_ref, misfit_ref, tmp,
):
    lane = lax.broadcasted_iota(jnp.int32, (KX, 128), 1)
    upper, lower = [], []
    tail = jnp.zeros((8, 128), F32)
    even = own[0] % 2 == 0
    for q in range(SPACE):
        mine, theirs = m_ref[q // 2], other_ref[q // 2]
        whole = jnp.where(even, mine, theirs) if q % 2 == 0 else jnp.where(even, theirs, mine)
        x = whole[:KX]
        tail = tail + whole[KX:]
        turned = jnp.where(lane % 2 == 0, -pltpu.roll(x, 127, 1), pltpu.roll(x, 1, 1))
        upper.append(x)
        lower.append(turned)
    n = jnp.concatenate(
        [jnp.concatenate(upper, axis=1), jnp.concatenate(lower, axis=1)], axis=0
    )
    high, low = split(n)
    nearly = dot(off_rows_ref[...], high)
    diag = jnp.concatenate([diag_rows_ref[...]] * 8, axis=1)
    left = n * diag + nearly
    right = n * diag_ref[...] + dot(high, off_ref[...])
    square = jnp.sum(jnp.sum(left * right, axis=0, keepdims=True), axis=1, keepdims=True)
    sums = jnp.sum(tail, axis=1, keepdims=True)
    total = square + 2.0 * sums[0:1] + sums[5:6]
    scale = 1.0 / jnp.sqrt(total / float(16 * GH * GW) + EPSILON)
    rows = dot(back_ref[0], high) + dot(back_ref[0], low)
    group = lax.broadcasted_iota(jnp.int32, (ROWS, 1024), 1) % 128 // 32
    rows = jnp.concatenate([jnp.where(group == a, rows, 0.0) for a in range(4)], axis=0)
    rh, rl = split(rows)
    block = dot(rh, block_ref[0]) + dot(rl, block_ref[0])
    for a in range(4):
        tmp[pl.ds(a, ROWS, stride=4), 0:64] = block[ROWS * a : ROWS * a + ROWS]
    out_ref[...] = (tmp[...].T[0:64] + local_ref[...]) * scale
    place = lax.broadcasted_iota(jnp.int32, (1, 4), 1)
    misfit = jnp.zeros((1, 4), F32)
    for s in range(4):
        misfit = jnp.where(place == s, sums[s + 1 : s + 2] * (0.5 / float(REC * GW)), misfit)
    misfit_ref[...] = misfit


def turn(size, stride, count, by):
    pairs = []
    for i in range(count):
        digit = (i // stride) % size
        pairs.append((i, i + ((digit + by) % size - digit) * stride))
    return pairs


def from_x(*parts):
    return [
        lax.ppermute(part, "shot", turn(4, 1, SHOT, by + 1)) for by, part in enumerate(parts)
    ]


def from_y(*parts):
    return [
        lax.ppermute(part, "shot", turn(4, 4, SHOT, by + 1)) for by, part in enumerate(parts)
    ]


def gather_space(copies):
    mine = lax.all_to_all(
        copies, "space", 0, 0, axis_index_groups=[[0, 2, 4, 6], [1, 3, 5, 7]], tiled=True
    )
    return mine, lax.ppermute(mine, "space", [(n, n ^ 1) for n in range(SPACE)])


def shards(
    velocity,
    encoder_weight,
    encoder_bias,
    source_amplitude,
    source_row,
    source_column,
    receiver_rows,
    point_weight,
    spectral_weight,
    layer_bias,
    out_weight,
    observed,
):
    p = lax.axis_index("space").astype(jnp.int32)
    i = lax.axis_index("shot").astype(jnp.int32)
    own, shot = p[None], i[None]
    fine = (128, 4 * GW)
    operator_rows = KOWN * KX * 24
    encoder = encoder_weight.reshape(16, C)
    bias, amplitude = encoder_bias[None], source_amplitude[None]
    rows = receiver_rows.reshape(PAIRS)
    index = jnp.stack(
        [rows, jnp.repeat(source_row, REC), jnp.repeat(source_column, REC)], axis=1
    ).astype(F32)
    both_rows = jnp.asarray(BOTH_ROWS)
    table = jnp.asarray(WEIGHTED)
    record = observed.reshape(PAIRS, GW)
    row_spec = full_spec((1, C))

    partial = call(
        velocity_body, 1, shaped((SPACE, KX, 128)),
        [full_spec(fine), full_spec((4 * GW, 256)), own_spec((192, 256))],
        full_spec((SPACE, KX, 128)), name="velocity_spectrum",
    )(own, velocity, jnp.asarray(COLUMNS), jnp.asarray(ROW_SUMS))
    spectra = lax.all_to_all(partial, "space", 0, 0, tiled=True)

    index, _ = lax.optimization_barrier((index, partial))
    operator, sides, bumps = call(
        operator_body, 1,
        (shaped((operator_rows, 128)), shaped((KOWN, PAIRS, 256), BF16), shaped((PAIRS, GW))),
        [
            full_spec((16, C)), row_spec, row_spec, full_spec((KX, KOWN, C, 128)),
            full_spec((PAIRS, 3)), full_spec((128, GH)), own_spec((8, GW)),
        ],
        (full_spec((operator_rows, 128)), full_spec((KOWN, PAIRS, 256)), full_spec((PAIRS, GW))),
        name="operator",
    )(
        own, encoder, bias, amplitude, spectral_weight, index, jnp.asarray(PAIRED_ROWS),
        jnp.asarray(OWN_COLUMNS),
    )

    sent = call(
        mix_body, 1, shaped((SPACE // 2, PAIRS, 384), BF16),
        [
            full_spec((SPACE, KX, 128)), own_spec((KX, 128)),
            full_spec((operator_rows, 128)), full_spec((KOWN, PAIRS, 256)),
        ],
        full_spec((SPACE // 2, PAIRS, 384)), name="mix_modes",
    )(own, spectra, jnp.asarray(ONES), operator, sides)
    gathered, others = gather_space(sent)

    late_bias, _ = lax.optimization_barrier((layer_bias[None], sent))
    planes, wk, vectors, placed, spread_high, spread_low = call(
        planes_body, 1,
        (
            shaped((ROWS, 16, GW)), shaped((48, C), BF16), shaped((3, C, 128)),
            shaped((8, 128, 128), BF16), shaped((KOWN, 128, 128), BF16),
            shaped((KOWN, 128, 128), BF16),
        ),
        [
            full_spec(fine), full_spec((512, 512)), full_spec((16, C)), row_spec, row_spec,
            full_spec((C, C)), row_spec, row_spec, full_spec((KOWN * 2, 128, 128)),
        ],
        (
            full_spec((ROWS, 16, GW)), full_spec((48, C)), full_spec((3, C, 128)),
            full_spec((8, 128, 128)), full_spec((KOWN, 128, 128)), full_spec((KOWN, 128, 128)),
        ),
        [pltpu.VMEM((128, 512), F32)], name="velocity_planes",
    )(
        own, velocity, jnp.asarray(SELECT), encoder, bias, amplitude, point_weight, late_bias,
        out_weight[None], jnp.asarray(LANES),
    )

    predicted, slopes, stats = call(
        forward_body, 2,
        (shaped((PAIRS, GW)), shaped((PAIRS * C, GW), BF16), shaped((SPACE, 8, 128))),
        [
            full_spec((SPACE // 2, PAIRS, 384)), full_spec((SPACE // 2, PAIRS, 384)),
            full_spec((ROWS, 16, GW)), full_spec((48, GW)),
            full_spec((48, C)), full_spec((PAIRS, GW)), full_spec((3, C, 128)),
            full_spec((PAIRS, GW)),
        ],
        (full_spec((PAIRS, GW)), full_spec((PAIRS * C, GW)), full_spec((SPACE, 8, 128))),
        [pltpu.VMEM((3 * SPACE * PAIRS, 128), F32), pltpu.VMEM((8, GW), F32)], name="forward_rows",
    )(own, rows, gathered, others, planes, table, wk, bumps, vectors, record)
    stats = lax.all_to_all(stats, "space", 0, 0, tiled=True)

    columns, near, after, far, last, misfits = call(
        backward_body, 3,
        (shaped((SPACE, ROWS, 384), BF16),) + (shaped((GW, 128), BF16),) * 4 + (shaped((8, 128)),),
        [
            full_spec((SPACE, 8, 128)), full_spec((PAIRS, GW)),
            full_spec((PAIRS, GW)), full_spec((PAIRS * C, GW)), full_spec((48, GW)),
            full_spec((8, 128, 128)),
        ],
        (full_spec((SPACE, ROWS, 384)),) + (full_spec((GW, 128)),) * 4 + (full_spec((8, 128)),),
        [
            pltpu.VMEM((16, GW), F32), pltpu.VMEM((ROWS * 48, 128), F32),
            pltpu.VMEM((4, GW, 128), F32),
        ],
        name="backward_rows",
    )(own, rows, shot, stats, record, predicted, slopes, table, placed)

    columns = lax.all_to_all(columns, "space", 0, 0, tiled=True)
    adjoint = call(
        adjoint_body, 0, shaped((KOWN * KX, 128)),
        [full_spec((SPACE, ROWS, 384)), full_spec((96, GH))],
        full_spec((KOWN * KX, 128)), name="adjoint_rows",
    )(columns, both_rows)
    arrived = from_x(after, far, last)
    blocks = call(
        along_x_body, 1, (shaped((128, 128)),) * 4, [full_spec((GW, 128))] * 4,
        (full_spec((128, 128)),) * 4, [pltpu.VMEM((GW, 128), F32)], name="along_x",
    )(shot, near, *arrived)
    sums = call(
        along_y_body, 0, shaped((MODES + 128, 128)),
        [full_spec((128, 128))] * 4 + [full_spec((MODES, 128))],
        full_spec((MODES + 128, 128)), name="along_y",
    )(blocks[0], *from_y(*blocks[1:]), adjoint)
    local, sums = call(
        along_z_body, 1, (shaped((64, 128)), shaped((MODES + 8, 128))),
        [full_spec((MODES + 128, 128))] * 2,
        (full_spec((64, 128)), full_spec((MODES + 8, 128))), [pltpu.VMEM((128, 128), F32)],
        name="along_z",
    )(shot, sums, lax.ppermute(sums, "shot", turn(2, 16, SHOT, 1)))
    parts = from_x(sums, sums, sums)
    sums = (sums + parts[0]) + (parts[1] + parts[2])

    modes = call(
        adjoint_mix_body, 0, shaped((SPACE // 2, KX + 8, 128)),
        [full_spec((MODES + 8, 128))] * 4
        + [
            full_spec((operator_rows, 128)), full_spec((KOWN, 128, 128)),
            full_spec((KOWN, 128, 128)), full_spec((8, 128)),
        ],
        full_spec((SPACE // 2, KX + 8, 128)), name="adjoint_mix",
    )(sums, *from_y(sums, sums, sums), operator, spread_high, spread_low, misfits)
    modes, other_modes = gather_space(modes)
    local = local.reshape(4, 16, 8, 4, 4).transpose(1, 4, 0, 2, 3).reshape(64, 128)

    block, misfit = call(
        output_body, 2, (shaped((64, 128)), shaped((1, 4))),
        [
            full_spec((SPACE // 2, KX + 8, 128)), full_spec((SPACE // 2, KX + 8, 128)),
            own_spec((ROWS, 96)), own_spec((1024, 64), 1),
            full_spec((64, 128)), full_spec((96, 128)), full_spec((96, 96)),
            full_spec((1, 1024)), full_spec((1024, 1024)),
        ],
        (full_spec((64, 128)), full_spec((1, 4))), [pltpu.VMEM((128, 128), F32)],
        name="output_block",
    )(
        own, shot, modes, other_modes, jnp.asarray(ROWS_BACK), jnp.asarray(BLOCKS), local, jnp.asarray(DIAG_ROWS),
        jnp.asarray(OFF_ROWS), jnp.asarray(DIAG_WIDE), jnp.asarray(OFF_WIDE),
    )
    return (misfit.reshape(4), block.T)


def solution(mesh):
    in_specs = (
        P("space", None),
        P(),
        P(),
        P(),
        P("shot"),
        P("shot"),
        P("shot", None),
        P(),
        P(None, "space", None, None),
        P(),
        P(),
        P("shot", None, None),
    )
    out_specs = (P("shot"), P("space", "shot"))
    return jax.shard_map(shards, mesh=mesh, in_specs=in_specs, out_specs=out_specs, check_vma=False)
```

time: 727 us -> 151 us (0.21)
  waiting for transfers between devices: 317 us -> 21.9 us
  matrix products: 122 us -> 0 us
  local copies, waits for them, and re-layouts: 105 us -> 9.76 us
  blocking collectives: 113 us -> 21.8 us
  Pallas kernels: 0 us -> 45.2 us
  starting transfers between devices: 16.2 us -> 48.7 us
  other arithmetic: 29.5 us -> 1.55 us
  between operations: 15.7 us -> 0.79 us
    unnamed x3 -> x0, waiting for transfers between devices: 202 us -> none
    dot_general x23 -> x0, matrix products: 122 us -> none  [the longest x1 44.2 us: shards(): jnp.einsum('hawb,abc->chw', patches, encoder_weight, precision=HIGHEST)]
    psum x1 -> x0, blocking collectives: 95.7 us -> none  [shards(): total_squares = lax.psum(jnp.sum(own_block * own_block), ('shot', 'space'))]
    psum x1 -> x0, waiting for transfers between devices: 68 us -> none  [shards(): predicted = lax.psum(partial_rows, 'space')]
    unnamed x44, local copies, waits for them, and re-layouts: 56.7 us -> 6.08 us
    pallas_call x0 -> x12, Pallas kernels: none -> 45.2 us  [the longest x1 8.53 us: shards(): call(forward_body, 2, (shaped((PAIRS, GW)), shaped((PAIRS * C, GW), BF16)...]
    all_to_all x3, waiting for transfers between devices: 46.6 us -> 5.08 us  [the longest x1 4.77 us: shards(): stats = lax.all_to_all(stats, 'space', 0, 0, tiled=True)]
    reshape x2 -> x3, local copies, waits for them, and re-layouts: 37.8 us -> 2.01 us  [the longest x2 1.42 us: shards(): local.reshape(4, 16, 8, 4, 4).transpose(1, 4, 0, 2, 3).reshape(64, 128)]
  transfers between devices with their start and end apart: 5 -> 18, of which waited for: 5 -> 11; matrix products, arithmetic and copies ran while one was open for 1% -> 3% of each run, Pallas kernels for 0% -> 8%
where the time goes in v1:
time: 151 us; the launch traced here: 150 us
  starting transfers between devices  48.7 us (32%)
  Pallas kernels  45.2 us (30%)
  waiting for transfers between devices  21.9 us (15%)
  blocking collectives  21.8 us (14%)
  local copies, waits for them, and re-layouts  9.76 us (6%)
  other arithmetic  1.55 us (1%)
    all_to_all x2, blocking collectives, gather_space(): lax.all_to_all(copies, 'space', 0, 0, axis_index_groups=[[0, 2, 4, 6], [1...  21.8 us
    ppermute x6, starting transfers between devices, from_y(): lax.ppermute(part, 'shot', turn(4, 4, SHOT, by + 1))  10.2 us
    ppermute x6, waiting for transfers between devices, from_x(): lax.ppermute(part, 'shot', turn(4, 1, SHOT, by + 1))  9.54 us
    ppermute x6, starting transfers between devices, from_x(): lax.ppermute(part, 'shot', turn(4, 1, SHOT, by + 1))  9.25 us
    ppermute x2, starting transfers between devices, gather_space(): lax.ppermute(mine, 'space', [(n, n ^ 1) for n in range(SPACE)])  9.11 us
    pallas_call x1, Pallas kernels, shards(): call(forward_body, 2, (shaped((PAIRS, GW)), shaped((PAIRS * C, GW), BF16)...  8.53 us
    all_to_all x1, starting transfers between devices, shards(): spectra = lax.all_to_all(partial, 'space', 0, 0, tiled=True)  7.4 us
    pallas_call x1, Pallas kernels, shards(): call(backward_body, 3, (shaped((SPACE, ROWS, 384), BF16),) + (shaped((GW,...  7.28 us
  transfers between devices with their start and end apart: 18, of which 11 were waited for; matrix products, arithmetic and copies ran while one was open for 3% of the time, Pallas kernels for 8%

profile of v1, /device:TPU:1, one launch (start us, length us, event | category | flops | bytes accessed | tf_op | source)
XLA Modules:
  0.0 149.7 jit_solution(16677236632199442594)
XLA Ops:
  0.7 3.3 %velocity_spectrum.1 = f32[8,48,128]{2,1,0:T(8,128)} custom-call(s32[1]{0:T(128)} %bitcast.own, f32[128,2048]{1,0:T(8,128)} %v_ref.3, bf16[2048,256]{1,0:T(8,128)(2,1)} %constant.41.clone.cols_ref, bf16[8,192,256]{2,1,0:T(8,128)(2,1)} %constant.42.clone.rows_ref), custom_call_target="tpu_custom_call" | custom-call | tf_op jit(solution)/shard_map/velocity_spectrum/pallas_call | solution.py:654
  3.9 7.4 %all-to-all-start = ((f32[8,48,128]{2,1,0:T(8,128)}), f32[8,48,128]{2,1,0:T(8,128)S(1)}, u32[]{:S(2)}, u32[]{:S(2)}) async-start(f32[8,48,128]{2,1,0:T(8,128)} %velocity_spectrum.1), calls=%async_computation | async-start | bytes 393216 | tf_op jit(solution)/shard_map/all_to_all | solution.py:659
  12.5 5.0 %operator.1 = (f32[3456,128]{1,0:T(8,128)}, bf16[3,64,256]{2,1,0:T(8,128)(2,1)}, f32[64,512]{1,0:T(8,128)}) custom-call(s32[1]{0:T(128)} %bitcast.own, f32[16,64]{1,0:T(8,128)} %bitcast.18, f32[1,64]{1,0:T(1,128)} %bitcast.20, f32[1,64]{1,0:T(1,128)} %bitcast.22, bf16[48,3,64,128]{3,2,1,0:T(8,128)(2,1)} %w_ref.1, f32[64,3]{1,0:T(8,128)} %convert_element_type.3.index_ref, ...), custom_call_target="tpu_custom_call" | custom-call | tf_op jit(solution)/shard_map/operator/pallas_call | solution.py:662
  18.5 3.7 %mix_modes.1 = bf16[4,64,384]{2,1,0:T(8,128)(2,1)} custom-call(s32[1]{0:T(128)} %bitcast.own, f32[8,48,128]{2,1,0:T(8,128)} %copy-done.2, f32[8,48,128]{2,1,0:T(8,128)} %constant.45.clone.ones_ref, f32[3456,128]{1,0:T(8,128)} %get-tuple-element.31.t_ref, bf16[3,64,256]{2,1,0:T(8,128)(2,1)} %get-tuple-element.32.l_ref), custom_call_target="tpu_custom_call" | custom-call | tf_op jit(solution)/shard_map/mix_modes/pallas_call | solution.py:676
  22.2 9.9 %all_to_all.25.d_ref = bf16[4,64,384]{2,1,0:T(8,128)(2,1)S(1)} all-to-all(bf16[4,64,384]{2,1,0:T(8,128)(2,1)} %mix_modes.1), channel_id=1, replica_groups={{0,2,4,6},{1,3,5,7},{8,10,12,14},{9,11,13,15},{16,18,20,22},{17,19,21,2..., dimensions={0} | all-to-all | bytes 393216 | tf_op jit(solution)/shard_map/all_to_all | solution.py:618
  32.1 2.8 %collective-permute-start = (bf16[4,64,384]{2,1,0:T(8,128)(2,1)S(1)}, bf16[4,64,384]{2,1,0:T(8,128)(2,1)S(1)}, u32[]{:S(2)}, u32[]{:S(2)}) collective-permute-start(bf16[4,64,384]{2,1,0:T(8,128)(2,1)S(1)} %all_to_all.25.d_ref), channel_id=1, source_target_pairs={{0,1},{1,0},{2,3},{3,2},{4,5},{5,4},{6,7},{7,6},{8,9},{9,8},{10,11... | collective-permute-start | bytes 589832 | tf_op jit(solution)/shard_map/ppermute | solution.py:621
  35.5 3.5 %velocity_planes.1 = (f32[32,16,512]{2,1,0:T(8,128)}, bf16[48,64]{1,0:T(8,128)(2,1)}, f32[3,64,128]{2,1,0:T(8,128)}, bf16[8,128,128]{2,1,0:T(8,128)(2,1)}, bf16[...) custom-call(s32[1]{0:T(128)} %bitcast.own, f32[128,2048]{1,0:T(8,128)} %v_ref.3, ...), custom_call_target="tpu_custom_call" | custom-call | tf_op jit(solution)/shard_map/velocity_planes/pallas_call | solution.py:687
  39.7 8.5 %forward_rows.1 = (f32[64,512]{1,0:T(8,128)}, bf16[4096,512]{1,0:T(8,128)(2,1)}, f32[8,8,128]{2,1,0:T(8,128)}) custom-call(s32[1]{0:T(128)} %bitcast.own, s32[64]{0:T(128)} %reshape.22.rows_ref, bf16[4,64,384]{2,1,0:T(8,128)(2,1)} %copy-done, bf16[4,64,384]{2,1,0:T(8,128)(2,1)} %copy-done.5, f32[32,16,512]{2,1,0:T(8,128)} %get-tuple-element.34.planes_ref, ...), custom_call_target="tpu_custom_call" | custom-call | tf_op jit(solution)/shard_map/forward_rows/pallas_call | solution.py:708
  48.2 3.3 %all-to-all-start.2 = ((f32[8,8,128]{2,1,0:T(8,128)}), f32[8,8,128]{2,1,0:T(8,128)S(1)}, u32[]{:S(2)}, u32[]{:S(2)}) async-start(f32[8,8,128]{2,1,0:T(8,128)} %get-tuple-element.38), calls=%async_computation.2 | async-start | bytes 65536 | tf_op jit(solution)/shard_map/all_to_all | solution.py:720
  51.5 4.8 %all-to-all-done.2.stats_ref = f32[8,8,128]{2,1,0:T(8,128)S(1)} async-done(((f32[8,8,128]{2,1,0:T(8,128)}), f32[8,8,128]{2,1,0:T(8,128)S(1)}, u32[]{:S(2)}, u32[]{:S(2)}) %all-to-all-start.2) | async-done | bytes 32800 | tf_op jit(solution)/shard_map/all_to_all | solution.py:720
  56.9 7.3 %backward_rows.1 = (bf16[8,32,384]{2,1,0:T(8,128)(2,1)}, bf16[512,128]{1,0:T(8,128)(2,1)}, bf16[512,128]{1,0:T(8,128)(2,1)}, bf16[512,128]{1,0:T(8,128)(2,1)}, b...) custom-call(s32[1]{0:T(128)} %bitcast.own, s32[64]{0:T(128)} %reshape.22.rows_ref, s32[1]{0:T(128)} %bitcast.1.shot, ...), custom_call_target="tpu_custom_call" | custom-call | tf_op jit(solution)/shard_map/backward_rows/pallas_call | solution.py:722
  64.2 3.4 %all-to-all-start.3 = ((bf16[8,32,384]{2,1,0:T(8,128)(2,1)}), bf16[8,32,384]{2,1,0:T(8,128)(2,1)S(1)}, u32[]{:S(2)}, u32[]{:S(2)}) async-start(bf16[8,32,384]{2,1,0:T(8,128)(2,1)} %get-tuple-element.50), calls=%async_computation.3 | async-start | bytes 393216 | tf_op jit(solution)/shard_map/all_to_all | solution.py:738
  69.1 3.1 %collective-permute-start.2 = (bf16[512,128]{1,0:T(8,128)(2,1)}, bf16[512,128]{1,0:T(8,128)(2,1)S(1)}, u32[]{:S(2)}, u32[]{:S(2)}) collective-permute-start(bf16[512,128]{1,0:T(8,128)(2,1)} %get-tuple-element.44), channel_id=1, source_target_pairs={{0,16},{8,24},{16,0},{24,8},{32,48},{40,56},{48,32},{56,40},{64,80... | collective-permute-start | bytes 393224 | tf_op jit(solution)/shard_map/ppermute | solution.py:607
  74.9 3.7 %collective-permute-done.2.c_ref = bf16[512,128]{1,0:T(8,128)(2,1)S(1)} collective-permute-done((bf16[512,128]{1,0:T(8,128)(2,1)}, bf16[512,128]{1,0:T(8,128)(2,1)S(1)}, u32[]{:S(2)}, u32[]{:S(2)}) %collective-permute-start.2) | collective-permute-done | bytes 131104 | tf_op jit(solution)/shard_map/ppermute | solution.py:607
  81.3 5.0 %collective-permute-start.4 = (f32[128,128]{1,0:T(8,128)}, f32[128,128]{1,0:T(8,128)S(1)}, u32[]{:S(2)}, u32[]{:S(2)}) collective-permute-start(f32[128,128]{1,0:T(8,128)} %get-tuple-element.47), channel_id=1, source_target_pairs={{0,32},{8,40},{16,48},{24,56},{32,64},{40,72},{48,80},{56,88},{64,... | collective-permute-start | bytes 196616 | tf_op jit(solution)/shard_map/ppermute | solution.py:613
  86.4 2.4 %collective-permute-start.6 = (f32[128,128]{1,0:T(8,128)}, f32[128,128]{1,0:T(8,128)S(1)}, u32[]{:S(2)}, u32[]{:S(2)}) collective-permute-start(f32[128,128]{1,0:T(8,128)} %get-tuple-element.49), channel_id=1, source_target_pairs={{0,96},{8,104},{16,112},{24,120},{32,0},{40,8},{48,16},{56,24},{64... | collective-permute-start | bytes 196616 | tf_op jit(solution)/shard_map/ppermute | solution.py:613
  93.7 6.0 %collective-permute-start.7 = (f32[272,128]{1,0:T(8,128)}, f32[272,128]{1,0:T(8,128)S(1)}, u32[]{:S(2)}, u32[]{:S(2)}) collective-permute-start(f32[272,128]{1,0:T(8,128)} %along_y.1.a_ref), channel_id=1, source_target_pairs={{0,128},{8,136},{16,144},{24,152},{32,160},{40,168},{48,176},{56,1... | collective-permute-start | bytes 417800 | tf_op jit(solution)/shard_map/ppermute | solution.py:759
  99.7 2.8 %collective-permute-done.7.b_ref = f32[272,128]{1,0:T(8,128)S(1)} collective-permute-done((f32[272,128]{1,0:T(8,128)}, f32[272,128]{1,0:T(8,128)S(1)}, u32[]{:S(2)}, u32[]{:S(2)}) %collective-permute-start.7) | collective-permute-done | bytes 139296 | tf_op jit(solution)/shard_map/ppermute | solution.py:759
  109.5 2.5 %collective-permute-done.9 = f32[152,128]{1,0:T(8,128)S(1)} collective-permute-done((f32[152,128]{1,0:T(8,128)}, f32[152,128]{1,0:T(8,128)S(1)}, u32[]{:S(2)}, u32[]{:S(2)}) %collective-permute-start.9) | collective-permute-done | bytes 77856 | tf_op jit(solution)/shard_map/ppermute | solution.py:607
  117.6 2.7 %collective-permute-done.12.far_ref = f32[152,128]{1,0:T(8,128)S(1)} collective-permute-done((f32[152,128]{1,0:T(8,128)S(1)}, f32[152,128]{1,0:T(8,128)S(1)}, u32[]{:S(2)}, u32[]{:S(2)}) %collective-permute-start.12) | collective-permute-done | bytes 77856 | tf_op jit(solution)/shard_map/ppermute | solution.py:613
  121.3 3.2 %adjoint_mix.1 = f32[4,56,128]{2,1,0:T(8,128)} custom-call(f32[152,128]{1,0:T(8,128)} %copy-done.4, f32[152,128]{1,0:T(8,128)} %copy-done.14, f32[152,128]{1,0:T(8,128)} %copy-done.13, f32[152,128]{1,0:T(8,128)} %copy-done.12, f32[3456,128]{1,0:T(8,128)} %get-tuple-element.31.t_ref, bf16[3,128,128]{2,1,0:T(8,128)(2,1)} %get-tuple-element.52.high_ref, ...), custom_call_target="tpu_custom_call" | custom-call | tf_op jit(solution)/shard_map/adjoint_mix/pallas_call | solution.py:763
  124.6 12.0 %all_to_all.26.m_ref = f32[4,56,128]{2,1,0:T(8,128)S(1)} all-to-all(f32[4,56,128]{2,1,0:T(8,128)} %adjoint_mix.1), channel_id=1, replica_groups={{0,2,4,6},{1,3,5,7},{8,10,12,14},{9,11,13,15},{16,18,20,22},{17,19,21,2..., dimensions={0} | all-to-all | bytes 229376 | tf_op jit(solution)/shard_map/all_to_all | solution.py:618
  136.6 6.3 %collective-permute-start.14 = (f32[4,56,128]{2,1,0:T(8,128)S(1)}, f32[4,56,128]{2,1,0:T(8,128)S(1)}, u32[]{:S(2)}, u32[]{:S(2)}) collective-permute-start(f32[4,56,128]{2,1,0:T(8,128)S(1)} %all_to_all.26.m_ref), channel_id=1, source_target_pairs={{0,1},{1,0},{2,3},{3,2},{4,5},{5,4},{6,7},{7,6},{8,9},{9,8},{10,11... | collective-permute-start | bytes 344072 | tf_op jit(solution)/shard_map/ppermute | solution.py:621
  146.1 3.6 %output_block.1 = (f32[64,128]{1,0:T(8,128)}, f32[1,4]{1,0:T(1,128)}) custom-call(s32[1]{0:T(128)} %bitcast.own, s32[1]{0:T(128)} %bitcast.1.shot, f32[4,56,128]{2,1,0:T(8,128)} %copy-done.3, f32[4,56,128]{2,1,0:T(8,128)} %copy-done.11, bf16[8,32,96]{2,1,0:T(8,128)(2,1)} %constant.48.clone.back_ref, bf16[32,1024,64]{2,1,0:T(8,128)(2,1)} %constant.49.clone.block_ref, ...), custom_call_target="tpu_custom_call" | custom-call | tf_op jit(solution)/shard_map/output_block/pallas_call | solution.py:775
  (84 shorter events, 32.7 us)
Async XLA Ops:
  0.6 10.7 %copy-start.19 = (s32[4,16]{1,0:T(4,128)S(1)}, s32[4,16]{1,0:T(4,128)}, u32[]{:S(2)}) copy-start(s32[4,16]{1,0:T(4,128)} %param.33) | copy-start | bytes 772
  0.6 10.8 %copy-start.20 = (s32[4]{0:T(128)S(1)}, s32[4]{0:T(128)}, u32[]{:S(2)}) copy-start(s32[4]{0:T(128)} %param.31) | copy-start | bytes 52
  0.7 10.9 %copy-start.21 = (s32[4]{0:T(128)S(1)}, s32[4]{0:T(128)}, u32[]{:S(2)}) copy-start(s32[4]{0:T(128)} %param.32) | copy-start | bytes 52
  3.9 13.9 %all-to-all-start = ((f32[8,48,128]{2,1,0:T(8,128)}), f32[8,48,128]{2,1,0:T(8,128)S(1)}, u32[]{:S(2)}, u32[]{:S(2)}) async-start(f32[8,48,128]{2,1,0:T(8,128)} %velocity_spectrum.1), calls=%async_computation | async-start | bytes 393216 | tf_op jit(solution)/shard_map/all_to_all | solution.py:659
  32.1 6.9 %collective-permute-start = (bf16[4,64,384]{2,1,0:T(8,128)(2,1)S(1)}, bf16[4,64,384]{2,1,0:T(8,128)(2,1)S(1)}, u32[]{:S(2)}, u32[]{:S(2)}) collective-permute-start(bf16[4,64,384]{2,1,0:T(8,128)(2,1)S(1)} %all_to_all.25.d_ref), channel_id=1, source_target_pairs={{0,1},{1,0},{2,3},{3,2},{4,5},{5,4},{6,7},{7,6},{8,9},{9,8},{10,11... | collective-permute-start | bytes 589832 | tf_op jit(solution)/shard_map/ppermute | solution.py:621
  48.2 8.1 %all-to-all-start.2 = ((f32[8,8,128]{2,1,0:T(8,128)}), f32[8,8,128]{2,1,0:T(8,128)S(1)}, u32[]{:S(2)}, u32[]{:S(2)}) async-start(f32[8,8,128]{2,1,0:T(8,128)} %get-tuple-element.38), calls=%async_computation.2 | async-start | bytes 65536 | tf_op jit(solution)/shard_map/all_to_all | solution.py:720
  64.2 24.6 %all-to-all-start.3 = ((bf16[8,32,384]{2,1,0:T(8,128)(2,1)}), bf16[8,32,384]{2,1,0:T(8,128)(2,1)S(1)}, u32[]{:S(2)}, u32[]{:S(2)}) async-start(bf16[8,32,384]{2,1,0:T(8,128)(2,1)} %get-tuple-element.50), calls=%async_computation.3 | async-start | bytes 393216 | tf_op jit(solution)/shard_map/all_to_all | solution.py:738
  67.6 7.3 %collective-permute-start.1 = (bf16[512,128]{1,0:T(8,128)(2,1)}, bf16[512,128]{1,0:T(8,128)(2,1)S(1)}, u32[]{:S(2)}, u32[]{:S(2)}) collective-permute-start(bf16[512,128]{1,0:T(8,128)(2,1)} %get-tuple-element.43), channel_id=1, source_target_pairs={{0,8},{8,16},{16,24},{24,0},{32,40},{40,48},{48,56},{56,32},{64,72... | collective-permute-start | bytes 393224 | tf_op jit(solution)/shard_map/ppermute | solution.py:607
  69.1 9.6 %collective-permute-start.2 = (bf16[512,128]{1,0:T(8,128)(2,1)}, bf16[512,128]{1,0:T(8,128)(2,1)S(1)}, u32[]{:S(2)}, u32[]{:S(2)}) collective-permute-start(bf16[512,128]{1,0:T(8,128)(2,1)} %get-tuple-element.44), channel_id=1, source_target_pairs={{0,16},{8,24},{16,0},{24,8},{32,48},{40,56},{48,32},{56,40},{64,80... | collective-permute-start | bytes 393224 | tf_op jit(solution)/shard_map/ppermute | solution.py:607
  72.2 6.5 %collective-permute-start.3 = (bf16[512,128]{1,0:T(8,128)(2,1)}, bf16[512,128]{1,0:T(8,128)(2,1)S(1)}, u32[]{:S(2)}, u32[]{:S(2)}) collective-permute-start(bf16[512,128]{1,0:T(8,128)(2,1)} %get-tuple-element.45), channel_id=1, source_target_pairs={{0,24},{8,0},{16,8},{24,16},{32,56},{40,32},{48,40},{56,48},{64,88... | collective-permute-start | bytes 393224 | tf_op jit(solution)/shard_map/ppermute | solution.py:607
  81.3 9.9 %collective-permute-start.4 = (f32[128,128]{1,0:T(8,128)}, f32[128,128]{1,0:T(8,128)S(1)}, u32[]{:S(2)}, u32[]{:S(2)}) collective-permute-start(f32[128,128]{1,0:T(8,128)} %get-tuple-element.47), channel_id=1, source_target_pairs={{0,32},{8,40},{16,48},{24,56},{32,64},{40,72},{48,80},{56,88},{64,... | collective-permute-start | bytes 196616 | tf_op jit(solution)/shard_map/ppermute | solution.py:613
  86.4 4.9 %collective-permute-start.5 = (f32[128,128]{1,0:T(8,128)}, f32[128,128]{1,0:T(8,128)S(1)}, u32[]{:S(2)}, u32[]{:S(2)}) collective-permute-start(f32[128,128]{1,0:T(8,128)} %get-tuple-element.48), channel_id=1, source_target_pairs={{0,64},{8,72},{16,80},{24,88},{32,96},{40,104},{48,112},{56,120},{... | collective-permute-start | bytes 196616 | tf_op jit(solution)/shard_map/ppermute | solution.py:613
  86.4 4.9 %collective-permute-start.6 = (f32[128,128]{1,0:T(8,128)}, f32[128,128]{1,0:T(8,128)S(1)}, u32[]{:S(2)}, u32[]{:S(2)}) collective-permute-start(f32[128,128]{1,0:T(8,128)} %get-tuple-element.49), channel_id=1, source_target_pairs={{0,96},{8,104},{16,112},{24,120},{32,0},{40,8},{48,16},{56,24},{64... | collective-permute-start | bytes 196616 | tf_op jit(solution)/shard_map/ppermute | solution.py:613
  93.7 8.7 %collective-permute-start.7 = (f32[272,128]{1,0:T(8,128)}, f32[272,128]{1,0:T(8,128)S(1)}, u32[]{:S(2)}, u32[]{:S(2)}) collective-permute-start(f32[272,128]{1,0:T(8,128)} %along_y.1.a_ref), channel_id=1, source_target_pairs={{0,128},{8,136},{16,144},{24,152},{32,160},{40,168},{48,176},{56,1... | collective-permute-start | bytes 417800 | tf_op jit(solution)/shard_map/ppermute | solution.py:759
  104.7 38.1 %copy-start.18 = (f32[64,128]{1,0:T(8,128)S(1)}, f32[64,128]{1,0:T(8,128)}, u32[]{:S(2)}) copy-start(f32[64,128]{1,0:T(8,128)} %get-tuple-element.55) | copy-start | bytes 98308
  104.7 4.7 %collective-permute-start.10 = (f32[152,128]{1,0:T(8,128)}, f32[152,128]{1,0:T(8,128)S(1)}, u32[]{:S(2)}, u32[]{:S(2)}) collective-permute-start(f32[152,128]{1,0:T(8,128)} %get-tuple-element.51), channel_id=1, source_target_pairs={{0,24},{8,0},{16,8},{24,16},{32,56},{40,32},{48,40},{56,48},{64,88... | collective-permute-start | bytes 233480 | tf_op jit(solution)/shard_map/ppermute | solution.py:607
  106.9 5.1 %collective-permute-start.9 = (f32[152,128]{1,0:T(8,128)}, f32[152,128]{1,0:T(8,128)S(1)}, u32[]{:S(2)}, u32[]{:S(2)}) collective-permute-start(f32[152,128]{1,0:T(8,128)} %get-tuple-element.51), channel_id=1, source_target_pairs={{0,16},{8,24},{16,0},{24,8},{32,48},{40,56},{48,32},{56,40},{64,80... | collective-permute-start | bytes 233480 | tf_op jit(solution)/shard_map/ppermute | solution.py:607
  106.9 5.5 %collective-permute-start.8 = (f32[152,128]{1,0:T(8,128)}, f32[152,128]{1,0:T(8,128)S(1)}, u32[]{:S(2)}, u32[]{:S(2)}) collective-permute-start(f32[152,128]{1,0:T(8,128)} %get-tuple-element.51), channel_id=1, source_target_pairs={{0,8},{8,16},{16,24},{24,0},{32,40},{40,48},{48,56},{56,32},{64,72... | collective-permute-start | bytes 233480 | tf_op jit(solution)/shard_map/ppermute | solution.py:607
  113.3 7.4 %copy-start.4 = (f32[152,128]{1,0:T(8,128)}, f32[152,128]{1,0:T(8,128)S(1)}, u32[]{:S(2)}) copy-start(f32[152,128]{1,0:T(8,128)S(1)} %add_add_fusion.near_ref) | copy-start | bytes 233476
  113.4 4.2 %collective-permute-start.13 = (f32[152,128]{1,0:T(8,128)S(1)}, f32[152,128]{1,0:T(8,128)S(1)}, u32[]{:S(2)}, u32[]{:S(2)}) collective-permute-start(f32[152,128]{1,0:T(8,128)S(1)} %add_add_fusion.near_ref), channel_id=1, source_target_pairs={{0,96},{8,104},{16,112},{24,120},{32,0},{40,8},{48,16},{56,24},{64... | collective-permute-start | bytes 233480 | tf_op jit(solution)/shard_map/ppermute | solution.py:613
  115.4 4.9 %collective-permute-start.12 = (f32[152,128]{1,0:T(8,128)S(1)}, f32[152,128]{1,0:T(8,128)S(1)}, u32[]{:S(2)}, u32[]{:S(2)}) collective-permute-start(f32[152,128]{1,0:T(8,128)S(1)} %add_add_fusion.near_ref), channel_id=1, source_target_pairs={{0,64},{8,72},{16,80},{24,88},{32,96},{40,104},{48,112},{56,120},{... | collective-permute-start | bytes 233480 | tf_op jit(solution)/shard_map/ppermute | solution.py:613
  115.4 5.3 %collective-permute-start.11 = (f32[152,128]{1,0:T(8,128)S(1)}, f32[152,128]{1,0:T(8,128)S(1)}, u32[]{:S(2)}, u32[]{:S(2)}) collective-permute-start(f32[152,128]{1,0:T(8,128)S(1)} %add_add_fusion.near_ref), channel_id=1, source_target_pairs={{0,32},{8,40},{16,48},{24,56},{32,64},{40,72},{48,80},{56,88},{64,... | collective-permute-start | bytes 233480 | tf_op jit(solution)/shard_map/ppermute | solution.py:613
  136.6 8.9 %copy-start.3 = (f32[4,56,128]{2,1,0:T(8,128)}, f32[4,56,128]{2,1,0:T(8,128)S(1)}, u32[]{:S(2)}) copy-start(f32[4,56,128]{2,1,0:T(8,128)S(1)} %all_to_all.26.m_ref) | copy-start | bytes 344068
  136.6 8.9 %collective-permute-start.14 = (f32[4,56,128]{2,1,0:T(8,128)S(1)}, f32[4,56,128]{2,1,0:T(8,128)S(1)}, u32[]{:S(2)}, u32[]{:S(2)}) collective-permute-start(f32[4,56,128]{2,1,0:T(8,128)S(1)} %all_to_all.26.m_ref), channel_id=1, source_target_pairs={{0,1},{1,0},{2,3},{3,2},{4,5},{5,4},{6,7},{7,6},{8,9},{9,8},{10,11... | collective-permute-start | bytes 344072 | tf_op jit(solution)/shard_map/ppermute | solution.py:621
  (16 other events, 22.5 us)

commit v2 on v1

--- a/solution.py
+++ b/solution.py
@@ -19,6 +19,8 @@
 SHOT = 32
 ROWS = GH // SPACE
 KOWN = KY // SPACE
+COUNT = 64
+FIRST = 72
 PAIRS = 64
 EPSILON = 1e-06
 VELOCITY_MEAN = 3.0
@@ -26,7 +28,8 @@
 HIGHEST = lax.Precision.HIGHEST
 F32 = jnp.float32
 BF16 = jnp.bfloat16
-VMEM_LIMIT = 56 << 20
+SMALL = 28 << 20
+LARGE = 56 << 20
 
 
 def bf(values):
@@ -190,7 +193,11 @@
     return pl.BlockSpec((1,) + shape, lambda i, *own: (own[place][0],) + (0,) * len(shape))
 
 
-def call(body, prefetch, out_shape, in_specs, out_specs, scratch=(), name=None):
+def kept_spec(shape):
+    return pl.BlockSpec(memory_space=pltpu.VMEM)
+
+
+def call(body, prefetch, out_shape, in_specs, out_specs, scratch=(), name=None, limit=LARGE):
     return pl.pallas_call(
         body,
         out_shape=out_shape,
@@ -201,7 +208,7 @@
             out_specs=out_specs,
             scratch_shapes=list(scratch),
         ),
-        compiler_params=pltpu.CompilerParams(vmem_limit_bytes=VMEM_LIMIT),
+        compiler_params=pltpu.CompilerParams(vmem_limit_bytes=limit),
         name=name,
     )
 
@@ -235,9 +242,16 @@
 
 
 def planes_body(
-    own, v_ref, sel_ref, enc_ref, bias_ref, amp_ref, point_ref, layer_ref, weight_ref, lanes_ref,
-    out_ref, wk_ref, vec_ref, place_ref, high_ref, low_ref, tmp,
+    own, rows_ref, v_ref, sel_ref, enc_ref, bias_ref, amp_ref, point_ref, layer_ref, weight_ref, lanes_ref,
+    out_ref, wk_ref, vec_ref, place_ref, high_ref, low_ref, list_ref, tmp,
 ):
+    def find(r, count):
+        row = rows_ref[r >> 4, r & 15] - own[0] * ROWS
+        list_ref[count] = r
+        list_ref[FIRST + count] = row
+        return count + jnp.where((row >= 0) & (row < ROWS), 1, 0)
+
+    list_ref[COUNT] = lax.fori_loop(0, PAIRS, find, 0)
     for m in range(4):
         vn = (v_ref[:, 512 * m : 512 * m + 512] - VELOCITY_MEAN) / VELOCITY_SCALE
         high, low = split(vn)
@@ -279,7 +293,8 @@
 
 
 def operator_body(
-    own, enc_ref, bias_ref, amp_ref, w_ref, index_ref, rows_ref, cols_ref, out_ref, side_ref, bump_ref
+    own, source_row, source_column, enc_ref, bias_ref, amp_ref, w_ref, index_ref, rows_ref,
+    cols_ref, out_ref, side_ref, bump_ref,
 ):
     stack = jnp.concatenate(
         [enc_ref[...], bias_ref[...], amp_ref[...], jnp.zeros((6, C), F32)], axis=0
@@ -294,7 +309,17 @@
         return carry
 
     lax.fori_loop(0, KX, step, 0, unroll=8)
-    receiver, row, column = index_ref[:, 0:1], index_ref[:, 1:2], index_ref[:, 2:3]
+    square = (REC, REC)
+    same = lax.broadcasted_iota(jnp.int32, square, 0) == lax.broadcasted_iota(jnp.int32, square, 1)
+    receivers, row, column = [], [], []
+    for s in range(4):
+        wide = jnp.broadcast_to(index_ref[s : s + 1, :].astype(F32), square)
+        receivers.append(jnp.sum(jnp.where(same, wide, 0.0), axis=1, keepdims=True))
+        row.append(jnp.full((REC, 1), source_row[s], jnp.int32).astype(F32))
+        column.append(jnp.full((REC, 1), source_column[s], jnp.int32).astype(F32))
+    receiver = jnp.concatenate(receivers, axis=0)
+    row = jnp.concatenate(row, axis=0)
+    column = jnp.concatenate(column, axis=0)
     line = lax.broadcasted_iota(jnp.int32, (PAIRS, GH), 1).astype(F32)
     chosen = jnp.where(line == receiver, 1.0, 0.0).astype(BF16)
     at_rows = dot(chosen, rows_ref[...], ((1,), (1,)))
@@ -349,10 +374,11 @@
 
 
 def forward_body(
-    own, rows_ref, d_ref, other_ref, planes_ref, table_ref, wk_ref, col_ref, vec_ref, obs_ref,
-    pred_ref, slope_ref, stats_ref, dd, acc,
+    own, list_ref, d_ref, other_ref, planes_ref, table_ref, wk_ref, col_ref, vec_ref, obs_ref,
+    pred_ref, slope_ref, stats_ref, dd, acc, slopes, sems,
 ):
     p = own[0]
+    count = list_ref[COUNT]
     gain = gain_row()
     for m in range(3):
         for z in range(SPACE // 2):
@@ -362,22 +388,28 @@
     acc[...] = jnp.zeros_like(acc)
     root = math.sqrt(2.0 / math.pi)
 
-    def step(r, carry):
-        row = rows_ref[r] - p * ROWS
-
-        @pl.when((row >= 0) & (row < ROWS))
-        def _():
-            s = r // REC
-            pieces = []
-            for m in range(3):
-                block = dd[pl.ds(SPACE * PAIRS * m + r, SPACE, stride=PAIRS), :]
-                pieces.append(block[:, :64])
-                pieces.append(pltpu.roll(block, 64, 1)[:, :64])
-            lhs = jnp.concatenate(pieces, axis=0).astype(BF16)
-            lhs = jnp.concatenate([lhs, wk_ref[...]], axis=0)
-            high, low = split(planes_ref[row])
-            rhs = jnp.concatenate([table_ref[...], high, low, high], axis=0)
-            x = dot(lhs, rhs, ((0,), (0,)))
+    def preactivation(n):
+        r = list_ref[n]
+        pieces = []
+        for m in range(3):
+            block = dd[pl.ds(SPACE * PAIRS * m + r, SPACE, stride=PAIRS), :]
+            pieces.append(block[:, :64])
+            pieces.append(pltpu.roll(block, 64, 1)[:, :64])
+        lhs = jnp.concatenate(pieces, axis=0).astype(BF16)
+        lhs = jnp.concatenate([lhs, wk_ref[...]], axis=0)
+        high, low = split(planes_ref[list_ref[FIRST + n]])
+        rhs = jnp.concatenate([table_ref[...], high, low, high], axis=0)
+        return r, dot(lhs, rhs, ((0,), (0,)))
+
+    def outgoing(t):
+        rows = pl.ds(pl.multiple_of(2 * C * t, 2 * C), 2 * C)
+        return pltpu.make_async_copy(slopes.at[rows], slope_ref.at[rows], sems.at[t])
+
+    def step(t, carry):
+        second = jnp.minimum(2 * t + 1, count - 1)
+        both = [preactivation(2 * t), preactivation(second)]
+        weights = [1.0, jnp.where(2 * t + 1 < count, 1.0, 0.0)]
+        for e, (r, x) in enumerate(both):
             amp, const, weight = vec_ref[0], vec_ref[1], vec_ref[2]
             col = col_ref[pl.ds(r, 1), :]
             total = []
@@ -385,33 +417,51 @@
                 lanes = slice(128 * m, 128 * m + 128)
                 xm = x[:, lanes] + const + amp * col[:, lanes]
                 square = xm * xm
-                t = jnp.tanh(root * (xm + 0.044715 * (square * xm)))
-                cdf = 0.5 * (1.0 + t)
+                u = jnp.tanh(root * (xm + 0.044715 * (square * xm)))
+                cdf = 0.5 * (1.0 + u)
                 slope = cdf + xm * (
-                    (0.5 * root) * (1.0 - t * t) * (1.0 + 3.0 * 0.044715 * square)
+                    (0.5 * root) * (1.0 - u * u) * (1.0 + 3.0 * 0.044715 * square)
                 )
-                slope_ref[pl.ds(pl.multiple_of(r * C, C), C), lanes] = (slope * weight).astype(BF16)
+                slopes[pl.ds(pl.multiple_of(C * (2 * t + e), C), C), lanes] = (
+                    slope * weight
+                ).astype(BF16)
                 total.append(jnp.sum(weight * (xm * cdf), axis=0, keepdims=True))
             predicted = jnp.concatenate(total, axis=1)
             pred_ref[pl.ds(r, 1), :] = predicted
-            weighted = predicted * gain
+            weighted = predicted * gain * weights[e]
             target = obs_ref[pl.ds(r, 1), :] * gain
+            s = r >> 4
             acc[pl.ds(s, 1), :] += weighted * weighted
             acc[pl.ds(s + 4, 1), :] += weighted * target
-
+        outgoing(t).start()
         return carry
 
-    lax.fori_loop(0, PAIRS, step, 0)
+    def finish(t, carry):
+        outgoing(t).wait()
+        return carry
+
+    lax.fori_loop(0, (count + 1) >> 1, step, 0)
     stats = acc[:, :128] + acc[:, 128:256] + acc[:, 256:384] + acc[:, 384:]
     for q in range(SPACE):
         stats_ref[q] = stats
+    lax.fori_loop(0, (count + 1) >> 1, finish, 0)
 
 
 def backward_body(
-    own, rows_ref, shot, stats_ref, obs_ref, pred_ref, slope_ref, table_ref, place_ref,
-    cols_ref, near_ref, next_ref, far_ref, last_ref, misfit_ref, coef, acc, planes,
+    own, list_ref, shot, stats_ref, obs_ref, pred_ref, slope_ref, table_ref, place_ref,
+    cols_ref, near_ref, next_ref, far_ref, last_ref, misfit_ref, coef, acc, planes, slopes, sems,
 ):
-    p = own[0]
+    pairs = list_ref[COUNT]
+
+    def incoming(t):
+        rows = pl.ds(pl.multiple_of(2 * C * t, 2 * C), 2 * C)
+        return pltpu.make_async_copy(slope_ref.at[rows], slopes.at[rows], sems.at[t])
+
+    def begin(t, carry):
+        incoming(t).start()
+        return carry
+
+    lax.fori_loop(0, (pairs + 1) >> 1, begin, 0)
     count = float(REC * GW)
     stats = stats_ref[0]
     for q in range(1, SPACE):
@@ -434,37 +484,41 @@
     acc[...] = jnp.zeros_like(acc)
     planes[...] = jnp.zeros_like(planes)
 
-    def step(r, carry):
-        row = rows_ref[r] - p * ROWS
-
-        @pl.when((row >= 0) & (row < ROWS))
-        def _():
-            s = r // REC
-            isp = coef[pl.ds(s, 1), :]
-            isq = coef[pl.ds(s + 4, 1), :]
-            kappa = coef[pl.ds(s + 8, 1), :]
-            weighted = pred_ref[pl.ds(r, 1), :] * gain * isp
-            target = obs_ref[pl.ds(r, 1), :] * gain * isq
-            differ = weighted - target
-            coef[pl.ds(s + 12, 1), :] += differ * differ
-            data = (GH * GW / count) * gain * isp * (differ - kappa * weighted)
-            slope = slope_ref[pl.ds(pl.multiple_of(r * C, C), C), :].astype(F32)
-            inner = (slope * data).astype(BF16)
-            spectra = dot(table_ref[...], inner, ((1,), (1,)))
-            acc[pl.ds(pl.multiple_of(row * 48, 8), 48), 0:64] += spectra
-            eighth = row % 8
-            two = jnp.concatenate([inner, inner], axis=0)
-            planes[row // 8] += dot(two, place_ref[eighth], ((0,), (0,)))
-
+    def inner_gradient(t, e, r, valid):
+        s = r >> 4
+        isp = coef[pl.ds(s, 1), :]
+        isq = coef[pl.ds(s + 4, 1), :]
+        kappa = coef[pl.ds(s + 8, 1), :]
+        weighted = pred_ref[pl.ds(r, 1), :] * gain * isp
+        target = obs_ref[pl.ds(r, 1), :] * gain * isq
+        differ = (weighted - target) * valid
+        coef[pl.ds(s + 12, 1), :] += differ * differ
+        data = (GH * GW / count) * gain * isp * (differ - kappa * weighted * valid)
+        slope = slopes[pl.ds(pl.multiple_of(C * (2 * t + e), C), C), :].astype(F32)
+        return (slope * data).astype(BF16)
+
+    def step(t, carry):
+        second = jnp.minimum(2 * t + 1, pairs - 1)
+        valid = jnp.where(2 * t + 1 < pairs, 1.0, 0.0)
+        incoming(t).wait()
+        one = inner_gradient(t, 0, list_ref[2 * t], 1.0)
+        two = inner_gradient(t, 1, list_ref[second], valid)
+        spectra = dot(table_ref[...], jnp.concatenate([one, two], axis=0), ((1,), (1,)))
+        for e, (n, inner) in enumerate(((2 * t, one), (second, two))):
+            row = list_ref[FIRST + n]
+            half = slice(64 * e, 64 * e + 64)
+            acc[pl.ds(pl.multiple_of(row * 48, 8), 48), half] += spectra[:, half]
+            twice = jnp.concatenate([inner, inner], axis=0)
+            planes[row >> 3] += dot(twice, place_ref[row & 7], ((0,), (0,)))
         return carry
 
-    lax.fori_loop(0, PAIRS, step, 0)
+    lax.fori_loop(0, (pairs + 1) >> 1, step, 0)
     lane = lax.broadcasted_iota(jnp.int32, (ROWS, 128), 1)
     for q in range(SPACE):
         for m in range(3):
             even = acc[pl.ds(16 * m + q, ROWS, stride=48), :]
             odd = acc[pl.ds(16 * m + 8 + q, ROWS, stride=48), :]
-            joined = jnp.where(lane < 64, even, pltpu.roll(odd, 64, 1))
+            joined = jnp.where(lane < 64, even + pltpu.roll(even, 64, 1), odd + pltpu.roll(odd, 64, 1))
             cols_ref[q, :, 128 * m : 128 * m + 128] = joined.astype(BF16)
     x = shot[0] % 4
     for by, grad_ref in enumerate((near_ref, next_ref, far_ref, last_ref)):
@@ -552,7 +606,7 @@
 
 
 def output_body(
-    own, shot, m_ref, other_ref, back_ref, block_ref, local_ref, diag_rows_ref, off_rows_ref, diag_ref, off_ref,
+    own, m_ref, other_ref, back_ref, block_ref, local_ref, diag_rows_ref, off_rows_ref, diag_ref, off_ref,
     out_ref, misfit_ref, tmp,
 ):
     lane = lax.broadcasted_iota(jnp.int32, (KX, 128), 1)
@@ -583,7 +637,7 @@
     group = lax.broadcasted_iota(jnp.int32, (ROWS, 1024), 1) % 128 // 32
     rows = jnp.concatenate([jnp.where(group == a, rows, 0.0) for a in range(4)], axis=0)
     rh, rl = split(rows)
-    block = dot(rh, block_ref[0]) + dot(rl, block_ref[0])
+    block = dot(rh, block_ref[...]) + dot(rl, block_ref[...])
     for a in range(4):
         tmp[pl.ds(a, ROWS, stride=4), 0:64] = block[ROWS * a : ROWS * a + ROWS]
     out_ref[...] = (tmp[...].T[0:64] + local_ref[...]) * scale
@@ -614,11 +668,14 @@
     ]
 
 
-def gather_space(copies):
-    mine = lax.all_to_all(
+def gather_z(copies):
+    return lax.all_to_all(
         copies, "space", 0, 0, axis_index_groups=[[0, 2, 4, 6], [1, 3, 5, 7]], tiled=True
     )
-    return mine, lax.ppermute(mine, "space", [(n, n ^ 1) for n in range(SPACE)])
+
+
+def from_core(values):
+    return lax.ppermute(values, "space", [(n, n ^ 1) for n in range(SPACE)])
 
 
 def shards(
@@ -642,10 +699,6 @@
     operator_rows = KOWN * KX * 24
     encoder = encoder_weight.reshape(16, C)
     bias, amplitude = encoder_bias[None], source_amplitude[None]
-    rows = receiver_rows.reshape(PAIRS)
-    index = jnp.stack(
-        [rows, jnp.repeat(source_row, REC), jnp.repeat(source_column, REC)], axis=1
-    ).astype(F32)
     both_rows = jnp.asarray(BOTH_ROWS)
     table = jnp.asarray(WEIGHTED)
     record = observed.reshape(PAIRS, GW)
@@ -654,42 +707,44 @@
     partial = call(
         velocity_body, 1, shaped((SPACE, KX, 128)),
         [full_spec(fine), full_spec((4 * GW, 256)), own_spec((192, 256))],
-        full_spec((SPACE, KX, 128)), name="velocity_spectrum",
+        kept_spec((SPACE, KX, 128)), name="velocity_spectrum",
     )(own, velocity, jnp.asarray(COLUMNS), jnp.asarray(ROW_SUMS))
     spectra = lax.all_to_all(partial, "space", 0, 0, tiled=True)
 
-    index, _ = lax.optimization_barrier((index, partial))
+    bias, _ = lax.optimization_barrier((bias, partial))
     operator, sides, bumps = call(
-        operator_body, 1,
+        operator_body, 3,
         (shaped((operator_rows, 128)), shaped((KOWN, PAIRS, 256), BF16), shaped((PAIRS, GW))),
         [
             full_spec((16, C)), row_spec, row_spec, full_spec((KX, KOWN, C, 128)),
-            full_spec((PAIRS, 3)), full_spec((128, GH)), own_spec((8, GW)),
+            full_spec((4, REC)), full_spec((128, GH)), own_spec((8, GW)),
         ],
         (full_spec((operator_rows, 128)), full_spec((KOWN, PAIRS, 256)), full_spec((PAIRS, GW))),
         name="operator",
     )(
-        own, encoder, bias, amplitude, spectral_weight, index, jnp.asarray(PAIRED_ROWS),
+        own, source_row, source_column, encoder, bias, amplitude, spectral_weight, receiver_rows,
+        jnp.asarray(PAIRED_ROWS),
         jnp.asarray(OWN_COLUMNS),
     )
 
     sent = call(
         mix_body, 1, shaped((SPACE // 2, PAIRS, 384), BF16),
         [
-            full_spec((SPACE, KX, 128)), own_spec((KX, 128)),
+            kept_spec((SPACE, KX, 128)), own_spec((KX, 128)),
             full_spec((operator_rows, 128)), full_spec((KOWN, PAIRS, 256)),
         ],
-        full_spec((SPACE // 2, PAIRS, 384)), name="mix_modes",
+        kept_spec((SPACE // 2, PAIRS, 384)), name="mix_modes",
     )(own, spectra, jnp.asarray(ONES), operator, sides)
-    gathered, others = gather_space(sent)
-
+    gathered = gather_z(sent)
+
+    mine = lax.dynamic_index_in_dim(jnp.asarray(BLOCKS), i, 0, keepdims=False)
     late_bias, _ = lax.optimization_barrier((layer_bias[None], sent))
-    planes, wk, vectors, placed, spread_high, spread_low = call(
-        planes_body, 1,
+    planes, wk, vectors, placed, spread_high, spread_low, pairs = call(
+        planes_body, 2,
         (
             shaped((ROWS, 16, GW)), shaped((48, C), BF16), shaped((3, C, 128)),
             shaped((8, 128, 128), BF16), shaped((KOWN, 128, 128), BF16),
-            shaped((KOWN, 128, 128), BF16),
+            shaped((KOWN, 128, 128), BF16), shaped((144,), jnp.int32),
         ),
         [
             full_spec(fine), full_spec((512, 512)), full_spec((16, C)), row_spec, row_spec,
@@ -698,92 +753,103 @@
         (
             full_spec((ROWS, 16, GW)), full_spec((48, C)), full_spec((3, C, 128)),
             full_spec((8, 128, 128)), full_spec((KOWN, 128, 128)), full_spec((KOWN, 128, 128)),
+            pl.BlockSpec(memory_space=pltpu.SMEM),
         ),
         [pltpu.VMEM((128, 512), F32)], name="velocity_planes",
     )(
-        own, velocity, jnp.asarray(SELECT), encoder, bias, amplitude, point_weight, late_bias,
+        own, receiver_rows, velocity, jnp.asarray(SELECT), encoder, bias, amplitude, point_weight, late_bias,
         out_weight[None], jnp.asarray(LANES),
     )
 
+    gathered, planes, mine = lax.optimization_barrier((gathered, planes, mine))
+    others = from_core(gathered)
     predicted, slopes, stats = call(
         forward_body, 2,
         (shaped((PAIRS, GW)), shaped((PAIRS * C, GW), BF16), shaped((SPACE, 8, 128))),
         [
-            full_spec((SPACE // 2, PAIRS, 384)), full_spec((SPACE // 2, PAIRS, 384)),
+            kept_spec((SPACE // 2, PAIRS, 384)), kept_spec((SPACE // 2, PAIRS, 384)),
             full_spec((ROWS, 16, GW)), full_spec((48, GW)),
             full_spec((48, C)), full_spec((PAIRS, GW)), full_spec((3, C, 128)),
             full_spec((PAIRS, GW)),
         ],
-        (full_spec((PAIRS, GW)), full_spec((PAIRS * C, GW)), full_spec((SPACE, 8, 128))),
-        [pltpu.VMEM((3 * SPACE * PAIRS, 128), F32), pltpu.VMEM((8, GW), F32)], name="forward_rows",
-    )(own, rows, gathered, others, planes, table, wk, bumps, vectors, record)
+        (
+            full_spec((PAIRS, GW)), pl.BlockSpec(memory_space=pl.ANY),
+            kept_spec((SPACE, 8, 128)),
+        ),
+        [
+            pltpu.VMEM((3 * SPACE * PAIRS, 128), F32), pltpu.VMEM((8, GW), F32),
+            pltpu.VMEM((PAIRS * C, GW), BF16), pltpu.SemaphoreType.DMA((PAIRS // 2,)),
+        ], name="forward_rows",
+    )(own, pairs, gathered, others, planes, table, wk, bumps, vectors, record)
     stats = lax.all_to_all(stats, "space", 0, 0, tiled=True)
 
     columns, near, after, far, last, misfits = call(
         backward_body, 3,
         (shaped((SPACE, ROWS, 384), BF16),) + (shaped((GW, 128), BF16),) * 4 + (shaped((8, 128)),),
         [
-            full_spec((SPACE, 8, 128)), full_spec((PAIRS, GW)),
-            full_spec((PAIRS, GW)), full_spec((PAIRS * C, GW)), full_spec((48, GW)),
+            kept_spec((SPACE, 8, 128)), full_spec((PAIRS, GW)),
+            full_spec((PAIRS, GW)), pl.BlockSpec(memory_space=pl.ANY), full_spec((48, GW)),
             full_spec((8, 128, 128)),
         ],
-        (full_spec((SPACE, ROWS, 384)),) + (full_spec((GW, 128)),) * 4 + (full_spec((8, 128)),),
+        (kept_spec((SPACE, ROWS, 384)),) + (kept_spec((GW, 128)),) * 4 + (full_spec((8, 128)),),
         [
             pltpu.VMEM((16, GW), F32), pltpu.VMEM((ROWS * 48, 128), F32),
-            pltpu.VMEM((4, GW, 128), F32),
+            pltpu.VMEM((4, GW, 128), F32), pltpu.VMEM((PAIRS * C, GW), BF16),
+            pltpu.SemaphoreType.DMA((PAIRS // 2,)),
         ],
         name="backward_rows",
-    )(own, rows, shot, stats, record, predicted, slopes, table, placed)
+    )(own, pairs, shot, stats, record, predicted, slopes, table, placed)
 
     columns = lax.all_to_all(columns, "space", 0, 0, tiled=True)
     adjoint = call(
         adjoint_body, 0, shaped((KOWN * KX, 128)),
-        [full_spec((SPACE, ROWS, 384)), full_spec((96, GH))],
-        full_spec((KOWN * KX, 128)), name="adjoint_rows",
+        [kept_spec((SPACE, ROWS, 384)), full_spec((96, GH))],
+        kept_spec((KOWN * KX, 128)), name="adjoint_rows", limit=SMALL,
     )(columns, both_rows)
     arrived = from_x(after, far, last)
     blocks = call(
-        along_x_body, 1, (shaped((128, 128)),) * 4, [full_spec((GW, 128))] * 4,
-        (full_spec((128, 128)),) * 4, [pltpu.VMEM((GW, 128), F32)], name="along_x",
+        along_x_body, 1, (shaped((128, 128)),) * 4, [kept_spec((GW, 128))] * 4,
+        (kept_spec((128, 128)),) * 4, [pltpu.VMEM((GW, 128), F32)], name="along_x", limit=SMALL,
     )(shot, near, *arrived)
     sums = call(
         along_y_body, 0, shaped((MODES + 128, 128)),
-        [full_spec((128, 128))] * 4 + [full_spec((MODES, 128))],
-        full_spec((MODES + 128, 128)), name="along_y",
+        [kept_spec((128, 128))] * 4 + [kept_spec((MODES, 128))],
+        kept_spec((MODES + 128, 128)), name="along_y", limit=SMALL,
     )(blocks[0], *from_y(*blocks[1:]), adjoint)
     local, sums = call(
         along_z_body, 1, (shaped((64, 128)), shaped((MODES + 8, 128))),
-        [full_spec((MODES + 128, 128))] * 2,
-        (full_spec((64, 128)), full_spec((MODES + 8, 128))), [pltpu.VMEM((128, 128), F32)],
-        name="along_z",
+        [kept_spec((MODES + 128, 128))] * 2,
+        (kept_spec((64, 128)), kept_spec((MODES + 8, 128))), [pltpu.VMEM((128, 128), F32)],
+        name="along_z", limit=SMALL,
     )(shot, sums, lax.ppermute(sums, "shot", turn(2, 16, SHOT, 1)))
     parts = from_x(sums, sums, sums)
+    local = local.reshape(4, 16, 8, 4, 4).transpose(1, 4, 0, 2, 3).reshape(64, 128)
+    parts, local = lax.optimization_barrier((parts, local))
     sums = (sums + parts[0]) + (parts[1] + parts[2])
 
     modes = call(
         adjoint_mix_body, 0, shaped((SPACE // 2, KX + 8, 128)),
-        [full_spec((MODES + 8, 128))] * 4
+        [kept_spec((MODES + 8, 128))] * 4
         + [
             full_spec((operator_rows, 128)), full_spec((KOWN, 128, 128)),
             full_spec((KOWN, 128, 128)), full_spec((8, 128)),
         ],
-        full_spec((SPACE // 2, KX + 8, 128)), name="adjoint_mix",
+        kept_spec((SPACE // 2, KX + 8, 128)), name="adjoint_mix", limit=SMALL,
     )(sums, *from_y(sums, sums, sums), operator, spread_high, spread_low, misfits)
-    modes, other_modes = gather_space(modes)
-    local = local.reshape(4, 16, 8, 4, 4).transpose(1, 4, 0, 2, 3).reshape(64, 128)
-
+    modes = gather_z(modes)
+    other_modes = from_core(modes)
     block, misfit = call(
-        output_body, 2, (shaped((64, 128)), shaped((1, 4))),
+        output_body, 1, (shaped((64, 128)), shaped((1, 4))),
         [
-            full_spec((SPACE // 2, KX + 8, 128)), full_spec((SPACE // 2, KX + 8, 128)),
-            own_spec((ROWS, 96)), own_spec((1024, 64), 1),
+            kept_spec((SPACE // 2, KX + 8, 128)), kept_spec((SPACE // 2, KX + 8, 128)),
+            own_spec((ROWS, 96)), full_spec((1024, 64)),
             full_spec((64, 128)), full_spec((96, 128)), full_spec((96, 96)),
             full_spec((1, 1024)), full_spec((1024, 1024)),
         ],
         (full_spec((64, 128)), full_spec((1, 4))), [pltpu.VMEM((128, 128), F32)],
-        name="output_block",
+        name="output_block", limit=SMALL,
     )(
-        own, shot, modes, other_modes, jnp.asarray(ROWS_BACK), jnp.asarray(BLOCKS), local, jnp.asarray(DIAG_ROWS),
+        own, modes, other_modes, jnp.asarray(ROWS_BACK), mine, local, jnp.asarray(DIAG_ROWS),
         jnp.asarray(OFF_ROWS), jnp.asarray(DIAG_WIDE), jnp.asarray(OFF_WIDE),
     )
     return (misfit.reshape(4), block.T)

time: 151 us -> 128 us (0.85)
  Pallas kernels: 45.2 us -> 30.5 us
  starting transfers between devices: 48.7 us -> 45.8 us
  local copies, waits for them, and re-layouts: 9.76 us -> 6.91 us
    pallas_call x9, Pallas kernels: 26.1 us -> 16.8 us  [the longest x1 5.72 us: shards(): call(operator_body, 3, (shaped((operator_rows, 128)), shaped((KOWN, PAIRS...]
    all_to_all x1, waiting for transfers between devices: 4.77 us -> 0.01 us  [gather_z(): lax.all_to_all(copies, 'space', 0, 0, axis_index_groups=[[0, 2, 4, 6], [1...]
    ppermute x6, starting transfers between devices: 10.2 us -> 6.43 us  [from_y(): lax.ppermute(part, 'shot', turn(4, 4, SHOT, by + 1))]
    unnamed x44 -> x28, local copies, waits for them, and re-layouts: 6.08 us -> 2.32 us
    ppermute x6, waiting for transfers between devices: 4.57 us -> 7.82 us  [from_y(): lax.ppermute(part, 'shot', turn(4, 4, SHOT, by + 1))]
    pallas_call x1, Pallas kernels: 8.53 us -> 5.37 us  [shards(): call(forward_body, 2, (shaped((PAIRS, GW)), shaped((PAIRS * C, GW), BF16)...]
    ppermute x6, waiting for transfers between devices: 9.54 us -> 6.43 us  [from_x(): lax.ppermute(part, 'shot', turn(4, 1, SHOT, by + 1))]
    pallas_call x1, Pallas kernels: 7.28 us -> 5.19 us  [shards(): call(backward_body, 3, (shaped((SPACE, ROWS, 384), BF16),) + (shaped((GW,...]
  transfers between devices with their start and end apart: 18 -> 18, of which waited for: 11 -> 13; matrix products, arithmetic and copies ran while one was open for 3% -> 4% of each run, Pallas kernels for 8% -> 8%
where the time goes in v2:
time: 128 us; the launch traced here: 127 us
  starting transfers between devices  45.8 us (36%)
  Pallas kernels  30.5 us (24%)
  blocking collectives  21.9 us (17%)
  waiting for transfers between devices  20.4 us (16%)
  local copies, waits for them, and re-layouts  6.91 us (5%)
    all_to_all x1, blocking collectives, gather_z(): lax.all_to_all(copies, 'space', 0, 0, axis_index_groups=[[0, 2, 4, 6], [1...  11.5 us
    all_to_all x1, blocking collectives, shards(): stats = lax.all_to_all(stats, 'space', 0, 0, tiled=True)  10.4 us
    ppermute x2, starting transfers between devices, from_core(): return lax.ppermute(values, 'space', [(n, n ^ 1) for n in range(SPACE)])  10 us
    ppermute x6, starting transfers between devices, from_x(): lax.ppermute(part, 'shot', turn(4, 1, SHOT, by + 1))  9.34 us
    ppermute x6, waiting for transfers between devices, from_y(): lax.ppermute(part, 'shot', turn(4, 4, SHOT, by + 1))  7.82 us
    all_to_all x1, starting transfers between devices, shards(): spectra = lax.all_to_all(partial, 'space', 0, 0, tiled=True)  7.4 us
    ppermute x6, waiting for transfers between devices, from_x(): lax.ppermute(part, 'shot', turn(4, 1, SHOT, by + 1))  6.43 us
    ppermute x6, starting transfers between devices, from_y(): lax.ppermute(part, 'shot', turn(4, 4, SHOT, by + 1))  6.43 us
  transfers between devices with their start and end apart: 18, of which 13 were waited for; matrix products, arithmetic and copies ran while one was open for 4% of the time, Pallas kernels for 8%

profile of v2, /device:TPU:1, one launch (start us, length us, event | category | flops | bytes accessed | tf_op | source)
XLA Modules:
  0.0 127.5 jit_solution(16312200899320598901)
XLA Ops:
  0.6 3.2 %velocity_spectrum.1 = f32[8,48,128]{2,1,0:T(8,128)} custom-call(s32[1]{0:T(128)} %bitcast.own, f32[128,2048]{1,0:T(8,128)} %v_ref.3, bf16[2048,256]{1,0:T(8,128)(2,1)} %constant.47.clone.cols_ref, bf16[8,192,256]{2,1,0:T(8,128)(2,1)} %constant.48.clone.rows_ref), custom_call_target="tpu_custom_call" | custom-call | tf_op jit(solution)/shard_map/velocity_spectrum/pallas_call | solution.py:707
  3.9 7.4 %all-to-all-start = ((f32[8,48,128]{2,1,0:T(8,128)}), f32[8,48,128]{2,1,0:T(8,128)S(1)}, u32[]{:S(2)}, u32[]{:S(2)}) async-start(f32[8,48,128]{2,1,0:T(8,128)} %velocity_spectrum.1), calls=%async_computation | async-start | bytes 393216 | tf_op jit(solution)/shard_map/all_to_all | solution.py:712
  11.3 5.7 %operator.1 = (f32[3456,128]{1,0:T(8,128)}, bf16[3,64,256]{2,1,0:T(8,128)(2,1)}, f32[64,512]{1,0:T(8,128)}) custom-call(s32[1]{0:T(128)} %bitcast.own, s32[4]{0:T(128)} %source_row.1, s32[4]{0:T(128)} %source_column.1, f32[16,64]{1,0:T(8,128)} %bitcast.20, f32[1,64]{1,0:T(1,128)} %bitcast.22, f32[1,64]{1,0:T(1,128)} %bitcast.24, ...), custom_call_target="tpu_custom_call" | custom-call | tf_op jit(solution)/shard_map/operator/pallas_call | solution.py:715
  18.4 3.7 %mix_modes.1 = bf16[4,64,384]{2,1,0:T(8,128)(2,1)} custom-call(s32[1]{0:T(128)} %bitcast.own, f32[8,48,128]{2,1,0:T(8,128)} %copy-done.12, f32[8,48,128]{2,1,0:T(8,128)} %constant.51.clone.ones_ref, f32[3456,128]{1,0:T(8,128)} %get-tuple-element.39.t_ref, bf16[3,64,256]{2,1,0:T(8,128)(2,1)} %get-tuple-element.40.l_ref), custom_call_target="tpu_custom_call" | custom-call | tf_op jit(solution)/shard_map/mix_modes/pallas_call | solution.py:730
  22.1 3.7 %all-to-all-start.1 = ((bf16[4,64,384]{2,1,0:T(8,128)(2,1)}), bf16[4,64,384]{2,1,0:T(8,128)(2,1)S(1)}, u32[]{:S(2)}, u32[]{:S(2)}) async-start(bf16[4,64,384]{2,1,0:T(8,128)(2,1)} %mix_modes.1), calls=%async_computation.1 | async-start | bytes 393216 | tf_op jit(solution)/shard_map/all_to_all | solution.py:672
  26.8 4.3 %velocity_planes.1 = (f32[32,16,512]{2,1,0:T(8,128)}, bf16[48,64]{1,0:T(8,128)(2,1)}, f32[3,64,128]{2,1,0:T(8,128)}, bf16[8,128,128]{2,1,0:T(8,128)(2,1)}, bf16[...) custom-call(s32[1]{0:T(128)} %bitcast.own, s32[4,16]{1,0:T(4,128)} %rows_ref.4, ...), custom_call_target="tpu_custom_call" | custom-call | tf_op jit(solution)/shard_map/velocity_planes/pallas_call | solution.py:742
  31.2 3.5 %collective-permute-start = (bf16[4,64,384]{2,1,0:T(8,128)(2,1)S(1)}, bf16[4,64,384]{2,1,0:T(8,128)(2,1)S(1)}, u32[]{:S(2)}, u32[]{:S(2)}) collective-permute-start(bf16[4,64,384]{2,1,0:T(8,128)(2,1)S(1)} %all-to-all-done.1.d_ref), channel_id=1, source_target_pairs={{0,1},{1,0},{2,3},{3,2},{4,5},{5,4},{6,7},{7,6},{8,9},{9,8},{10,11... | collective-permute-start | bytes 589832 | tf_op jit(solution)/shard_map/ppermute | solution.py:678
  36.4 5.4 %forward_rows.1 = (f32[64,512]{1,0:T(8,128)}, bf16[4096,512]{1,0:T(8,128)(2,1)}, f32[8,8,128]{2,1,0:T(8,128)}) custom-call(s32[1]{0:T(128)} %bitcast.own, s32[144]{0:T(256)} %get-tuple-element.42.list_ref, bf16[4,64,384]{2,1,0:T(8,128)(2,1)} %copy-done.11, bf16[4,64,384]{2,1,0:T(8,128)(2,1)} %copy-done.13, f32[32,16,512]{2,1,0:T(8,128)} %get-tuple-element.45.planes_ref, ...), custom_call_target="tpu_custom_call" | custom-call | tf_op jit(solution)/shard_map/forward_rows/pallas_call | solution.py:766
  41.8 10.4 %all_to_all.25.stats_ref = f32[8,8,128]{2,1,0:T(8,128)} all-to-all(f32[8,8,128]{2,1,0:T(8,128)} %get-tuple-element.49), channel_id=1, replica_groups=mesh['shot'=32,'space'=8] {'space'}, dimensions={0} | all-to-all | bytes 65536 | tf_op jit(solution)/shard_map/all_to_all | solution.py:784
  52.2 5.2 %backward_rows.1 = (bf16[8,32,384]{2,1,0:T(8,128)(2,1)}, bf16[512,128]{1,0:T(8,128)(2,1)}, bf16[512,128]{1,0:T(8,128)(2,1)}, bf16[512,128]{1,0:T(8,128)(2,1)}, b...) custom-call(s32[1]{0:T(128)} %bitcast.own, s32[144]{0:T(256)} %get-tuple-element.42.list_ref, s32[1]{0:T(128)} %bitcast.1.shot, ...), custom_call_target="tpu_custom_call" | custom-call | tf_op jit(solution)/shard_map/backward_rows/pallas_call | solution.py:786
  57.4 4.2 %all-to-all-start.3 = ((bf16[8,32,384]{2,1,0:T(8,128)(2,1)}), bf16[8,32,384]{2,1,0:T(8,128)(2,1)S(1)}, u32[]{:S(2)}, u32[]{:S(2)}) async-start(bf16[8,32,384]{2,1,0:T(8,128)(2,1)} %get-tuple-element.61), calls=%async_computation.3 | async-start | bytes 393216 | tf_op jit(solution)/shard_map/all_to_all | solution.py:803
  62.6 4.0 %collective-permute-start.2 = (bf16[512,128]{1,0:T(8,128)(2,1)}, bf16[512,128]{1,0:T(8,128)(2,1)S(1)}, u32[]{:S(2)}, u32[]{:S(2)}) collective-permute-start(bf16[512,128]{1,0:T(8,128)(2,1)} %get-tuple-element.55), channel_id=1, source_target_pairs={{0,16},{8,24},{16,0},{24,8},{32,48},{40,56},{48,32},{56,40},{64,80... | collective-permute-start | bytes 393224 | tf_op jit(solution)/shard_map/ppermute | solution.py:661
  67.0 2.4 %collective-permute-done.1.b_ref = bf16[512,128]{1,0:T(8,128)(2,1)S(1)} collective-permute-done((bf16[512,128]{1,0:T(8,128)(2,1)}, bf16[512,128]{1,0:T(8,128)(2,1)S(1)}, u32[]{:S(2)}, u32[]{:S(2)}) %collective-permute-start.1) | collective-permute-done | bytes 131104 | tf_op jit(solution)/shard_map/ppermute | solution.py:661
  69.4 3.7 %collective-permute-done.2.c_ref = bf16[512,128]{1,0:T(8,128)(2,1)S(1)} collective-permute-done((bf16[512,128]{1,0:T(8,128)(2,1)}, bf16[512,128]{1,0:T(8,128)(2,1)S(1)}, u32[]{:S(2)}, u32[]{:S(2)}) %collective-permute-start.2) | collective-permute-done | bytes 131104 | tf_op jit(solution)/shard_map/ppermute | solution.py:661
  74.2 4.1 %collective-permute-start.5 = (f32[128,128]{1,0:T(8,128)S(1)}, f32[128,128]{1,0:T(8,128)S(1)}, u32[]{:S(2)}, u32[]{:S(2)}) collective-permute-start(f32[128,128]{1,0:T(8,128)S(1)} %get-tuple-element.59), channel_id=1, source_target_pairs={{0,64},{8,72},{16,80},{24,88},{32,96},{40,104},{48,112},{56,120},{... | collective-permute-start | bytes 196616 | tf_op jit(solution)/shard_map/ppermute | solution.py:667
  78.8 2.1 %collective-permute-done.5.c_ref = f32[128,128]{1,0:T(8,128)S(1)} collective-permute-done((f32[128,128]{1,0:T(8,128)S(1)}, f32[128,128]{1,0:T(8,128)S(1)}, u32[]{:S(2)}, u32[]{:S(2)}) %collective-permute-start.5) | collective-permute-done | bytes 65568 | tf_op jit(solution)/shard_map/ppermute | solution.py:667
  81.8 4.7 %collective-permute-start.7 = (f32[272,128]{1,0:T(8,128)S(1)}, f32[272,128]{1,0:T(8,128)S(1)}, u32[]{:S(2)}, u32[]{:S(2)}) collective-permute-start(f32[272,128]{1,0:T(8,128)S(1)} %along_y.1.a_ref), channel_id=1, source_target_pairs={{0,128},{8,136},{16,144},{24,152},{32,160},{40,168},{48,176},{56,1... | collective-permute-start | bytes 417800 | tf_op jit(solution)/shard_map/ppermute | solution.py:824
  86.5 3.3 %collective-permute-done.7.b_ref = f32[272,128]{1,0:T(8,128)S(1)} collective-permute-done((f32[272,128]{1,0:T(8,128)S(1)}, f32[272,128]{1,0:T(8,128)S(1)}, u32[]{:S(2)}, u32[]{:S(2)}) %collective-permute-start.7) | collective-permute-done | bytes 139296 | tf_op jit(solution)/shard_map/ppermute | solution.py:824
  89.9 2.1 %collective-permute-start.10 = (f32[152,128]{1,0:T(8,128)S(1)}, f32[152,128]{1,0:T(8,128)}, u32[]{:S(2)}, u32[]{:S(2)}) collective-permute-start(f32[152,128]{1,0:T(8,128)S(1)} %get-tuple-element.62), channel_id=1, source_target_pairs={{0,24},{8,0},{16,8},{24,16},{32,56},{40,32},{48,40},{56,48},{64,88... | collective-permute-start | bytes 233480 | tf_op jit(solution)/shard_map/ppermute | solution.py:661
  94.8 2.0 %copy.31 = f32[16,4,4,8,4]{4,3,2,1,0:T(8,128)S(1)} copy(f32[16,4,4,8,4]{0,2,1,4,3:T(4,128)} %bitcast.17) | data formatting | bytes 65536 | tf_op jit(solution)/shard_map/transpose | solution.py:826
  102.3 3.0 %collective-permute-done.12.far_ref = f32[152,128]{1,0:T(8,128)S(1)} collective-permute-done((f32[152,128]{1,0:T(8,128)S(1)}, f32[152,128]{1,0:T(8,128)S(1)}, u32[]{:S(2)}, u32[]{:S(2)}) %collective-permute-start.12) | collective-permute-done | bytes 77856 | tf_op jit(solution)/shard_map/ppermute | solution.py:667
  106.7 11.5 %all_to_all.26.m_ref = f32[4,56,128]{2,1,0:T(8,128)S(1)} all-to-all(f32[4,56,128]{2,1,0:T(8,128)S(1)} %adjoint_mix.1), channel_id=1, replica_groups={{0,2,4,6},{1,3,5,7},{8,10,12,14},{9,11,13,15},{16,18,20,22},{17,19,21,2..., dimensions={0} | all-to-all | bytes 229376 | tf_op jit(solution)/shard_map/all_to_all | solution.py:672
  118.2 6.5 %collective-permute-start.14 = (f32[4,56,128]{2,1,0:T(8,128)S(1)}, f32[4,56,128]{2,1,0:T(8,128)S(1)}, u32[]{:S(2)}, u32[]{:S(2)}) collective-permute-start(f32[4,56,128]{2,1,0:T(8,128)S(1)} %all_to_all.26.m_ref), channel_id=1, source_target_pairs={{0,1},{1,0},{2,3},{3,2},{4,5},{5,4},{6,7},{7,6},{8,9},{9,8},{10,11... | collective-permute-start | bytes 344072 | tf_op jit(solution)/shard_map/ppermute | solution.py:678
  125.8 1.7 %output_block.1 = (f32[64,128]{1,0:T(8,128)}, f32[1,4]{1,0:T(1,128)}) custom-call(s32[1]{0:T(128)} %bitcast.own, f32[4,56,128]{2,1,0:T(8,128)S(1)} %all_to_all.26.m_ref, f32[4,56,128]{2,1,0:T(8,128)S(1)} %collective-permute-done.14.other_ref, bf16[8,32,96]{2,1,0:T(8,128)(2,1)S(1)} %copy-done.5, bf16[1024,64]{1,0:T(8,128)(2,1)S(1)} %dynamic-slice_bitcast_fusion.block_ref, ...), custom_call_target="tpu_custom_call" | custom-call | tf_op jit(solution)/shard_map/output_block/pallas_call | solution.py:841
  (60 shorter events, 18.7 us)
Async XLA Ops:
  3.9 13.9 %all-to-all-start = ((f32[8,48,128]{2,1,0:T(8,128)}), f32[8,48,128]{2,1,0:T(8,128)S(1)}, u32[]{:S(2)}, u32[]{:S(2)}) async-start(f32[8,48,128]{2,1,0:T(8,128)} %velocity_spectrum.1), calls=%async_computation | async-start | bytes 393216 | tf_op jit(solution)/shard_map/all_to_all | solution.py:712
  22.1 9.0 %all-to-all-start.1 = ((bf16[4,64,384]{2,1,0:T(8,128)(2,1)}), bf16[4,64,384]{2,1,0:T(8,128)(2,1)S(1)}, u32[]{:S(2)}, u32[]{:S(2)}) async-start(bf16[4,64,384]{2,1,0:T(8,128)(2,1)} %mix_modes.1), calls=%async_computation.1 | async-start | bytes 393216 | tf_op jit(solution)/shard_map/all_to_all | solution.py:672
  31.2 4.5 %collective-permute-start = (bf16[4,64,384]{2,1,0:T(8,128)(2,1)S(1)}, bf16[4,64,384]{2,1,0:T(8,128)(2,1)S(1)}, u32[]{:S(2)}, u32[]{:S(2)}) collective-permute-start(bf16[4,64,384]{2,1,0:T(8,128)(2,1)S(1)} %all-to-all-done.1.d_ref), channel_id=1, source_target_pairs={{0,1},{1,0},{2,3},{3,2},{4,5},{5,4},{6,7},{7,6},{8,9},{9,8},{10,11... | collective-permute-start | bytes 589832 | tf_op jit(solution)/shard_map/ppermute | solution.py:678
  52.2 53.7 %copy-start.3 = (bf16[3,128,128]{2,1,0:T(8,128)(2,1)S(1)}, bf16[3,128,128]{2,1,0:T(8,128)(2,1)}, u32[]{:S(2)}) copy-start(bf16[3,128,128]{2,1,0:T(8,128)(2,1)} %get-tuple-element.67.high_ref) | copy-start | bytes 294916
  52.2 53.7 %copy-start.4 = (bf16[3,128,128]{2,1,0:T(8,128)(2,1)S(1)}, bf16[3,128,128]{2,1,0:T(8,128)(2,1)}, u32[]{:S(2)}) copy-start(bf16[3,128,128]{2,1,0:T(8,128)(2,1)} %get-tuple-element.68.low_ref) | copy-start | bytes 294916
  57.4 68.4 %copy-start.5 = (bf16[8,32,96]{2,1,0:T(8,128)(2,1)S(1)}, bf16[8,32,96]{2,1,0:T(8,128)(2,1)}, u32[]{:S(2)}) copy-start(bf16[8,32,96]{2,1,0:T(8,128)(2,1)} %constant.55.clone.back_ref) | copy-start | bytes 147460
  57.4 68.4 %copy-start.7 = (f32[96,128]{1,0:T(8,128)S(1)}, f32[96,128]{1,0:T(8,128)}, u32[]{:S(2)}) copy-start(f32[96,128]{1,0:T(8,128)} %constant.56.clone.diag_rows_ref) | copy-start | bytes 147460
  57.4 68.4 %copy-start.8 = (bf16[96,96]{1,0:T(8,128)(2,1)S(1)}, bf16[96,96]{1,0:T(8,128)(2,1)}, u32[]{:S(2)}) copy-start(bf16[96,96]{1,0:T(8,128)(2,1)} %constant.57.clone.off_rows_ref) | copy-start | bytes 55300
  57.4 68.3 %copy-start.9 = (f32[1,1024]{1,0:T(1,128)S(1)}, f32[1,1024]{1,0:T(1,128)}, u32[]{:S(2)}) copy-start(f32[1,1024]{1,0:T(1,128)} %constant.58.clone.diag_ref) | copy-start | bytes 12292
  57.4 20.9 %all-to-all-start.3 = ((bf16[8,32,384]{2,1,0:T(8,128)(2,1)}), bf16[8,32,384]{2,1,0:T(8,128)(2,1)S(1)}, u32[]{:S(2)}, u32[]{:S(2)}) async-start(bf16[8,32,384]{2,1,0:T(8,128)(2,1)} %get-tuple-element.61), calls=%async_computation.3 | async-start | bytes 393216 | tf_op jit(solution)/shard_map/all_to_all | solution.py:803
  61.6 7.8 %collective-permute-start.1 = (bf16[512,128]{1,0:T(8,128)(2,1)}, bf16[512,128]{1,0:T(8,128)(2,1)S(1)}, u32[]{:S(2)}, u32[]{:S(2)}) collective-permute-start(bf16[512,128]{1,0:T(8,128)(2,1)} %get-tuple-element.54), channel_id=1, source_target_pairs={{0,8},{8,16},{16,24},{24,0},{32,40},{40,48},{48,56},{56,32},{64,72... | collective-permute-start | bytes 393224 | tf_op jit(solution)/shard_map/ppermute | solution.py:661
  62.6 10.4 %collective-permute-start.2 = (bf16[512,128]{1,0:T(8,128)(2,1)}, bf16[512,128]{1,0:T(8,128)(2,1)S(1)}, u32[]{:S(2)}, u32[]{:S(2)}) collective-permute-start(bf16[512,128]{1,0:T(8,128)(2,1)} %get-tuple-element.55), channel_id=1, source_target_pairs={{0,16},{8,24},{16,0},{24,8},{32,48},{40,56},{48,32},{56,40},{64,80... | collective-permute-start | bytes 393224 | tf_op jit(solution)/shard_map/ppermute | solution.py:661
  66.6 6.5 %collective-permute-start.3 = (bf16[512,128]{1,0:T(8,128)(2,1)}, bf16[512,128]{1,0:T(8,128)(2,1)S(1)}, u32[]{:S(2)}, u32[]{:S(2)}) collective-permute-start(bf16[512,128]{1,0:T(8,128)(2,1)} %get-tuple-element.56), channel_id=1, source_target_pairs={{0,24},{8,0},{16,8},{24,16},{32,56},{40,32},{48,40},{56,48},{64,88... | collective-permute-start | bytes 393224 | tf_op jit(solution)/shard_map/ppermute | solution.py:661
  74.1 4.7 %collective-permute-start.4 = (f32[128,128]{1,0:T(8,128)S(1)}, f32[128,128]{1,0:T(8,128)S(1)}, u32[]{:S(2)}, u32[]{:S(2)}) collective-permute-start(f32[128,128]{1,0:T(8,128)S(1)} %get-tuple-element.58), channel_id=1, source_target_pairs={{0,32},{8,40},{16,48},{24,56},{32,64},{40,72},{48,80},{56,88},{64,... | collective-permute-start | bytes 196616 | tf_op jit(solution)/shard_map/ppermute | solution.py:667
  74.2 6.7 %collective-permute-start.5 = (f32[128,128]{1,0:T(8,128)S(1)}, f32[128,128]{1,0:T(8,128)S(1)}, u32[]{:S(2)}, u32[]{:S(2)}) collective-permute-start(f32[128,128]{1,0:T(8,128)S(1)} %get-tuple-element.59), channel_id=1, source_target_pairs={{0,64},{8,72},{16,80},{24,88},{32,96},{40,104},{48,112},{56,120},{... | collective-permute-start | bytes 196616 | tf_op jit(solution)/shard_map/ppermute | solution.py:667
  78.3 3.5 %collective-permute-start.6 = (f32[128,128]{1,0:T(8,128)S(1)}, f32[128,128]{1,0:T(8,128)S(1)}, u32[]{:S(2)}, u32[]{:S(2)}) collective-permute-start(f32[128,128]{1,0:T(8,128)S(1)} %get-tuple-element.60), channel_id=1, source_target_pairs={{0,96},{8,104},{16,112},{24,120},{32,0},{40,8},{48,16},{56,24},{64... | collective-permute-start | bytes 196616 | tf_op jit(solution)/shard_map/ppermute | solution.py:667
  81.8 8.0 %collective-permute-start.7 = (f32[272,128]{1,0:T(8,128)S(1)}, f32[272,128]{1,0:T(8,128)S(1)}, u32[]{:S(2)}, u32[]{:S(2)}) collective-permute-start(f32[272,128]{1,0:T(8,128)S(1)} %along_y.1.a_ref), channel_id=1, source_target_pairs={{0,128},{8,136},{16,144},{24,152},{32,160},{40,168},{48,176},{56,1... | collective-permute-start | bytes 417800 | tf_op jit(solution)/shard_map/ppermute | solution.py:824
  89.9 7.7 %collective-permute-start.10 = (f32[152,128]{1,0:T(8,128)S(1)}, f32[152,128]{1,0:T(8,128)}, u32[]{:S(2)}, u32[]{:S(2)}) collective-permute-start(f32[152,128]{1,0:T(8,128)S(1)} %get-tuple-element.62), channel_id=1, source_target_pairs={{0,24},{8,0},{16,8},{24,16},{32,56},{40,32},{48,40},{56,48},{64,88... | collective-permute-start | bytes 233480 | tf_op jit(solution)/shard_map/ppermute | solution.py:661
  92.0 5.5 %collective-permute-start.9 = (f32[152,128]{1,0:T(8,128)S(1)}, f32[152,128]{1,0:T(8,128)}, u32[]{:S(2)}, u32[]{:S(2)}) collective-permute-start(f32[152,128]{1,0:T(8,128)S(1)} %get-tuple-element.62), channel_id=1, source_target_pairs={{0,16},{8,24},{16,0},{24,8},{32,48},{40,56},{48,32},{56,40},{64,80... | collective-permute-start | bytes 233480 | tf_op jit(solution)/shard_map/ppermute | solution.py:661
  93.3 4.6 %collective-permute-start.8 = (f32[152,128]{1,0:T(8,128)S(1)}, f32[152,128]{1,0:T(8,128)}, u32[]{:S(2)}, u32[]{:S(2)}) collective-permute-start(f32[152,128]{1,0:T(8,128)S(1)} %get-tuple-element.62), channel_id=1, source_target_pairs={{0,8},{8,16},{16,24},{24,0},{32,40},{40,48},{48,56},{56,32},{64,72... | collective-permute-start | bytes 233480 | tf_op jit(solution)/shard_map/ppermute | solution.py:661
  99.0 3.3 %collective-permute-start.13 = (f32[152,128]{1,0:T(8,128)S(1)}, f32[152,128]{1,0:T(8,128)S(1)}, u32[]{:S(2)}, u32[]{:S(2)}) collective-permute-start(f32[152,128]{1,0:T(8,128)S(1)} %add_add_fusion.near_ref), channel_id=1, source_target_pairs={{0,96},{8,104},{16,112},{24,120},{32,0},{40,8},{48,16},{56,24},{64... | collective-permute-start | bytes 233480 | tf_op jit(solution)/shard_map/ppermute | solution.py:667
  100.5 4.9 %collective-permute-start.12 = (f32[152,128]{1,0:T(8,128)S(1)}, f32[152,128]{1,0:T(8,128)S(1)}, u32[]{:S(2)}, u32[]{:S(2)}) collective-permute-start(f32[152,128]{1,0:T(8,128)S(1)} %add_add_fusion.near_ref), channel_id=1, source_target_pairs={{0,64},{8,72},{16,80},{24,88},{32,96},{40,104},{48,112},{56,120},{... | collective-permute-start | bytes 233480 | tf_op jit(solution)/shard_map/ppermute | solution.py:667
  100.5 5.3 %collective-permute-start.11 = (f32[152,128]{1,0:T(8,128)S(1)}, f32[152,128]{1,0:T(8,128)S(1)}, u32[]{:S(2)}, u32[]{:S(2)}) collective-permute-start(f32[152,128]{1,0:T(8,128)S(1)} %add_add_fusion.near_ref), channel_id=1, source_target_pairs={{0,32},{8,40},{16,48},{24,56},{32,64},{40,72},{48,80},{56,88},{64,... | collective-permute-start | bytes 233480 | tf_op jit(solution)/shard_map/ppermute | solution.py:667
  118.2 7.5 %collective-permute-start.14 = (f32[4,56,128]{2,1,0:T(8,128)S(1)}, f32[4,56,128]{2,1,0:T(8,128)S(1)}, u32[]{:S(2)}, u32[]{:S(2)}) collective-permute-start(f32[4,56,128]{2,1,0:T(8,128)S(1)} %all_to_all.26.m_ref), channel_id=1, source_target_pairs={{0,1},{1,0},{2,3},{3,2},{4,5},{5,4},{6,7},{7,6},{8,9},{9,8},{10,11... | collective-permute-start | bytes 344072 | tf_op jit(solution)/shard_map/ppermute | solution.py:678
  (8 other events, 184.4 us)

commit v3 on v2

--- a/solution.py
+++ b/solution.py
@@ -151,6 +151,13 @@
     return bf(table.reshape(SHOT, 1024, 64))
 
 
+REPEAT = np.zeros((64, 16), np.float32)
+REPEAT[np.arange(64), np.arange(64) // 4] = 1.0
+REPEAT = bf(REPEAT)
+PICK = np.zeros((4, 128, 128), np.float32)
+for g in range(4):
+    PICK[g, np.arange(128), 32 * g + np.arange(128) // 4] = 1.0
+PICK = bf(PICK)
 LANES = lanes_table()
 BLOCKS = block_table()
 BOTH_ROWS = bf(np.concatenate([COS_ROWS.astype(np.float32), SIN_ROWS.astype(np.float32)], 0))
@@ -556,33 +563,80 @@
     for by, out_ref in enumerate((near_ref, next_ref, far_ref, last_ref)):
         for z in range(2):
             start = pl.multiple_of(64 * (4 * z + (y + by) % 4), 64)
-            out_ref[64 * z : 64 * z + 64, :] = tmp[pl.ds(start, 64), :]
-
-
-def along_y_body(a_ref, b_ref, c_ref, d_ref, modes_ref, out_ref):
-    out_ref[0:MODES, :] = modes_ref[...]
-    out_ref[MODES:, :] = (a_ref[...] + b_ref[...]) + (c_ref[...] + d_ref[...])
-
-
-def along_z_body(shot, a_ref, b_ref, local_ref, out_ref, tmp):
-    out_ref[0:MODES, :] = a_ref[0:MODES, :] + b_ref[0:MODES, :]
-    total = a_ref[MODES:, :] + b_ref[MODES:, :]
-    tmp[...] = total
+            out_ref[64 * z : 64 * z + 64, :] = tmp[pl.ds(start, 64), :].astype(out_ref.dtype)
+
+
+def along_y_body(a_ref, b_ref, c_ref, d_ref, modes_ref, out_ref, send_ref):
+    modes = modes_ref[...]
+    total = (a_ref[...] + b_ref[...].astype(F32)) + (
+        c_ref[...].astype(F32) + d_ref[...].astype(F32)
+    )
+    out_ref[0:MODES, :] = modes
+    out_ref[MODES:, :] = total
+    send_ref[0:MODES, :] = modes.astype(BF16)
+    send_ref[MODES:, :] = total.astype(BF16)
+
+
+def keep_and_send(modes, squares, out_ref, send_ref):
+    out_ref[0:MODES, :] = modes
+    out_ref[MODES : MODES + 16, :] = jnp.broadcast_to(squares, (16, 128))
+    send_ref[0:MODES, :] = modes.astype(BF16)
+    high = squares.astype(BF16).astype(F32)
+    rest = squares - high
+    middle = rest.astype(BF16).astype(F32)
+    row = lax.broadcasted_iota(jnp.int32, (16, 128), 0)
+    terms = jnp.where(row == 0, high, jnp.where(row == 1, middle, rest - middle))
+    send_ref[MODES : MODES + 16, :] = jnp.where(row < 3, terms, 0.0).astype(BF16)
+
+
+def sum_of(own_ref, parts):
+    modes = own_ref[0:MODES, :]
+    squares = own_ref[MODES : MODES + 1, :]
+    for part in parts:
+        modes = modes + part[0:MODES, :].astype(F32)
+        terms = part[MODES : MODES + 16, :].astype(F32)
+        squares = squares + jnp.sum(terms, axis=0, keepdims=True)
+    return modes, squares
+
+
+def along_z_body(shot, a_ref, b_ref, local_ref, out_ref, send_ref, tmp):
+    total = a_ref[...] + b_ref[...].astype(F32)
+    planes = total[MODES:]
+    tmp[...] = planes
     local_ref[...] = tmp[pl.ds(pl.multiple_of(64 * (shot[0] // 16), 64), 64), :]
-    out_ref[MODES : MODES + 8, :] = jnp.broadcast_to(
-        jnp.sum(total * total, axis=0, keepdims=True), (8, 128)
-    )
+    squares = jnp.sum(planes * planes, axis=0, keepdims=True)
+    keep_and_send(total[0:MODES], squares, out_ref, send_ref)
+
+
+def join_body(a_ref, b_ref, c_ref, d_ref, out_ref, send_ref):
+    modes, squares = sum_of(a_ref, (b_ref, c_ref, d_ref))
+    keep_and_send(modes, squares, out_ref, send_ref)
+
+
+def arrange_body(in_ref, repeat_ref, pick_ref, out_ref):
+    row = lax.broadcasted_iota(jnp.int32, (64, 128), 0)
+    lane = lax.broadcasted_iota(jnp.int32, (64, 128), 1)
+    same = row % 4 == lane % 4
+    total = jnp.zeros((64, 128), F32)
+    for g in range(4):
+        rest = in_ref[16 * g : 16 * g + 16, :]
+        for _ in range(3):
+            part = rest.astype(BF16)
+            rest = rest - part.astype(F32)
+            wide = jnp.where(same, dot(repeat_ref[...], part), 0.0).astype(BF16)
+            total = total + dot(wide, pick_ref[g])
+    out_ref[...] = total
 
 
 def adjoint_mix_body(
     near_ref, next_ref, far_ref, last_ref, t_ref, high_ref, low_ref, extra_ref, out_ref
 ):
     lane = lax.broadcasted_iota(jnp.int32, (KX, 128), 1)
+    spectra, squares = sum_of(near_ref, (next_ref, far_ref, last_ref))
     total = jnp.zeros((KX, 128), F32)
     cross = jnp.zeros((KX, 128), F32)
     for k in range(KOWN):
-        own = slice(KX * k, KX * k + KX)
-        spectrum = (near_ref[own, :] + next_ref[own, :]) + (far_ref[own, :] + last_ref[own, :])
+        spectrum = spectra[KX * k : KX * k + KX]
         turned = minus_i(spectrum)
         for ab in range(16):
             base = (ab // 4) * 32 + (ab % 4) * 6 + 2 * k
@@ -595,8 +649,6 @@
         cross = cross + dot(sh, high_ref[k]) + dot(sl, high_ref[k]) + dot(sh, low_ref[k])
     total = total * (1.0 / VELOCITY_SCALE)
     product = jnp.sum(total * cross, axis=0, keepdims=True)
-    own = slice(MODES, MODES + 1)
-    squares = (near_ref[own, :] + next_ref[own, :]) + (far_ref[own, :] + last_ref[own, :])
     for z in range(SPACE // 2):
         out_ref[z, :KX, :] = total
         out_ref[z, KX : KX + 1, :] = product
@@ -737,7 +789,6 @@
     )(own, spectra, jnp.asarray(ONES), operator, sides)
     gathered = gather_z(sent)
 
-    mine = lax.dynamic_index_in_dim(jnp.asarray(BLOCKS), i, 0, keepdims=False)
     late_bias, _ = lax.optimization_barrier((layer_bias[None], sent))
     planes, wk, vectors, placed, spread_high, spread_low, pairs = call(
         planes_body, 2,
@@ -761,7 +812,7 @@
         out_weight[None], jnp.asarray(LANES),
     )
 
-    gathered, planes, mine = lax.optimization_barrier((gathered, planes, mine))
+    gathered, planes = lax.optimization_barrier((gathered, planes))
     others = from_core(gathered)
     predicted, slopes, stats = call(
         forward_body, 2,
@@ -807,35 +858,45 @@
         kept_spec((KOWN * KX, 128)), name="adjoint_rows", limit=SMALL,
     )(columns, both_rows)
     arrived = from_x(after, far, last)
-    blocks = call(
-        along_x_body, 1, (shaped((128, 128)),) * 4, [kept_spec((GW, 128))] * 4,
-        (kept_spec((128, 128)),) * 4, [pltpu.VMEM((GW, 128), F32)], name="along_x", limit=SMALL,
+    shares = call(
+        along_x_body, 1, (shaped((128, 128)),) + (shaped((128, 128), BF16),) * 3,
+        [kept_spec((GW, 128))] * 4, (kept_spec((128, 128)),) * 4, [pltpu.VMEM((GW, 128), F32)],
+        name="along_x", limit=SMALL,
     )(shot, near, *arrived)
-    sums = call(
-        along_y_body, 0, shaped((MODES + 128, 128)),
+    sums, sent = call(
+        along_y_body, 0, (shaped((MODES + 128, 128)), shaped((MODES + 128, 128), BF16)),
         [kept_spec((128, 128))] * 4 + [kept_spec((MODES, 128))],
-        kept_spec((MODES + 128, 128)), name="along_y", limit=SMALL,
-    )(blocks[0], *from_y(*blocks[1:]), adjoint)
-    local, sums = call(
-        along_z_body, 1, (shaped((64, 128)), shaped((MODES + 8, 128))),
-        [kept_spec((MODES + 128, 128))] * 2,
-        (kept_spec((64, 128)), kept_spec((MODES + 8, 128))), [pltpu.VMEM((128, 128), F32)],
-        name="along_z", limit=SMALL,
-    )(shot, sums, lax.ppermute(sums, "shot", turn(2, 16, SHOT, 1)))
-    parts = from_x(sums, sums, sums)
-    local = local.reshape(4, 16, 8, 4, 4).transpose(1, 4, 0, 2, 3).reshape(64, 128)
-    parts, local = lax.optimization_barrier((parts, local))
-    sums = (sums + parts[0]) + (parts[1] + parts[2])
+        (kept_spec((MODES + 128, 128)),) * 2, name="along_y", limit=SMALL,
+    )(shares[0], *from_y(*shares[1:]), adjoint)
+    carried = (shaped((MODES + 16, 128)), shaped((MODES + 16, 128), BF16))
+    carried_specs = (kept_spec((MODES + 16, 128)),) * 2
+    local, sums, sent = call(
+        along_z_body, 1, (shaped((64, 128)),) + carried,
+        [kept_spec((MODES + 128, 128))] * 2, (kept_spec((64, 128)),) + carried_specs,
+        [pltpu.VMEM((128, 128), F32)], name="along_z", limit=SMALL,
+    )(shot, sums, lax.ppermute(sent, "shot", turn(2, 16, SHOT, 1)))
+    parts = from_x(sent, sent, sent)
+    local = call(
+        arrange_body, 0, shaped((64, 128)),
+        [kept_spec((64, 128)), kept_spec((64, 16)), kept_spec((4, 128, 128))],
+        kept_spec((64, 128)), name="arrange", limit=SMALL,
+    )(local, jnp.asarray(REPEAT), jnp.asarray(PICK))
+    mine = lax.dynamic_index_in_dim(jnp.asarray(BLOCKS), i, 0, keepdims=False)
+    parts, local, mine = lax.optimization_barrier((parts, local, mine))
+    sums, sent = call(
+        join_body, 0, carried, [kept_spec((MODES + 16, 128))] * 4, carried_specs, name="join",
+        limit=SMALL,
+    )(sums, *parts)
 
     modes = call(
         adjoint_mix_body, 0, shaped((SPACE // 2, KX + 8, 128)),
-        [kept_spec((MODES + 8, 128))] * 4
+        [kept_spec((MODES + 16, 128))] * 4
         + [
             full_spec((operator_rows, 128)), full_spec((KOWN, 128, 128)),
             full_spec((KOWN, 128, 128)), full_spec((8, 128)),
         ],
         kept_spec((SPACE // 2, KX + 8, 128)), name="adjoint_mix", limit=SMALL,
-    )(sums, *from_y(sums, sums, sums), operator, spread_high, spread_low, misfits)
+    )(sums, *from_y(sent, sent, sent), operator, spread_high, spread_low, misfits)
     modes = gather_z(modes)
     other_modes = from_core(modes)
     block, misfit = call(

time: 128 us -> 123 us (0.961)
  blocking collectives: 21.9 us -> 8.85 us
  starting transfers between devices: 45.8 us -> 54.1 us
  Pallas kernels: 30.5 us -> 32.9 us
  local copies, waits for them, and re-layouts: 6.91 us -> 4.6 us
    all_to_all x1 -> x0, blocking collectives: 10.4 us -> none  [shards(): stats = lax.all_to_all(stats, 'space', 0, 0, tiled=True)]
    all_to_all x0 -> x1, waiting for transfers between devices: none -> 4.9 us  [shards(): stats = lax.all_to_all(stats, 'space', 0, 0, tiled=True)]
    ppermute x6, waiting for transfers between devices: 7.82 us -> 4.38 us  [from_y(): lax.ppermute(part, 'shot', turn(4, 4, SHOT, by + 1))]
    all_to_all x0 -> x1, starting transfers between devices: none -> 3.44 us  [shards(): stats = lax.all_to_all(stats, 'space', 0, 0, tiled=True)]
    ppermute x6, starting transfers between devices: 6.43 us -> 9.68 us  [from_y(): lax.ppermute(part, 'shot', turn(4, 4, SHOT, by + 1))]
    all_to_all x1, blocking collectives: 11.5 us -> 8.85 us  [gather_z(): lax.all_to_all(copies, 'space', 0, 0, axis_index_groups=[[0, 2, 4, 6], [1...]
    ppermute x2, starting transfers between devices: 10 us -> 12.3 us  [from_core(): return lax.ppermute(values, 'space', [(n, n ^ 1) for n in range(SPACE)])]
    transpose x1 -> x0, local copies, waits for them, and re-layouts: 2 us -> none  [shards(): local.reshape(4, 16, 8, 4, 4).transpose(1, 4, 0, 2, 3).reshape(64, 128)]
  transfers between devices with their start and end apart: 18 -> 19, of which waited for: 13 -> 14; matrix products, arithmetic and copies ran while one was open for 4% -> 1% of each run, Pallas kernels for 8% -> 9%
where the time goes in v3:
time: 123 us
  starting transfers between devices  54.1 us (44%)
  Pallas kernels  32.9 us (27%)
  waiting for transfers between devices  21.4 us (17%)
  blocking collectives  8.85 us (7%)
  local copies, waits for them, and re-layouts  4.6 us (4%)
    ppermute x2, starting transfers between devices, from_core(): return lax.ppermute(values, 'space', [(n, n ^ 1) for n in range(SPACE)])  12.3 us
    ppermute x6, starting transfers between devices, from_y(): lax.ppermute(part, 'shot', turn(4, 4, SHOT, by + 1))  9.68 us
    ppermute x6, starting transfers between devices, from_x(): lax.ppermute(part, 'shot', turn(4, 1, SHOT, by + 1))  9.47 us
    all_to_all x1, blocking collectives, gather_z(): lax.all_to_all(copies, 'space', 0, 0, axis_index_groups=[[0, 2, 4, 6], [1...  8.85 us
    all_to_all x1, starting transfers between devices, shards(): spectra = lax.all_to_all(partial, 'space', 0, 0, tiled=True)  7.4 us
    pallas_call x1, Pallas kernels, shards(): call(forward_body, 2, (shaped((PAIRS, GW)), shaped((PAIRS * C, GW), BF16)...  6.5 us
    pallas_call x1, Pallas kernels, shards(): call(backward_body, 3, (shaped((SPACE, ROWS, 384), BF16),) + (shaped((GW,...  5.88 us
    ppermute x6, waiting for transfers between devices, from_x(): lax.ppermute(part, 'shot', turn(4, 1, SHOT, by + 1))  5.83 us
  transfers between devices with their start and end apart: 19, of which 14 were waited for; matrix products, arithmetic and copies ran while one was open for 1% of the time, Pallas kernels for 9%

profile of v3, /device:TPU:1, one launch (start us, length us, event | category | flops | bytes accessed | tf_op | source)
XLA Modules:
  0.0 122.7 jit_solution(14058482481049290001)
XLA Ops:
  0.6 3.2 %velocity_spectrum.1 = f32[8,48,128]{2,1,0:T(8,128)} custom-call(s32[1]{0:T(128)} %bitcast.own, f32[128,2048]{1,0:T(8,128)} %v_ref.3, bf16[2048,256]{1,0:T(8,128)(2,1)} %constant.51.clone.cols_ref, bf16[8,192,256]{2,1,0:T(8,128)(2,1)} %constant.52.clone.rows_ref), custom_call_target="tpu_custom_call" | custom-call | tf_op jit(solution)/shard_map/velocity_spectrum/pallas_call | solution.py:759
  3.9 7.4 %all-to-all-start = ((f32[8,48,128]{2,1,0:T(8,128)}), f32[8,48,128]{2,1,0:T(8,128)S(1)}, u32[]{:S(2)}, u32[]{:S(2)}) async-start(f32[8,48,128]{2,1,0:T(8,128)} %velocity_spectrum.1), calls=%async_computation | async-start | bytes 393216 | tf_op jit(solution)/shard_map/all_to_all | solution.py:764
  11.3 5.7 %operator.1 = (f32[3456,128]{1,0:T(8,128)}, bf16[3,64,256]{2,1,0:T(8,128)(2,1)}, f32[64,512]{1,0:T(8,128)}) custom-call(s32[1]{0:T(128)} %bitcast.own, s32[4]{0:T(128)} %source_row.1, s32[4]{0:T(128)} %source_column.1, f32[16,64]{1,0:T(8,128)} %bitcast.14, f32[1,64]{1,0:T(1,128)} %bitcast.16, f32[1,64]{1,0:T(1,128)} %bitcast.18, ...), custom_call_target="tpu_custom_call" | custom-call | tf_op jit(solution)/shard_map/operator/pallas_call | solution.py:767
  18.4 3.7 %mix_modes.1 = bf16[4,64,384]{2,1,0:T(8,128)(2,1)} custom-call(s32[1]{0:T(128)} %bitcast.own, f32[8,48,128]{2,1,0:T(8,128)} %copy-done.14, f32[8,48,128]{2,1,0:T(8,128)} %constant.55.clone.ones_ref, f32[3456,128]{1,0:T(8,128)} %get-tuple-element.44.t_ref, bf16[3,64,256]{2,1,0:T(8,128)(2,1)} %get-tuple-element.45.l_ref), custom_call_target="tpu_custom_call" | custom-call | tf_op jit(solution)/shard_map/mix_modes/pallas_call | solution.py:782
  22.1 3.7 %all-to-all-start.1 = ((bf16[4,64,384]{2,1,0:T(8,128)(2,1)}), bf16[4,64,384]{2,1,0:T(8,128)(2,1)S(1)}, u32[]{:S(2)}, u32[]{:S(2)}) async-start(bf16[4,64,384]{2,1,0:T(8,128)(2,1)} %mix_modes.1), calls=%async_computation.1 | async-start | bytes 393216 | tf_op jit(solution)/shard_map/all_to_all | solution.py:724
  25.8 4.3 %velocity_planes.1 = (f32[32,16,512]{2,1,0:T(8,128)}, bf16[48,64]{1,0:T(8,128)(2,1)}, f32[3,64,128]{2,1,0:T(8,128)}, bf16[8,128,128]{2,1,0:T(8,128)(2,1)}, bf16[...) custom-call(s32[1]{0:T(128)} %bitcast.own, s32[4,16]{1,0:T(4,128)} %rows_ref.4, ...), custom_call_target="tpu_custom_call" | custom-call | tf_op jit(solution)/shard_map/velocity_planes/pallas_call | solution.py:793
  31.0 3.6 %collective-permute-start = (bf16[4,64,384]{2,1,0:T(8,128)(2,1)S(1)}, bf16[4,64,384]{2,1,0:T(8,128)(2,1)S(1)}, u32[]{:S(2)}, u32[]{:S(2)}) collective-permute-start(bf16[4,64,384]{2,1,0:T(8,128)(2,1)S(1)} %all-to-all-done.1.d_ref), channel_id=1, source_target_pairs={{0,1},{1,0},{2,3},{3,2},{4,5},{5,4},{6,7},{7,6},{8,9},{9,8},{10,11... | collective-permute-start | bytes 589832 | tf_op jit(solution)/shard_map/ppermute | solution.py:730
  36.4 6.5 %forward_rows.1 = (f32[64,512]{1,0:T(8,128)}, bf16[4096,512]{1,0:T(8,128)(2,1)}, f32[8,8,128]{2,1,0:T(8,128)}) custom-call(s32[1]{0:T(128)} %bitcast.own, s32[144]{0:T(256)} %get-tuple-element.47.list_ref, bf16[4,64,384]{2,1,0:T(8,128)(2,1)} %copy-done.13, bf16[4,64,384]{2,1,0:T(8,128)(2,1)} %copy-done.15, f32[32,16,512]{2,1,0:T(8,128)} %get-tuple-element.50.planes_ref, ...), custom_call_target="tpu_custom_call" | custom-call | tf_op jit(solution)/shard_map/forward_rows/pallas_call | solution.py:817
  43.0 3.4 %all-to-all-start.2 = ((f32[8,8,128]{2,1,0:T(8,128)}), f32[8,8,128]{2,1,0:T(8,128)S(1)}, u32[]{:S(2)}, u32[]{:S(2)}) async-start(f32[8,8,128]{2,1,0:T(8,128)} %get-tuple-element.54), calls=%async_computation.2 | async-start | bytes 65536 | tf_op jit(solution)/shard_map/all_to_all | solution.py:835
  46.4 4.9 %all-to-all-done.2.stats_ref = f32[8,8,128]{2,1,0:T(8,128)S(1)} async-done(((f32[8,8,128]{2,1,0:T(8,128)}), f32[8,8,128]{2,1,0:T(8,128)S(1)}, u32[]{:S(2)}, u32[]{:S(2)}) %all-to-all-start.2) | async-done | bytes 32800 | tf_op jit(solution)/shard_map/all_to_all | solution.py:835
  51.9 5.9 %backward_rows.1 = (bf16[8,32,384]{2,1,0:T(8,128)(2,1)}, bf16[512,128]{1,0:T(8,128)(2,1)}, bf16[512,128]{1,0:T(8,128)(2,1)}, bf16[512,128]{1,0:T(8,128)(2,1)}, b...) custom-call(s32[1]{0:T(128)} %bitcast.own, s32[144]{0:T(256)} %get-tuple-element.47.list_ref, s32[1]{0:T(128)} %bitcast.1.shot, ...), custom_call_target="tpu_custom_call" | custom-call | tf_op jit(solution)/shard_map/backward_rows/pallas_call | solution.py:837
  57.8 3.5 %all-to-all-start.3 = ((bf16[8,32,384]{2,1,0:T(8,128)(2,1)}), bf16[8,32,384]{2,1,0:T(8,128)(2,1)S(1)}, u32[]{:S(2)}, u32[]{:S(2)}) async-start(bf16[8,32,384]{2,1,0:T(8,128)(2,1)} %get-tuple-element.66), calls=%async_computation.3 | async-start | bytes 393216 | tf_op jit(solution)/shard_map/all_to_all | solution.py:854
  61.3 2.0 %collective-permute-start.1 = (bf16[512,128]{1,0:T(8,128)(2,1)}, bf16[512,128]{1,0:T(8,128)(2,1)S(1)}, u32[]{:S(2)}, u32[]{:S(2)}) collective-permute-start(bf16[512,128]{1,0:T(8,128)(2,1)} %get-tuple-element.59), channel_id=1, source_target_pairs={{0,8},{8,16},{16,24},{24,0},{32,40},{40,48},{48,56},{56,32},{64,72... | collective-permute-start | bytes 393224 | tf_op jit(solution)/shard_map/ppermute | solution.py:713
  63.3 1.9 %collective-permute-start.2 = (bf16[512,128]{1,0:T(8,128)(2,1)}, bf16[512,128]{1,0:T(8,128)(2,1)S(1)}, u32[]{:S(2)}, u32[]{:S(2)}) collective-permute-start(bf16[512,128]{1,0:T(8,128)(2,1)} %get-tuple-element.60), channel_id=1, source_target_pairs={{0,16},{8,24},{16,0},{24,8},{32,48},{40,56},{48,32},{56,40},{64,80... | collective-permute-start | bytes 393224 | tf_op jit(solution)/shard_map/ppermute | solution.py:713
  65.2 1.9 %collective-permute-start.3 = (bf16[512,128]{1,0:T(8,128)(2,1)}, bf16[512,128]{1,0:T(8,128)(2,1)S(1)}, u32[]{:S(2)}, u32[]{:S(2)}) collective-permute-start(bf16[512,128]{1,0:T(8,128)(2,1)} %get-tuple-element.61), channel_id=1, source_target_pairs={{0,24},{8,0},{16,8},{24,16},{32,56},{40,32},{48,40},{56,48},{64,88... | collective-permute-start | bytes 393224 | tf_op jit(solution)/shard_map/ppermute | solution.py:713
  67.7 4.0 %collective-permute-done.2.c_ref = bf16[512,128]{1,0:T(8,128)(2,1)S(1)} collective-permute-done((bf16[512,128]{1,0:T(8,128)(2,1)}, bf16[512,128]{1,0:T(8,128)(2,1)S(1)}, u32[]{:S(2)}, u32[]{:S(2)}) %collective-permute-start.2) | collective-permute-done | bytes 131104 | tf_op jit(solution)/shard_map/ppermute | solution.py:713
  73.3 4.0 %collective-permute-start.5 = (bf16[128,128]{1,0:T(8,128)(2,1)S(1)}, bf16[128,128]{1,0:T(8,128)(2,1)S(1)}, u32[]{:S(2)}, u32[]{:S(2)}) collective-permute-start(bf16[128,128]{1,0:T(8,128)(2,1)S(1)} %get-tuple-element.64), channel_id=1, source_target_pairs={{0,64},{8,72},{16,80},{24,88},{32,96},{40,104},{48,112},{56,120},{... | collective-permute-start | bytes 98312 | tf_op jit(solution)/shard_map/ppermute | solution.py:719
  80.4 4.6 %collective-permute-start.7 = (bf16[272,128]{1,0:T(8,128)(2,1)S(1)}, bf16[272,128]{1,0:T(8,128)(2,1)S(1)}, u32[]{:S(2)}, u32[]{:S(2)}) collective-permute-start(bf16[272,128]{1,0:T(8,128)(2,1)S(1)} %get-tuple-element.68), channel_id=1, source_target_pairs={{0,128},{8,136},{16,144},{24,152},{32,160},{40,168},{48,176},{56,1... | collective-permute-start | bytes 208904 | tf_op jit(solution)/shard_map/ppermute | solution.py:877
  85.0 2.6 %collective-permute-done.7.b_ref = bf16[272,128]{1,0:T(8,128)(2,1)S(1)} collective-permute-done((bf16[272,128]{1,0:T(8,128)(2,1)S(1)}, bf16[272,128]{1,0:T(8,128)(2,1)S(1)}, u32[]{:S(2)}, u32[]{:S(2)}) %collective-permute-start.7) | collective-permute-done | bytes 69664 | tf_op jit(solution)/shard_map/ppermute | solution.py:877
  87.7 2.0 %collective-permute-start.10 = (bf16[160,128]{1,0:T(8,128)(2,1)S(1)}, bf16[160,128]{1,0:T(8,128)(2,1)S(1)}, u32[]{:S(2)}, u32[]{:S(2)}) collective-permute-start(bf16[160,128]{1,0:T(8,128)(2,1)S(1)} %get-tuple-element.70), channel_id=1, source_target_pairs={{0,24},{8,0},{16,8},{24,16},{32,56},{40,32},{48,40},{56,48},{64,88... | collective-permute-start | bytes 122888 | tf_op jit(solution)/shard_map/ppermute | solution.py:713
  94.8 3.3 %collective-permute-start.12 = (bf16[160,128]{1,0:T(8,128)(2,1)S(1)}, bf16[160,128]{1,0:T(8,128)(2,1)S(1)}, u32[]{:S(2)}, u32[]{:S(2)}) collective-permute-start(bf16[160,128]{1,0:T(8,128)(2,1)S(1)} %get-tuple-element.76), channel_id=1, source_target_pairs={{0,64},{8,72},{16,80},{24,88},{32,96},{40,104},{48,112},{56,120},{... | collective-permute-start | bytes 122888 | tf_op jit(solution)/shard_map/ppermute | solution.py:719
  102.5 8.8 %all_to_all.25.m_ref = f32[4,56,128]{2,1,0:T(8,128)S(1)} all-to-all(f32[4,56,128]{2,1,0:T(8,128)S(1)} %adjoint_mix.1), channel_id=1, replica_groups={{0,2,4,6},{1,3,5,7},{8,10,12,14},{9,11,13,15},{16,18,20,22},{17,19,21,2..., dimensions={0} | all-to-all | bytes 229376 | tf_op jit(solution)/shard_map/all_to_all | solution.py:724
  111.3 8.7 %collective-permute-start.14 = (f32[4,56,128]{2,1,0:T(8,128)S(1)}, f32[4,56,128]{2,1,0:T(8,128)S(1)}, u32[]{:S(2)}, u32[]{:S(2)}) collective-permute-start(f32[4,56,128]{2,1,0:T(8,128)S(1)} %all_to_all.25.m_ref), channel_id=1, source_target_pairs={{0,1},{1,0},{2,3},{3,2},{4,5},{5,4},{6,7},{7,6},{8,9},{9,8},{10,11... | collective-permute-start | bytes 344072 | tf_op jit(solution)/shard_map/ppermute | solution.py:730
  121.0 1.7 %output_block.1 = (f32[64,128]{1,0:T(8,128)}, f32[1,4]{1,0:T(1,128)}) custom-call(s32[1]{0:T(128)} %bitcast.own, f32[4,56,128]{2,1,0:T(8,128)S(1)} %all_to_all.25.m_ref, f32[4,56,128]{2,1,0:T(8,128)S(1)} %collective-permute-done.14.other_ref, bf16[8,32,96]{2,1,0:T(8,128)(2,1)S(1)} %copy-done.6, bf16[1024,64]{1,0:T(8,128)(2,1)S(1)} %dynamic-slice_bitcast_fusion.block_ref, ...), custom_call_target="tpu_custom_call" | custom-call | tf_op jit(solution)/shard_map/output_block/pallas_call | solution.py:902
  (64 shorter events, 20.5 us)
Async XLA Ops:
  3.9 13.9 %all-to-all-start = ((f32[8,48,128]{2,1,0:T(8,128)}), f32[8,48,128]{2,1,0:T(8,128)S(1)}, u32[]{:S(2)}, u32[]{:S(2)}) async-start(f32[8,48,128]{2,1,0:T(8,128)} %velocity_spectrum.1), calls=%async_computation | async-start | bytes 393216 | tf_op jit(solution)/shard_map/all_to_all | solution.py:764
  22.1 8.8 %all-to-all-start.1 = ((bf16[4,64,384]{2,1,0:T(8,128)(2,1)}), bf16[4,64,384]{2,1,0:T(8,128)(2,1)S(1)}, u32[]{:S(2)}, u32[]{:S(2)}) async-start(bf16[4,64,384]{2,1,0:T(8,128)(2,1)} %mix_modes.1), calls=%async_computation.1 | async-start | bytes 393216 | tf_op jit(solution)/shard_map/all_to_all | solution.py:724
  31.0 4.7 %collective-permute-start = (bf16[4,64,384]{2,1,0:T(8,128)(2,1)S(1)}, bf16[4,64,384]{2,1,0:T(8,128)(2,1)S(1)}, u32[]{:S(2)}, u32[]{:S(2)}) collective-permute-start(bf16[4,64,384]{2,1,0:T(8,128)(2,1)S(1)} %all-to-all-done.1.d_ref), channel_id=1, source_target_pairs={{0,1},{1,0},{2,3},{3,2},{4,5},{5,4},{6,7},{7,6},{8,9},{9,8},{10,11... | collective-permute-start | bytes 589832 | tf_op jit(solution)/shard_map/ppermute | solution.py:730
  42.9 58.0 %copy-start = (f32[3456,128]{1,0:T(8,128)S(1)}, f32[3456,128]{1,0:T(8,128)}, u32[]{:S(2)}) copy-start(f32[3456,128]{1,0:T(8,128)} %get-tuple-element.44.t_ref) | copy-start | bytes 5308420
  43.0 8.3 %all-to-all-start.2 = ((f32[8,8,128]{2,1,0:T(8,128)}), f32[8,8,128]{2,1,0:T(8,128)S(1)}, u32[]{:S(2)}, u32[]{:S(2)}) async-start(f32[8,8,128]{2,1,0:T(8,128)} %get-tuple-element.54), calls=%async_computation.2 | async-start | bytes 65536 | tf_op jit(solution)/shard_map/all_to_all | solution.py:835
  51.9 69.0 %copy-start.6 = (bf16[8,32,96]{2,1,0:T(8,128)(2,1)S(1)}, bf16[8,32,96]{2,1,0:T(8,128)(2,1)}, u32[]{:S(2)}) copy-start(bf16[8,32,96]{2,1,0:T(8,128)(2,1)} %constant.61.clone.back_ref) | copy-start | bytes 147460
  51.9 69.0 %copy-start.8 = (f32[96,128]{1,0:T(8,128)S(1)}, f32[96,128]{1,0:T(8,128)}, u32[]{:S(2)}) copy-start(f32[96,128]{1,0:T(8,128)} %constant.62.clone.diag_rows_ref) | copy-start | bytes 147460
  51.9 69.0 %copy-start.9 = (bf16[96,96]{1,0:T(8,128)(2,1)S(1)}, bf16[96,96]{1,0:T(8,128)(2,1)}, u32[]{:S(2)}) copy-start(bf16[96,96]{1,0:T(8,128)(2,1)} %constant.63.clone.off_rows_ref) | copy-start | bytes 55300
  51.9 69.0 %copy-start.11 = (f32[1,1024]{1,0:T(1,128)S(1)}, f32[1,1024]{1,0:T(1,128)}, u32[]{:S(2)}) copy-start(f32[1,1024]{1,0:T(1,128)} %constant.64.clone.diag_ref) | copy-start | bytes 12292
  57.8 20.7 %all-to-all-start.3 = ((bf16[8,32,384]{2,1,0:T(8,128)(2,1)}), bf16[8,32,384]{2,1,0:T(8,128)(2,1)S(1)}, u32[]{:S(2)}, u32[]{:S(2)}) async-start(bf16[8,32,384]{2,1,0:T(8,128)(2,1)} %get-tuple-element.66), calls=%async_computation.3 | async-start | bytes 393216 | tf_op jit(solution)/shard_map/all_to_all | solution.py:854
  61.3 6.4 %collective-permute-start.1 = (bf16[512,128]{1,0:T(8,128)(2,1)}, bf16[512,128]{1,0:T(8,128)(2,1)S(1)}, u32[]{:S(2)}, u32[]{:S(2)}) collective-permute-start(bf16[512,128]{1,0:T(8,128)(2,1)} %get-tuple-element.59), channel_id=1, source_target_pairs={{0,8},{8,16},{16,24},{24,0},{32,40},{40,48},{48,56},{56,32},{64,72... | collective-permute-start | bytes 393224 | tf_op jit(solution)/shard_map/ppermute | solution.py:713
  63.3 8.4 %collective-permute-start.2 = (bf16[512,128]{1,0:T(8,128)(2,1)}, bf16[512,128]{1,0:T(8,128)(2,1)S(1)}, u32[]{:S(2)}, u32[]{:S(2)}) collective-permute-start(bf16[512,128]{1,0:T(8,128)(2,1)} %get-tuple-element.60), channel_id=1, source_target_pairs={{0,16},{8,24},{16,0},{24,8},{32,48},{40,56},{48,32},{56,40},{64,80... | collective-permute-start | bytes 393224 | tf_op jit(solution)/shard_map/ppermute | solution.py:713
  65.2 6.5 %collective-permute-start.3 = (bf16[512,128]{1,0:T(8,128)(2,1)}, bf16[512,128]{1,0:T(8,128)(2,1)S(1)}, u32[]{:S(2)}, u32[]{:S(2)}) collective-permute-start(bf16[512,128]{1,0:T(8,128)(2,1)} %get-tuple-element.61), channel_id=1, source_target_pairs={{0,24},{8,0},{16,8},{24,16},{32,56},{40,32},{48,40},{56,48},{64,88... | collective-permute-start | bytes 393224 | tf_op jit(solution)/shard_map/ppermute | solution.py:713
  72.7 6.1 %collective-permute-start.4 = (bf16[128,128]{1,0:T(8,128)(2,1)S(1)}, bf16[128,128]{1,0:T(8,128)(2,1)S(1)}, u32[]{:S(2)}, u32[]{:S(2)}) collective-permute-start(bf16[128,128]{1,0:T(8,128)(2,1)S(1)} %get-tuple-element.63), channel_id=1, source_target_pairs={{0,32},{8,40},{16,48},{24,56},{32,64},{40,72},{48,80},{56,88},{64,... | collective-permute-start | bytes 98312 | tf_op jit(solution)/shard_map/ppermute | solution.py:719
  73.3 5.6 %collective-permute-start.5 = (bf16[128,128]{1,0:T(8,128)(2,1)S(1)}, bf16[128,128]{1,0:T(8,128)(2,1)S(1)}, u32[]{:S(2)}, u32[]{:S(2)}) collective-permute-start(bf16[128,128]{1,0:T(8,128)(2,1)S(1)} %get-tuple-element.64), channel_id=1, source_target_pairs={{0,64},{8,72},{16,80},{24,88},{32,96},{40,104},{48,112},{56,120},{... | collective-permute-start | bytes 98312 | tf_op jit(solution)/shard_map/ppermute | solution.py:719
  77.3 3.1 %collective-permute-start.6 = (bf16[128,128]{1,0:T(8,128)(2,1)S(1)}, bf16[128,128]{1,0:T(8,128)(2,1)S(1)}, u32[]{:S(2)}, u32[]{:S(2)}) collective-permute-start(bf16[128,128]{1,0:T(8,128)(2,1)S(1)} %get-tuple-element.65), channel_id=1, source_target_pairs={{0,96},{8,104},{16,112},{24,120},{32,0},{40,8},{48,16},{56,24},{64... | collective-permute-start | bytes 98312 | tf_op jit(solution)/shard_map/ppermute | solution.py:719
  80.4 7.3 %collective-permute-start.7 = (bf16[272,128]{1,0:T(8,128)(2,1)S(1)}, bf16[272,128]{1,0:T(8,128)(2,1)S(1)}, u32[]{:S(2)}, u32[]{:S(2)}) collective-permute-start(bf16[272,128]{1,0:T(8,128)(2,1)S(1)} %get-tuple-element.68), channel_id=1, source_target_pairs={{0,128},{8,136},{16,144},{24,152},{32,160},{40,168},{48,176},{56,1... | collective-permute-start | bytes 208904 | tf_op jit(solution)/shard_map/ppermute | solution.py:877
  87.7 5.3 %collective-permute-start.10 = (bf16[160,128]{1,0:T(8,128)(2,1)S(1)}, bf16[160,128]{1,0:T(8,128)(2,1)S(1)}, u32[]{:S(2)}, u32[]{:S(2)}) collective-permute-start(bf16[160,128]{1,0:T(8,128)(2,1)S(1)} %get-tuple-element.70), channel_id=1, source_target_pairs={{0,24},{8,0},{16,8},{24,16},{32,56},{40,32},{48,40},{56,48},{64,88... | collective-permute-start | bytes 122888 | tf_op jit(solution)/shard_map/ppermute | solution.py:713
  89.7 4.5 %collective-permute-start.8 = (bf16[160,128]{1,0:T(8,128)(2,1)S(1)}, bf16[160,128]{1,0:T(8,128)(2,1)S(1)}, u32[]{:S(2)}, u32[]{:S(2)}) collective-permute-start(bf16[160,128]{1,0:T(8,128)(2,1)S(1)} %get-tuple-element.70), channel_id=1, source_target_pairs={{0,8},{8,16},{16,24},{24,0},{32,40},{40,48},{48,56},{56,32},{64,72... | collective-permute-start | bytes 122888 | tf_op jit(solution)/shard_map/ppermute | solution.py:713
  89.7 4.5 %collective-permute-start.9 = (bf16[160,128]{1,0:T(8,128)(2,1)S(1)}, bf16[160,128]{1,0:T(8,128)(2,1)S(1)}, u32[]{:S(2)}, u32[]{:S(2)}) collective-permute-start(bf16[160,128]{1,0:T(8,128)(2,1)S(1)} %get-tuple-element.70), channel_id=1, source_target_pairs={{0,16},{8,24},{16,0},{24,8},{32,48},{40,56},{48,32},{56,40},{64,80... | collective-permute-start | bytes 122888 | tf_op jit(solution)/shard_map/ppermute | solution.py:713
  94.2 4.4 %collective-permute-start.11 = (bf16[160,128]{1,0:T(8,128)(2,1)S(1)}, bf16[160,128]{1,0:T(8,128)(2,1)S(1)}, u32[]{:S(2)}, u32[]{:S(2)}) collective-permute-start(bf16[160,128]{1,0:T(8,128)(2,1)S(1)} %get-tuple-element.76), channel_id=1, source_target_pairs={{0,32},{8,40},{16,48},{24,56},{32,64},{40,72},{48,80},{56,88},{64,... | collective-permute-start | bytes 122888 | tf_op jit(solution)/shard_map/ppermute | solution.py:719
  94.8 5.1 %collective-permute-start.12 = (bf16[160,128]{1,0:T(8,128)(2,1)S(1)}, bf16[160,128]{1,0:T(8,128)(2,1)S(1)}, u32[]{:S(2)}, u32[]{:S(2)}) collective-permute-start(bf16[160,128]{1,0:T(8,128)(2,1)S(1)} %get-tuple-element.76), channel_id=1, source_target_pairs={{0,64},{8,72},{16,80},{24,88},{32,96},{40,104},{48,112},{56,120},{... | collective-permute-start | bytes 122888 | tf_op jit(solution)/shard_map/ppermute | solution.py:719
  98.0 2.9 %collective-permute-start.13 = (bf16[160,128]{1,0:T(8,128)(2,1)S(1)}, bf16[160,128]{1,0:T(8,128)(2,1)S(1)}, u32[]{:S(2)}, u32[]{:S(2)}) collective-permute-start(bf16[160,128]{1,0:T(8,128)(2,1)S(1)} %get-tuple-element.76), channel_id=1, source_target_pairs={{0,96},{8,104},{16,112},{24,120},{32,0},{40,8},{48,16},{56,24},{64... | collective-permute-start | bytes 122888 | tf_op jit(solution)/shard_map/ppermute | solution.py:719
  111.3 9.6 %collective-permute-start.14 = (f32[4,56,128]{2,1,0:T(8,128)S(1)}, f32[4,56,128]{2,1,0:T(8,128)S(1)}, u32[]{:S(2)}, u32[]{:S(2)}) collective-permute-start(f32[4,56,128]{2,1,0:T(8,128)S(1)} %all_to_all.25.m_ref), channel_id=1, source_target_pairs={{0,1},{1,0},{2,3},{3,2},{4,5},{5,4},{6,7},{7,6},{8,9},{9,8},{10,11... | collective-permute-start | bytes 344072 | tf_op jit(solution)/shard_map/ppermute | solution.py:730
  (12 other events, 320.3 us)

commit v4 on v3

--- a/solution.py
+++ b/solution.py
@@ -555,6 +555,11 @@
 MODES = KOWN * KX
 
 
+def hold_body(near_ref, misfit_ref, near_out_ref, misfit_out_ref):
+    near_out_ref[...] = near_ref[...]
+    misfit_out_ref[...] = misfit_ref[...]
+
+
 def along_x_body(shot, a_ref, b_ref, c_ref, d_ref, near_ref, next_ref, far_ref, last_ref, tmp):
     tmp[...] = (a_ref[...].astype(F32) + b_ref[...].astype(F32)) + (
         c_ref[...].astype(F32) + d_ref[...].astype(F32)
@@ -858,6 +863,12 @@
         kept_spec((KOWN * KX, 128)), name="adjoint_rows", limit=SMALL,
     )(columns, both_rows)
     arrived = from_x(after, far, last)
+    near, misfits = call(
+        hold_body, 0, (shaped((GW, 128), BF16), shaped((8, 128))),
+        [kept_spec((GW, 128)), kept_spec((8, 128))], (kept_spec((GW, 128)), kept_spec((8, 128))),
+        name="hold", limit=SMALL,
+    )(near, misfits)
+    near, misfits, *arrived = lax.optimization_barrier((near, misfits, *arrived))
     shares = call(
         along_x_body, 1, (shaped((128, 128)),) + (shaped((128, 128), BF16),) * 3,
         [kept_spec((GW, 128))] * 4, (kept_spec((128, 128)),) * 4, [pltpu.VMEM((GW, 128), F32)],

time: 123 us -> 122 us (level)
  starting transfers between devices: 54.1 us -> 52.3 us
    ppermute x1, starting transfers between devices: 4.64 us -> 3.38 us  [shards(): lax.ppermute(sent, 'shot', turn(2, 16, SHOT, 1))]
  transfers between devices with their start and end apart: 19 -> 19, of which waited for: 14 -> 13; matrix products, arithmetic and copies ran while one was open for 1% -> 1% of each run, Pallas kernels for 9% -> 9%
where the time goes in v4:
time: 122 us
  starting transfers between devices  52.3 us (43%)
  Pallas kernels  32.9 us (27%)
  waiting for transfers between devices  22.6 us (19%)
  blocking collectives  8.33 us (7%)
  local copies, waits for them, and re-layouts  4.62 us (4%)
    ppermute x2, starting transfers between devices, from_core(): return lax.ppermute(values, 'space', [(n, n ^ 1) for n in range(SPACE)])  12.2 us
    ppermute x6, starting transfers between devices, from_x(): lax.ppermute(part, 'shot', turn(4, 1, SHOT, by + 1))  9.26 us
    ppermute x6, starting transfers between devices, from_y(): lax.ppermute(part, 'shot', turn(4, 4, SHOT, by + 1))  9.16 us
    all_to_all x1, blocking collectives, gather_z(): lax.all_to_all(copies, 'space', 0, 0, axis_index_groups=[[0, 2, 4, 6], [1...  8.33 us
    all_to_all x1, starting transfers between devices, shards(): spectra = lax.all_to_all(partial, 'space', 0, 0, tiled=True)  7.4 us
    pallas_call x1, Pallas kernels, shards(): call(forward_body, 2, (shaped((PAIRS, GW)), shaped((PAIRS * C, GW), BF16)...  6.49 us
    pallas_call x1, Pallas kernels, shards(): call(backward_body, 3, (shaped((SPACE, ROWS, 384), BF16),) + (shaped((GW,...  5.84 us
    pallas_call x1, Pallas kernels, shards(): call(operator_body, 3, (shaped((operator_rows, 128)), shaped((KOWN, PAIRS...  5.67 us
  transfers between devices with their start and end apart: 19, of which 13 were waited for; matrix products, arithmetic and copies ran while one was open for 1% of the time, Pallas kernels for 9%

profile of v4, /device:TPU:1, one launch (start us, length us, event | category | flops | bytes accessed | tf_op | source)
XLA Modules:
  0.0 121.6 jit_solution(11911712198049356644)
XLA Ops:
  0.6 3.2 %velocity_spectrum.1 = f32[8,48,128]{2,1,0:T(8,128)} custom-call(s32[1]{0:T(128)} %bitcast.own, f32[128,2048]{1,0:T(8,128)} %v_ref.3, bf16[2048,256]{1,0:T(8,128)(2,1)} %constant.51.clone.cols_ref, bf16[8,192,256]{2,1,0:T(8,128)(2,1)} %constant.52.clone.rows_ref), custom_call_target="tpu_custom_call" | custom-call | tf_op jit(solution)/shard_map/velocity_spectrum/pallas_call | solution.py:764
  3.9 7.4 %all-to-all-start = ((f32[8,48,128]{2,1,0:T(8,128)}), f32[8,48,128]{2,1,0:T(8,128)S(1)}, u32[]{:S(2)}, u32[]{:S(2)}) async-start(f32[8,48,128]{2,1,0:T(8,128)} %velocity_spectrum.1), calls=%async_computation | async-start | bytes 393216 | tf_op jit(solution)/shard_map/all_to_all | solution.py:769
  11.3 5.7 %operator.1 = (f32[3456,128]{1,0:T(8,128)}, bf16[3,64,256]{2,1,0:T(8,128)(2,1)}, f32[64,512]{1,0:T(8,128)}) custom-call(s32[1]{0:T(128)} %bitcast.own, s32[4]{0:T(128)} %source_row.1, s32[4]{0:T(128)} %source_column.1, f32[16,64]{1,0:T(8,128)} %bitcast.14, f32[1,64]{1,0:T(1,128)} %bitcast.16, f32[1,64]{1,0:T(1,128)} %bitcast.18, ...), custom_call_target="tpu_custom_call" | custom-call | tf_op jit(solution)/shard_map/operator/pallas_call | solution.py:772
  18.4 3.7 %mix_modes.1 = bf16[4,64,384]{2,1,0:T(8,128)(2,1)} custom-call(s32[1]{0:T(128)} %bitcast.own, f32[8,48,128]{2,1,0:T(8,128)} %copy-done.14, f32[8,48,128]{2,1,0:T(8,128)} %constant.55.clone.ones_ref, f32[3456,128]{1,0:T(8,128)} %get-tuple-element.51.t_ref, bf16[3,64,256]{2,1,0:T(8,128)(2,1)} %get-tuple-element.52.l_ref), custom_call_target="tpu_custom_call" | custom-call | tf_op jit(solution)/shard_map/mix_modes/pallas_call | solution.py:787
  22.2 3.7 %all-to-all-start.1 = ((bf16[4,64,384]{2,1,0:T(8,128)(2,1)}), bf16[4,64,384]{2,1,0:T(8,128)(2,1)S(1)}, u32[]{:S(2)}, u32[]{:S(2)}) async-start(bf16[4,64,384]{2,1,0:T(8,128)(2,1)} %mix_modes.1), calls=%async_computation.1 | async-start | bytes 393216 | tf_op jit(solution)/shard_map/all_to_all | solution.py:729
  25.8 4.3 %velocity_planes.1 = (f32[32,16,512]{2,1,0:T(8,128)}, bf16[48,64]{1,0:T(8,128)(2,1)}, f32[3,64,128]{2,1,0:T(8,128)}, bf16[8,128,128]{2,1,0:T(8,128)(2,1)}, bf16[...) custom-call(s32[1]{0:T(128)} %bitcast.own, s32[4,16]{1,0:T(4,128)} %rows_ref.4, ...), custom_call_target="tpu_custom_call" | custom-call | tf_op jit(solution)/shard_map/velocity_planes/pallas_call | solution.py:798
  31.0 3.6 %collective-permute-start = (bf16[4,64,384]{2,1,0:T(8,128)(2,1)S(1)}, bf16[4,64,384]{2,1,0:T(8,128)(2,1)S(1)}, u32[]{:S(2)}, u32[]{:S(2)}) collective-permute-start(bf16[4,64,384]{2,1,0:T(8,128)(2,1)S(1)} %all-to-all-done.1.d_ref), channel_id=1, source_target_pairs={{0,1},{1,0},{2,3},{3,2},{4,5},{5,4},{6,7},{7,6},{8,9},{9,8},{10,11... | collective-permute-start | bytes 589832 | tf_op jit(solution)/shard_map/ppermute | solution.py:735
  36.4 6.5 %forward_rows.1 = (f32[64,512]{1,0:T(8,128)}, bf16[4096,512]{1,0:T(8,128)(2,1)}, f32[8,8,128]{2,1,0:T(8,128)}) custom-call(s32[1]{0:T(128)} %bitcast.own, s32[144]{0:T(256)} %get-tuple-element.54.list_ref, bf16[4,64,384]{2,1,0:T(8,128)(2,1)} %copy-done.13, bf16[4,64,384]{2,1,0:T(8,128)(2,1)} %copy-done.15, f32[32,16,512]{2,1,0:T(8,128)} %get-tuple-element.57.planes_ref, ...), custom_call_target="tpu_custom_call" | custom-call | tf_op jit(solution)/shard_map/forward_rows/pallas_call | solution.py:822
  43.0 3.4 %all-to-all-start.2 = ((f32[8,8,128]{2,1,0:T(8,128)}), f32[8,8,128]{2,1,0:T(8,128)S(1)}, u32[]{:S(2)}, u32[]{:S(2)}) async-start(f32[8,8,128]{2,1,0:T(8,128)} %get-tuple-element.61), calls=%async_computation.2 | async-start | bytes 65536 | tf_op jit(solution)/shard_map/all_to_all | solution.py:840
  46.4 4.8 %all-to-all-done.2.stats_ref = f32[8,8,128]{2,1,0:T(8,128)S(1)} async-done(((f32[8,8,128]{2,1,0:T(8,128)}), f32[8,8,128]{2,1,0:T(8,128)S(1)}, u32[]{:S(2)}, u32[]{:S(2)}) %all-to-all-start.2) | async-done | bytes 32800 | tf_op jit(solution)/shard_map/all_to_all | solution.py:840
  51.9 5.8 %backward_rows.1 = (bf16[8,32,384]{2,1,0:T(8,128)(2,1)}, bf16[512,128]{1,0:T(8,128)(2,1)}, bf16[512,128]{1,0:T(8,128)(2,1)}, bf16[512,128]{1,0:T(8,128)(2,1)}, b...) custom-call(s32[1]{0:T(128)} %bitcast.own, s32[144]{0:T(256)} %get-tuple-element.54.list_ref, s32[1]{0:T(128)} %bitcast.1.shot, ...), custom_call_target="tpu_custom_call" | custom-call | tf_op jit(solution)/shard_map/backward_rows/pallas_call | solution.py:842
  57.7 3.8 %all-to-all-start.3 = ((bf16[8,32,384]{2,1,0:T(8,128)(2,1)}), bf16[8,32,384]{2,1,0:T(8,128)(2,1)S(1)}, u32[]{:S(2)}, u32[]{:S(2)}) async-start(bf16[8,32,384]{2,1,0:T(8,128)(2,1)} %get-tuple-element.80), calls=%async_computation.3 | async-start | bytes 393216 | tf_op jit(solution)/shard_map/all_to_all | solution.py:859
  61.5 1.6 %collective-permute-start.1 = (bf16[512,128]{1,0:T(8,128)(2,1)}, bf16[512,128]{1,0:T(8,128)(2,1)S(1)}, u32[]{:S(2)}, u32[]{:S(2)}) collective-permute-start(bf16[512,128]{1,0:T(8,128)(2,1)} %get-tuple-element.69), channel_id=1, source_target_pairs={{0,8},{8,16},{16,24},{24,0},{32,40},{40,48},{48,56},{56,32},{64,72... | collective-permute-start | bytes 393224 | tf_op jit(solution)/shard_map/ppermute | solution.py:718
  63.1 2.2 %collective-permute-start.2 = (bf16[512,128]{1,0:T(8,128)(2,1)}, bf16[512,128]{1,0:T(8,128)(2,1)S(1)}, u32[]{:S(2)}, u32[]{:S(2)}) collective-permute-start(bf16[512,128]{1,0:T(8,128)(2,1)} %get-tuple-element.70), channel_id=1, source_target_pairs={{0,16},{8,24},{16,0},{24,8},{32,48},{40,56},{48,32},{56,40},{64,80... | collective-permute-start | bytes 393224 | tf_op jit(solution)/shard_map/ppermute | solution.py:718
  67.9 3.9 %collective-permute-done.2.c_ref = bf16[512,128]{1,0:T(8,128)(2,1)S(1)} collective-permute-done((bf16[512,128]{1,0:T(8,128)(2,1)}, bf16[512,128]{1,0:T(8,128)(2,1)S(1)}, u32[]{:S(2)}, u32[]{:S(2)}) %collective-permute-start.2) | collective-permute-done | bytes 131104 | tf_op jit(solution)/shard_map/ppermute | solution.py:718
  71.9 2.3 %collective-permute-start.4 = (bf16[128,128]{1,0:T(8,128)(2,1)S(1)}, bf16[128,128]{1,0:T(8,128)(2,1)S(1)}, u32[]{:S(2)}, u32[]{:S(2)}) collective-permute-start(bf16[128,128]{1,0:T(8,128)(2,1)S(1)} %get-tuple-element.77), channel_id=1, source_target_pairs={{0,32},{8,40},{16,48},{24,56},{32,64},{40,72},{48,80},{56,88},{64,... | collective-permute-start | bytes 98312 | tf_op jit(solution)/shard_map/ppermute | solution.py:724
  74.2 3.2 %collective-permute-start.5 = (bf16[128,128]{1,0:T(8,128)(2,1)S(1)}, bf16[128,128]{1,0:T(8,128)(2,1)S(1)}, u32[]{:S(2)}, u32[]{:S(2)}) collective-permute-start(bf16[128,128]{1,0:T(8,128)(2,1)S(1)} %get-tuple-element.78), channel_id=1, source_target_pairs={{0,64},{8,72},{16,80},{24,88},{32,96},{40,104},{48,112},{56,120},{... | collective-permute-start | bytes 98312 | tf_op jit(solution)/shard_map/ppermute | solution.py:724
  80.6 3.4 %collective-permute-start.7 = (bf16[272,128]{1,0:T(8,128)(2,1)S(1)}, bf16[272,128]{1,0:T(8,128)(2,1)S(1)}, u32[]{:S(2)}, u32[]{:S(2)}) collective-permute-start(bf16[272,128]{1,0:T(8,128)(2,1)S(1)} %get-tuple-element.82), channel_id=1, source_target_pairs={{0,128},{8,136},{16,144},{24,152},{32,160},{40,168},{48,176},{56,1... | collective-permute-start | bytes 208904 | tf_op jit(solution)/shard_map/ppermute | solution.py:888
  84.0 3.8 %collective-permute-done.7.b_ref = bf16[272,128]{1,0:T(8,128)(2,1)S(1)} collective-permute-done((bf16[272,128]{1,0:T(8,128)(2,1)S(1)}, bf16[272,128]{1,0:T(8,128)(2,1)S(1)}, u32[]{:S(2)}, u32[]{:S(2)}) %collective-permute-start.7) | collective-permute-done | bytes 69664 | tf_op jit(solution)/shard_map/ppermute | solution.py:888
  87.9 3.0 %collective-permute-start.10 = (bf16[160,128]{1,0:T(8,128)(2,1)S(1)}, bf16[160,128]{1,0:T(8,128)(2,1)S(1)}, u32[]{:S(2)}, u32[]{:S(2)}) collective-permute-start(bf16[160,128]{1,0:T(8,128)(2,1)S(1)} %get-tuple-element.84), channel_id=1, source_target_pairs={{0,24},{8,0},{16,8},{24,16},{32,56},{40,32},{48,40},{56,48},{64,88... | collective-permute-start | bytes 122888 | tf_op jit(solution)/shard_map/ppermute | solution.py:718
  95.5 2.7 %collective-permute-start.12 = (bf16[160,128]{1,0:T(8,128)(2,1)S(1)}, bf16[160,128]{1,0:T(8,128)(2,1)S(1)}, u32[]{:S(2)}, u32[]{:S(2)}) collective-permute-start(bf16[160,128]{1,0:T(8,128)(2,1)S(1)} %get-tuple-element.90), channel_id=1, source_target_pairs={{0,64},{8,72},{16,80},{24,88},{32,96},{40,104},{48,112},{56,120},{... | collective-permute-start | bytes 122888 | tf_op jit(solution)/shard_map/ppermute | solution.py:724
  102.0 8.3 %all_to_all.25.m_ref = f32[4,56,128]{2,1,0:T(8,128)S(1)} all-to-all(f32[4,56,128]{2,1,0:T(8,128)S(1)} %adjoint_mix.1), channel_id=1, replica_groups={{0,2,4,6},{1,3,5,7},{8,10,12,14},{9,11,13,15},{16,18,20,22},{17,19,21,2..., dimensions={0} | all-to-all | bytes 229376 | tf_op jit(solution)/shard_map/all_to_all | solution.py:729
  110.4 8.6 %collective-permute-start.14 = (f32[4,56,128]{2,1,0:T(8,128)S(1)}, f32[4,56,128]{2,1,0:T(8,128)S(1)}, u32[]{:S(2)}, u32[]{:S(2)}) collective-permute-start(f32[4,56,128]{2,1,0:T(8,128)S(1)} %all_to_all.25.m_ref), channel_id=1, source_target_pairs={{0,1},{1,0},{2,3},{3,2},{4,5},{5,4},{6,7},{7,6},{8,9},{9,8},{10,11... | collective-permute-start | bytes 344072 | tf_op jit(solution)/shard_map/ppermute | solution.py:735
  119.9 1.7 %output_block.1 = (f32[64,128]{1,0:T(8,128)}, f32[1,4]{1,0:T(1,128)}) custom-call(s32[1]{0:T(128)} %bitcast.own, f32[4,56,128]{2,1,0:T(8,128)S(1)} %all_to_all.25.m_ref, f32[4,56,128]{2,1,0:T(8,128)S(1)} %collective-permute-done.14.other_ref, bf16[8,32,96]{2,1,0:T(8,128)(2,1)S(1)} %copy-done.6, bf16[1024,64]{1,0:T(8,128)(2,1)S(1)} %dynamic-slice_bitcast_fusion.block_ref, ...), custom_call_target="tpu_custom_call" | custom-call | tf_op jit(solution)/shard_map/output_block/pallas_call | solution.py:913
  (65 shorter events, 20.1 us)
Async XLA Ops:
  3.9 13.9 %all-to-all-start = ((f32[8,48,128]{2,1,0:T(8,128)}), f32[8,48,128]{2,1,0:T(8,128)S(1)}, u32[]{:S(2)}, u32[]{:S(2)}) async-start(f32[8,48,128]{2,1,0:T(8,128)} %velocity_spectrum.1), calls=%async_computation | async-start | bytes 393216 | tf_op jit(solution)/shard_map/all_to_all | solution.py:769
  22.2 8.8 %all-to-all-start.1 = ((bf16[4,64,384]{2,1,0:T(8,128)(2,1)}), bf16[4,64,384]{2,1,0:T(8,128)(2,1)S(1)}, u32[]{:S(2)}, u32[]{:S(2)}) async-start(bf16[4,64,384]{2,1,0:T(8,128)(2,1)} %mix_modes.1), calls=%async_computation.1 | async-start | bytes 393216 | tf_op jit(solution)/shard_map/all_to_all | solution.py:729
  31.0 4.7 %collective-permute-start = (bf16[4,64,384]{2,1,0:T(8,128)(2,1)S(1)}, bf16[4,64,384]{2,1,0:T(8,128)(2,1)S(1)}, u32[]{:S(2)}, u32[]{:S(2)}) collective-permute-start(bf16[4,64,384]{2,1,0:T(8,128)(2,1)S(1)} %all-to-all-done.1.d_ref), channel_id=1, source_target_pairs={{0,1},{1,0},{2,3},{3,2},{4,5},{5,4},{6,7},{7,6},{8,9},{9,8},{10,11... | collective-permute-start | bytes 589832 | tf_op jit(solution)/shard_map/ppermute | solution.py:735
  42.9 58.2 %copy-start = (f32[3456,128]{1,0:T(8,128)S(1)}, f32[3456,128]{1,0:T(8,128)}, u32[]{:S(2)}) copy-start(f32[3456,128]{1,0:T(8,128)} %get-tuple-element.51.t_ref) | copy-start | bytes 5308420
  43.0 8.3 %all-to-all-start.2 = ((f32[8,8,128]{2,1,0:T(8,128)}), f32[8,8,128]{2,1,0:T(8,128)S(1)}, u32[]{:S(2)}, u32[]{:S(2)}) async-start(f32[8,8,128]{2,1,0:T(8,128)} %get-tuple-element.61), calls=%async_computation.2 | async-start | bytes 65536 | tf_op jit(solution)/shard_map/all_to_all | solution.py:840
  51.9 68.0 %copy-start.6 = (bf16[8,32,96]{2,1,0:T(8,128)(2,1)S(1)}, bf16[8,32,96]{2,1,0:T(8,128)(2,1)}, u32[]{:S(2)}) copy-start(bf16[8,32,96]{2,1,0:T(8,128)(2,1)} %constant.61.clone.back_ref) | copy-start | bytes 147460
  51.9 68.0 %copy-start.8 = (f32[96,128]{1,0:T(8,128)S(1)}, f32[96,128]{1,0:T(8,128)}, u32[]{:S(2)}) copy-start(f32[96,128]{1,0:T(8,128)} %constant.62.clone.diag_rows_ref) | copy-start | bytes 147460
  51.9 68.0 %copy-start.9 = (bf16[96,96]{1,0:T(8,128)(2,1)S(1)}, bf16[96,96]{1,0:T(8,128)(2,1)}, u32[]{:S(2)}) copy-start(bf16[96,96]{1,0:T(8,128)(2,1)} %constant.63.clone.off_rows_ref) | copy-start | bytes 55300
  51.9 68.0 %copy-start.11 = (f32[1,1024]{1,0:T(1,128)S(1)}, f32[1,1024]{1,0:T(1,128)}, u32[]{:S(2)}) copy-start(f32[1,1024]{1,0:T(1,128)} %constant.64.clone.diag_ref) | copy-start | bytes 12292
  57.7 19.9 %all-to-all-start.3 = ((bf16[8,32,384]{2,1,0:T(8,128)(2,1)}), bf16[8,32,384]{2,1,0:T(8,128)(2,1)S(1)}, u32[]{:S(2)}, u32[]{:S(2)}) async-start(bf16[8,32,384]{2,1,0:T(8,128)(2,1)} %get-tuple-element.80), calls=%async_computation.3 | async-start | bytes 393216 | tf_op jit(solution)/shard_map/all_to_all | solution.py:859
  61.5 6.4 %collective-permute-start.1 = (bf16[512,128]{1,0:T(8,128)(2,1)}, bf16[512,128]{1,0:T(8,128)(2,1)S(1)}, u32[]{:S(2)}, u32[]{:S(2)}) collective-permute-start(bf16[512,128]{1,0:T(8,128)(2,1)} %get-tuple-element.69), channel_id=1, source_target_pairs={{0,8},{8,16},{16,24},{24,0},{32,40},{40,48},{48,56},{56,32},{64,72... | collective-permute-start | bytes 393224 | tf_op jit(solution)/shard_map/ppermute | solution.py:718
  63.1 8.7 %collective-permute-start.2 = (bf16[512,128]{1,0:T(8,128)(2,1)}, bf16[512,128]{1,0:T(8,128)(2,1)S(1)}, u32[]{:S(2)}, u32[]{:S(2)}) collective-permute-start(bf16[512,128]{1,0:T(8,128)(2,1)} %get-tuple-element.70), channel_id=1, source_target_pairs={{0,16},{8,24},{16,0},{24,8},{32,48},{40,56},{48,32},{56,40},{64,80... | collective-permute-start | bytes 393224 | tf_op jit(solution)/shard_map/ppermute | solution.py:718
  65.2 6.6 %collective-permute-start.3 = (bf16[512,128]{1,0:T(8,128)(2,1)}, bf16[512,128]{1,0:T(8,128)(2,1)S(1)}, u32[]{:S(2)}, u32[]{:S(2)}) collective-permute-start(bf16[512,128]{1,0:T(8,128)(2,1)} %get-tuple-element.71), channel_id=1, source_target_pairs={{0,24},{8,0},{16,8},{24,16},{32,56},{40,32},{48,40},{56,48},{64,88... | collective-permute-start | bytes 393224 | tf_op jit(solution)/shard_map/ppermute | solution.py:718
  71.9 6.0 %collective-permute-start.4 = (bf16[128,128]{1,0:T(8,128)(2,1)S(1)}, bf16[128,128]{1,0:T(8,128)(2,1)S(1)}, u32[]{:S(2)}, u32[]{:S(2)}) collective-permute-start(bf16[128,128]{1,0:T(8,128)(2,1)S(1)} %get-tuple-element.77), channel_id=1, source_target_pairs={{0,32},{8,40},{16,48},{24,56},{32,64},{40,72},{48,80},{56,88},{64,... | collective-permute-start | bytes 98312 | tf_op jit(solution)/shard_map/ppermute | solution.py:724
  74.2 4.9 %collective-permute-start.5 = (bf16[128,128]{1,0:T(8,128)(2,1)S(1)}, bf16[128,128]{1,0:T(8,128)(2,1)S(1)}, u32[]{:S(2)}, u32[]{:S(2)}) collective-permute-start(bf16[128,128]{1,0:T(8,128)(2,1)S(1)} %get-tuple-element.78), channel_id=1, source_target_pairs={{0,64},{8,72},{16,80},{24,88},{32,96},{40,104},{48,112},{56,120},{... | collective-permute-start | bytes 98312 | tf_op jit(solution)/shard_map/ppermute | solution.py:724
  77.4 3.2 %collective-permute-start.6 = (bf16[128,128]{1,0:T(8,128)(2,1)S(1)}, bf16[128,128]{1,0:T(8,128)(2,1)S(1)}, u32[]{:S(2)}, u32[]{:S(2)}) collective-permute-start(bf16[128,128]{1,0:T(8,128)(2,1)S(1)} %get-tuple-element.79), channel_id=1, source_target_pairs={{0,96},{8,104},{16,112},{24,120},{32,0},{40,8},{48,16},{56,24},{64... | collective-permute-start | bytes 98312 | tf_op jit(solution)/shard_map/ppermute | solution.py:724
  80.6 7.2 %collective-permute-start.7 = (bf16[272,128]{1,0:T(8,128)(2,1)S(1)}, bf16[272,128]{1,0:T(8,128)(2,1)S(1)}, u32[]{:S(2)}, u32[]{:S(2)}) collective-permute-start(bf16[272,128]{1,0:T(8,128)(2,1)S(1)} %get-tuple-element.82), channel_id=1, source_target_pairs={{0,128},{8,136},{16,144},{24,152},{32,160},{40,168},{48,176},{56,1... | collective-permute-start | bytes 208904 | tf_op jit(solution)/shard_map/ppermute | solution.py:888
  87.9 6.1 %collective-permute-start.10 = (bf16[160,128]{1,0:T(8,128)(2,1)S(1)}, bf16[160,128]{1,0:T(8,128)(2,1)S(1)}, u32[]{:S(2)}, u32[]{:S(2)}) collective-permute-start(bf16[160,128]{1,0:T(8,128)(2,1)S(1)} %get-tuple-element.84), channel_id=1, source_target_pairs={{0,24},{8,0},{16,8},{24,16},{32,56},{40,32},{48,40},{56,48},{64,88... | collective-permute-start | bytes 122888 | tf_op jit(solution)/shard_map/ppermute | solution.py:718
  90.9 4.5 %collective-permute-start.8 = (bf16[160,128]{1,0:T(8,128)(2,1)S(1)}, bf16[160,128]{1,0:T(8,128)(2,1)S(1)}, u32[]{:S(2)}, u32[]{:S(2)}) collective-permute-start(bf16[160,128]{1,0:T(8,128)(2,1)S(1)} %get-tuple-element.84), channel_id=1, source_target_pairs={{0,8},{8,16},{16,24},{24,0},{32,40},{40,48},{48,56},{56,32},{64,72... | collective-permute-start | bytes 122888 | tf_op jit(solution)/shard_map/ppermute | solution.py:718
  90.9 4.5 %collective-permute-start.9 = (bf16[160,128]{1,0:T(8,128)(2,1)S(1)}, bf16[160,128]{1,0:T(8,128)(2,1)S(1)}, u32[]{:S(2)}, u32[]{:S(2)}) collective-permute-start(bf16[160,128]{1,0:T(8,128)(2,1)S(1)} %get-tuple-element.84), channel_id=1, source_target_pairs={{0,16},{8,24},{16,0},{24,8},{32,48},{40,56},{48,32},{56,40},{64,80... | collective-permute-start | bytes 122888 | tf_op jit(solution)/shard_map/ppermute | solution.py:718
  95.4 4.2 %collective-permute-start.11 = (bf16[160,128]{1,0:T(8,128)(2,1)S(1)}, bf16[160,128]{1,0:T(8,128)(2,1)S(1)}, u32[]{:S(2)}, u32[]{:S(2)}) collective-permute-start(bf16[160,128]{1,0:T(8,128)(2,1)S(1)} %get-tuple-element.90), channel_id=1, source_target_pairs={{0,32},{8,40},{16,48},{24,56},{32,64},{40,72},{48,80},{56,88},{64,... | collective-permute-start | bytes 122888 | tf_op jit(solution)/shard_map/ppermute | solution.py:724
  95.5 4.6 %collective-permute-start.12 = (bf16[160,128]{1,0:T(8,128)(2,1)S(1)}, bf16[160,128]{1,0:T(8,128)(2,1)S(1)}, u32[]{:S(2)}, u32[]{:S(2)}) collective-permute-start(bf16[160,128]{1,0:T(8,128)(2,1)S(1)} %get-tuple-element.90), channel_id=1, source_target_pairs={{0,64},{8,72},{16,80},{24,88},{32,96},{40,104},{48,112},{56,120},{... | collective-permute-start | bytes 122888 | tf_op jit(solution)/shard_map/ppermute | solution.py:724
  98.3 2.9 %collective-permute-start.13 = (bf16[160,128]{1,0:T(8,128)(2,1)S(1)}, bf16[160,128]{1,0:T(8,128)(2,1)S(1)}, u32[]{:S(2)}, u32[]{:S(2)}) collective-permute-start(bf16[160,128]{1,0:T(8,128)(2,1)S(1)} %get-tuple-element.90), channel_id=1, source_target_pairs={{0,96},{8,104},{16,112},{24,120},{32,0},{40,8},{48,16},{56,24},{64... | collective-permute-start | bytes 122888 | tf_op jit(solution)/shard_map/ppermute | solution.py:724
  110.4 9.5 %collective-permute-start.14 = (f32[4,56,128]{2,1,0:T(8,128)S(1)}, f32[4,56,128]{2,1,0:T(8,128)S(1)}, u32[]{:S(2)}, u32[]{:S(2)}) collective-permute-start(f32[4,56,128]{2,1,0:T(8,128)S(1)} %all_to_all.25.m_ref), channel_id=1, source_target_pairs={{0,1},{1,0},{2,3},{3,2},{4,5},{5,4},{6,7},{7,6},{8,9},{9,8},{10,11... | collective-permute-start | bytes 344072 | tf_op jit(solution)/shard_map/ppermute | solution.py:735
  (12 other events, 321.8 us)

commit v5 on v4

--- a/solution.py
+++ b/solution.py
@@ -249,8 +249,8 @@
 
 
 def planes_body(
-    own, rows_ref, v_ref, sel_ref, enc_ref, bias_ref, amp_ref, point_ref, layer_ref, weight_ref, lanes_ref,
-    out_ref, wk_ref, vec_ref, place_ref, high_ref, low_ref, list_ref, tmp,
+    own, rows_ref, v_ref, sel_ref, enc_ref, bias_ref, amp_ref, point_ref, layer_ref, weight_ref,
+    out_ref, wk_ref, vec_ref, list_ref, tmp,
 ):
     def find(r, count):
         row = rows_ref[r >> 4, r & 15] - own[0] * ROWS
@@ -283,6 +283,11 @@
     vec_ref[0] = column_of(pointed[17:18])
     vec_ref[1] = column_of(pointed[16:17] + layer_ref[...])
     vec_ref[2] = column_of(weight_ref[...])
+
+
+def weights_body(own, enc_ref, point_ref, lanes_ref, place_ref, high_ref, low_ref):
+    high, low = split(enc_ref[...])
+    pointed = dot(high, point_ref[...]) + dot(low, point_ref[...])
     turned = jnp.concatenate([pointed[:16], jnp.zeros((112, C), F32)], axis=0).T
     scaled = turned * (1.0 / VELOCITY_SCALE)
     for e in range(8):
@@ -795,26 +800,24 @@
     gathered = gather_z(sent)
 
     late_bias, _ = lax.optimization_barrier((layer_bias[None], sent))
-    planes, wk, vectors, placed, spread_high, spread_low, pairs = call(
+    planes, wk, vectors, pairs = call(
         planes_body, 2,
         (
             shaped((ROWS, 16, GW)), shaped((48, C), BF16), shaped((3, C, 128)),
-            shaped((8, 128, 128), BF16), shaped((KOWN, 128, 128), BF16),
-            shaped((KOWN, 128, 128), BF16), shaped((144,), jnp.int32),
+            shaped((144,), jnp.int32),
         ),
         [
             full_spec(fine), full_spec((512, 512)), full_spec((16, C)), row_spec, row_spec,
-            full_spec((C, C)), row_spec, row_spec, full_spec((KOWN * 2, 128, 128)),
+            full_spec((C, C)), row_spec, row_spec,
         ],
         (
             full_spec((ROWS, 16, GW)), full_spec((48, C)), full_spec((3, C, 128)),
-            full_spec((8, 128, 128)), full_spec((KOWN, 128, 128)), full_spec((KOWN, 128, 128)),
             pl.BlockSpec(memory_space=pltpu.SMEM),
         ),
         [pltpu.VMEM((128, 512), F32)], name="velocity_planes",
     )(
         own, receiver_rows, velocity, jnp.asarray(SELECT), encoder, bias, amplitude, point_weight, late_bias,
-        out_weight[None], jnp.asarray(LANES),
+        out_weight[None],
     )
 
     gathered, planes = lax.optimization_barrier((gathered, planes))
@@ -839,6 +842,14 @@
     )(own, pairs, gathered, others, planes, table, wk, bumps, vectors, record)
     stats = lax.all_to_all(stats, "space", 0, 0, tiled=True)
 
+    late_encoder, _ = lax.optimization_barrier((encoder, predicted))
+    placed, spread_high, spread_low = call(
+        weights_body, 1,
+        (shaped((8, 128, 128), BF16),) + (shaped((KOWN, 128, 128), BF16),) * 2,
+        [full_spec((16, C)), full_spec((C, C)), full_spec((KOWN * 2, 128, 128))],
+        (full_spec((8, 128, 128)), full_spec((KOWN, 128, 128)), full_spec((KOWN, 128, 128))),
+        name="point_weights",
+    )(own, late_encoder, point_weight, jnp.asarray(LANES))
     columns, near, after, far, last, misfits = call(
         backward_body, 3,
         (shaped((SPACE, ROWS, 384), BF16),) + (shaped((GW, 128), BF16),) * 4 + (shaped((8, 128)),),

time: 122 us -> 122 us (level)
  waiting for transfers between devices: 22.6 us -> 18.3 us
  starting transfers between devices: 52.3 us -> 54.3 us
  Pallas kernels: 32.9 us -> 34.6 us
    all_to_all x1, waiting for transfers between devices: 4.82 us -> 2.73 us  [shards(): stats = lax.all_to_all(stats, 'space', 0, 0, tiled=True)]
    pallas_call x0 -> x1, Pallas kernels: none -> 2.07 us  [shards(): call(weights_body, 1, (shaped((8, 128, 128), BF16),) + (shaped((KOWN, 128...]
    ppermute x1, starting transfers between devices: 3.38 us -> 5.26 us  [shards(): lax.ppermute(sent, 'shot', turn(2, 16, SHOT, 1))]
    ppermute x1, waiting for transfers between devices: 3.82 us -> 1.97 us  [shards(): lax.ppermute(sent, 'shot', turn(2, 16, SHOT, 1))]
  transfers between devices with their start and end apart: 19 -> 19, of which waited for: 13 -> 13; matrix products, arithmetic and copies ran while one was open for 1% -> 1% of each run, Pallas kernels for 9% -> 10%
where the time goes in v5:
time: 122 us; the launch traced here: 121 us
  starting transfers between devices  54.3 us (45%)
  Pallas kernels  34.6 us (28%)
  waiting for transfers between devices  18.3 us (15%)
  blocking collectives  8.67 us (7%)
  local copies, waits for them, and re-layouts  4.58 us (4%)
    ppermute x2, starting transfers between devices, from_core(): return lax.ppermute(values, 'space', [(n, n ^ 1) for n in range(SPACE)])  12.3 us
    ppermute x6, starting transfers between devices, from_y(): lax.ppermute(part, 'shot', turn(4, 4, SHOT, by + 1))  9.52 us
    ppermute x6, starting transfers between devices, from_x(): lax.ppermute(part, 'shot', turn(4, 1, SHOT, by + 1))  8.81 us
    all_to_all x1, blocking collectives, gather_z(): lax.all_to_all(copies, 'space', 0, 0, axis_index_groups=[[0, 2, 4, 6], [1...  8.67 us
    all_to_all x1, starting transfers between devices, shards(): spectra = lax.all_to_all(partial, 'space', 0, 0, tiled=True)  7.4 us
    pallas_call x1, Pallas kernels, shards(): call(forward_body, 2, (shaped((PAIRS, GW)), shaped((PAIRS * C, GW), BF16)...  6.39 us
    ppermute x6, waiting for transfers between devices, from_x(): lax.ppermute(part, 'shot', turn(4, 1, SHOT, by + 1))  5.88 us
    pallas_call x1, Pallas kernels, shards(): call(backward_body, 3, (shaped((SPACE, ROWS, 384), BF16),) + (shaped((GW,...  5.81 us
  transfers between devices with their start and end apart: 19, of which 13 were waited for; matrix products, arithmetic and copies ran while one was open for 1% of the time, Pallas kernels for 10%

profile of v5, /device:TPU:1, one launch (start us, length us, event | category | flops | bytes accessed | tf_op | source)
XLA Modules:
  0.0 121.3 jit_solution(7124025881728372438)
XLA Ops:
  0.6 3.3 %velocity_spectrum.1 = f32[8,48,128]{2,1,0:T(8,128)} custom-call(s32[1]{0:T(128)} %bitcast.own, f32[128,2048]{1,0:T(8,128)} %v_ref.3, bf16[2048,256]{1,0:T(8,128)(2,1)} %constant.51.clone.cols_ref, bf16[8,192,256]{2,1,0:T(8,128)(2,1)} %constant.52.clone.rows_ref), custom_call_target="tpu_custom_call" | custom-call | tf_op jit(solution)/shard_map/velocity_spectrum/pallas_call | solution.py:769
  3.9 7.4 %all-to-all-start = ((f32[8,48,128]{2,1,0:T(8,128)}), f32[8,48,128]{2,1,0:T(8,128)S(1)}, u32[]{:S(2)}, u32[]{:S(2)}) async-start(f32[8,48,128]{2,1,0:T(8,128)} %velocity_spectrum.1), calls=%async_computation | async-start | bytes 393216 | tf_op jit(solution)/shard_map/all_to_all | solution.py:774
  11.3 5.7 %operator.1 = (f32[3456,128]{1,0:T(8,128)}, bf16[3,64,256]{2,1,0:T(8,128)(2,1)}, f32[64,512]{1,0:T(8,128)}) custom-call(s32[1]{0:T(128)} %bitcast.own, s32[4]{0:T(128)} %source_row.1, s32[4]{0:T(128)} %source_column.1, f32[16,64]{1,0:T(8,128)} %bitcast.14, f32[1,64]{1,0:T(1,128)} %bitcast.17, f32[1,64]{1,0:T(1,128)} %bitcast.19, ...), custom_call_target="tpu_custom_call" | custom-call | tf_op jit(solution)/shard_map/operator/pallas_call | solution.py:777
  18.4 3.8 %mix_modes.1 = bf16[4,64,384]{2,1,0:T(8,128)(2,1)} custom-call(s32[1]{0:T(128)} %bitcast.own, f32[8,48,128]{2,1,0:T(8,128)} %copy-done.14, f32[8,48,128]{2,1,0:T(8,128)} %constant.55.clone.ones_ref, f32[3456,128]{1,0:T(8,128)} %get-tuple-element.52.t_ref, bf16[3,64,256]{2,1,0:T(8,128)(2,1)} %get-tuple-element.53.l_ref), custom_call_target="tpu_custom_call" | custom-call | tf_op jit(solution)/shard_map/mix_modes/pallas_call | solution.py:792
  22.2 3.7 %all-to-all-start.1 = ((bf16[4,64,384]{2,1,0:T(8,128)(2,1)}), bf16[4,64,384]{2,1,0:T(8,128)(2,1)S(1)}, u32[]{:S(2)}, u32[]{:S(2)}) async-start(bf16[4,64,384]{2,1,0:T(8,128)(2,1)} %mix_modes.1), calls=%async_computation.1 | async-start | bytes 393216 | tf_op jit(solution)/shard_map/all_to_all | solution.py:734
  25.9 4.0 %velocity_planes.1 = (f32[32,16,512]{2,1,0:T(8,128)}, bf16[48,64]{1,0:T(8,128)(2,1)}, f32[3,64,128]{2,1,0:T(8,128)}, s32[144]{0:T(256)}) custom-call(s32[1]{0:T(128)} %bitcast.own, s32[4,16]{1,0:T(4,128)} %rows_ref.4, f32[128,2048]{1,0:T(8,128)} %v_ref.3, bf16[512,512]{1,0:T(8,128)(2,1)} %constant.56.clone.sel_ref, f32[16,64]{1,0:T(8,128)} %bitcast.15, ...), custom_call_target="tpu_custom_call" | custom-call | tf_op jit(solution)/shard_map/velocity_planes/pallas_call | solution.py:803
  31.1 3.6 %collective-permute-start = (bf16[4,64,384]{2,1,0:T(8,128)(2,1)S(1)}, bf16[4,64,384]{2,1,0:T(8,128)(2,1)S(1)}, u32[]{:S(2)}, u32[]{:S(2)}) collective-permute-start(bf16[4,64,384]{2,1,0:T(8,128)(2,1)S(1)} %all-to-all-done.1.d_ref), channel_id=1, source_target_pairs={{0,1},{1,0},{2,3},{3,2},{4,5},{5,4},{6,7},{7,6},{8,9},{9,8},{10,11... | collective-permute-start | bytes 589832 | tf_op jit(solution)/shard_map/ppermute | solution.py:740
  36.5 6.4 %forward_rows.1 = (f32[64,512]{1,0:T(8,128)}, bf16[4096,512]{1,0:T(8,128)(2,1)}, f32[8,8,128]{2,1,0:T(8,128)}) custom-call(s32[1]{0:T(128)} %bitcast.own, s32[144]{0:T(256)} %get-tuple-element.55.list_ref, bf16[4,64,384]{2,1,0:T(8,128)(2,1)} %copy-done.13, bf16[4,64,384]{2,1,0:T(8,128)(2,1)} %copy-done.15, f32[32,16,512]{2,1,0:T(8,128)} %get-tuple-element.58.planes_ref, ...), custom_call_target="tpu_custom_call" | custom-call | tf_op jit(solution)/shard_map/forward_rows/pallas_call | solution.py:825
  42.9 3.4 %all-to-all-start.2 = ((f32[8,8,128]{2,1,0:T(8,128)}), f32[8,8,128]{2,1,0:T(8,128)S(1)}, u32[]{:S(2)}, u32[]{:S(2)}) async-start(f32[8,8,128]{2,1,0:T(8,128)} %get-tuple-element.62), calls=%async_computation.2 | async-start | bytes 65536 | tf_op jit(solution)/shard_map/all_to_all | solution.py:843
  46.3 2.1 %point_weights.1 = (bf16[8,128,128]{2,1,0:T(8,128)(2,1)}, bf16[3,128,128]{2,1,0:T(8,128)(2,1)}, bf16[3,128,128]{2,1,0:T(8,128)(2,1)}) custom-call(s32[1]{0:T(128)} %bitcast.own, f32[16,64]{1,0:T(8,128)} %bitcast.16, bf16[64,64]{1,0:T(8,128)(2,1)} %point_ref.3, bf16[6,128,128]{2,1,0:T(8,128)(2,1)} %constant.57.clone.lanes_ref), custom_call_target="tpu_custom_call" | custom-call | tf_op jit(solution)/shard_map/point_weights/pallas_call | solution.py:846
  48.4 2.7 %all-to-all-done.2.stats_ref = f32[8,8,128]{2,1,0:T(8,128)S(1)} async-done(((f32[8,8,128]{2,1,0:T(8,128)}), f32[8,8,128]{2,1,0:T(8,128)S(1)}, u32[]{:S(2)}, u32[]{:S(2)}) %all-to-all-start.2) | async-done | bytes 32800 | tf_op jit(solution)/shard_map/all_to_all | solution.py:843
  51.8 5.8 %backward_rows.1 = (bf16[8,32,384]{2,1,0:T(8,128)(2,1)}, bf16[512,128]{1,0:T(8,128)(2,1)}, bf16[512,128]{1,0:T(8,128)(2,1)}, bf16[512,128]{1,0:T(8,128)(2,1)}, b...) custom-call(s32[1]{0:T(128)} %bitcast.own, s32[144]{0:T(256)} %get-tuple-element.55.list_ref, s32[1]{0:T(128)} %bitcast.1.shot, ...), custom_call_target="tpu_custom_call" | custom-call | tf_op jit(solution)/shard_map/backward_rows/pallas_call | solution.py:853
  57.6 3.8 %all-to-all-start.3 = ((bf16[8,32,384]{2,1,0:T(8,128)(2,1)}), bf16[8,32,384]{2,1,0:T(8,128)(2,1)S(1)}, u32[]{:S(2)}, u32[]{:S(2)}) async-start(bf16[8,32,384]{2,1,0:T(8,128)(2,1)} %get-tuple-element.82), calls=%async_computation.3 | async-start | bytes 393216 | tf_op jit(solution)/shard_map/all_to_all | solution.py:870
  61.8 3.3 %collective-permute-start.2 = (bf16[512,128]{1,0:T(8,128)(2,1)}, bf16[512,128]{1,0:T(8,128)(2,1)S(1)}, u32[]{:S(2)}, u32[]{:S(2)}) collective-permute-start(bf16[512,128]{1,0:T(8,128)(2,1)} %get-tuple-element.72), channel_id=1, source_target_pairs={{0,16},{8,24},{16,0},{24,8},{32,48},{40,56},{48,32},{56,40},{64,80... | collective-permute-start | bytes 393224 | tf_op jit(solution)/shard_map/ppermute | solution.py:723
  67.7 3.8 %collective-permute-done.2.c_ref = bf16[512,128]{1,0:T(8,128)(2,1)S(1)} collective-permute-done((bf16[512,128]{1,0:T(8,128)(2,1)}, bf16[512,128]{1,0:T(8,128)(2,1)S(1)}, u32[]{:S(2)}, u32[]{:S(2)}) %collective-permute-start.2) | collective-permute-done | bytes 131104 | tf_op jit(solution)/shard_map/ppermute | solution.py:723
  71.6 3.0 %collective-permute-start.4 = (bf16[128,128]{1,0:T(8,128)(2,1)S(1)}, bf16[128,128]{1,0:T(8,128)(2,1)S(1)}, u32[]{:S(2)}, u32[]{:S(2)}) collective-permute-start(bf16[128,128]{1,0:T(8,128)(2,1)S(1)} %get-tuple-element.79), channel_id=1, source_target_pairs={{0,32},{8,40},{16,48},{24,56},{32,64},{40,72},{48,80},{56,88},{64,... | collective-permute-start | bytes 98312 | tf_op jit(solution)/shard_map/ppermute | solution.py:729
  75.6 1.5 %collective-permute-start.6 = (bf16[128,128]{1,0:T(8,128)(2,1)S(1)}, bf16[128,128]{1,0:T(8,128)(2,1)S(1)}, u32[]{:S(2)}, u32[]{:S(2)}) collective-permute-start(bf16[128,128]{1,0:T(8,128)(2,1)S(1)} %get-tuple-element.81), channel_id=1, source_target_pairs={{0,96},{8,104},{16,112},{24,120},{32,0},{40,8},{48,16},{56,24},{64... | collective-permute-start | bytes 98312 | tf_op jit(solution)/shard_map/ppermute | solution.py:729
  79.0 5.3 %collective-permute-start.7 = (bf16[272,128]{1,0:T(8,128)(2,1)S(1)}, bf16[272,128]{1,0:T(8,128)(2,1)S(1)}, u32[]{:S(2)}, u32[]{:S(2)}) collective-permute-start(bf16[272,128]{1,0:T(8,128)(2,1)S(1)} %get-tuple-element.84), channel_id=1, source_target_pairs={{0,128},{8,136},{16,144},{24,152},{32,160},{40,168},{48,176},{56,1... | collective-permute-start | bytes 208904 | tf_op jit(solution)/shard_map/ppermute | solution.py:899
  84.2 2.0 %collective-permute-done.7.b_ref = bf16[272,128]{1,0:T(8,128)(2,1)S(1)} collective-permute-done((bf16[272,128]{1,0:T(8,128)(2,1)S(1)}, bf16[272,128]{1,0:T(8,128)(2,1)S(1)}, u32[]{:S(2)}, u32[]{:S(2)}) %collective-permute-start.7) | collective-permute-done | bytes 69664 | tf_op jit(solution)/shard_map/ppermute | solution.py:899
  86.2 3.2 %collective-permute-start.10 = (bf16[160,128]{1,0:T(8,128)(2,1)S(1)}, bf16[160,128]{1,0:T(8,128)(2,1)S(1)}, u32[]{:S(2)}, u32[]{:S(2)}) collective-permute-start(bf16[160,128]{1,0:T(8,128)(2,1)S(1)} %get-tuple-element.86), channel_id=1, source_target_pairs={{0,24},{8,0},{16,8},{24,16},{32,56},{40,32},{48,40},{56,48},{64,88... | collective-permute-start | bytes 122888 | tf_op jit(solution)/shard_map/ppermute | solution.py:723
  94.2 3.3 %collective-permute-start.12 = (bf16[160,128]{1,0:T(8,128)(2,1)S(1)}, bf16[160,128]{1,0:T(8,128)(2,1)S(1)}, u32[]{:S(2)}, u32[]{:S(2)}) collective-permute-start(bf16[160,128]{1,0:T(8,128)(2,1)S(1)} %get-tuple-element.92), channel_id=1, source_target_pairs={{0,64},{8,72},{16,80},{24,88},{32,96},{40,104},{48,112},{56,120},{... | collective-permute-start | bytes 122888 | tf_op jit(solution)/shard_map/ppermute | solution.py:729
  101.2 8.7 %all_to_all.25.m_ref = f32[4,56,128]{2,1,0:T(8,128)S(1)} all-to-all(f32[4,56,128]{2,1,0:T(8,128)S(1)} %adjoint_mix.1), channel_id=1, replica_groups={{0,2,4,6},{1,3,5,7},{8,10,12,14},{9,11,13,15},{16,18,20,22},{17,19,21,2..., dimensions={0} | all-to-all | bytes 229376 | tf_op jit(solution)/shard_map/all_to_all | solution.py:734
  109.9 8.7 %collective-permute-start.14 = (f32[4,56,128]{2,1,0:T(8,128)S(1)}, f32[4,56,128]{2,1,0:T(8,128)S(1)}, u32[]{:S(2)}, u32[]{:S(2)}) collective-permute-start(f32[4,56,128]{2,1,0:T(8,128)S(1)} %all_to_all.25.m_ref), channel_id=1, source_target_pairs={{0,1},{1,0},{2,3},{3,2},{4,5},{5,4},{6,7},{7,6},{8,9},{9,8},{10,11... | collective-permute-start | bytes 344072 | tf_op jit(solution)/shard_map/ppermute | solution.py:740
  119.6 1.7 %output_block.1 = (f32[64,128]{1,0:T(8,128)}, f32[1,4]{1,0:T(1,128)}) custom-call(s32[1]{0:T(128)} %bitcast.own, f32[4,56,128]{2,1,0:T(8,128)S(1)} %all_to_all.25.m_ref, f32[4,56,128]{2,1,0:T(8,128)S(1)} %collective-permute-done.14.other_ref, bf16[8,32,96]{2,1,0:T(8,128)(2,1)S(1)} %copy-done.6, bf16[1024,64]{1,0:T(8,128)(2,1)S(1)} %dynamic-slice_bitcast_fusion.block_ref, ...), custom_call_target="tpu_custom_call" | custom-call | tf_op jit(solution)/shard_map/output_block/pallas_call | solution.py:924
  (66 shorter events, 20.4 us)
Async XLA Ops:
  3.9 13.9 %all-to-all-start = ((f32[8,48,128]{2,1,0:T(8,128)}), f32[8,48,128]{2,1,0:T(8,128)S(1)}, u32[]{:S(2)}, u32[]{:S(2)}) async-start(f32[8,48,128]{2,1,0:T(8,128)} %velocity_spectrum.1), calls=%async_computation | async-start | bytes 393216 | tf_op jit(solution)/shard_map/all_to_all | solution.py:774
  22.2 8.9 %all-to-all-start.1 = ((bf16[4,64,384]{2,1,0:T(8,128)(2,1)}), bf16[4,64,384]{2,1,0:T(8,128)(2,1)S(1)}, u32[]{:S(2)}, u32[]{:S(2)}) async-start(bf16[4,64,384]{2,1,0:T(8,128)(2,1)} %mix_modes.1), calls=%async_computation.1 | async-start | bytes 393216 | tf_op jit(solution)/shard_map/all_to_all | solution.py:734
  31.1 4.7 %collective-permute-start = (bf16[4,64,384]{2,1,0:T(8,128)(2,1)S(1)}, bf16[4,64,384]{2,1,0:T(8,128)(2,1)S(1)}, u32[]{:S(2)}, u32[]{:S(2)}) collective-permute-start(bf16[4,64,384]{2,1,0:T(8,128)(2,1)S(1)} %all-to-all-done.1.d_ref), channel_id=1, source_target_pairs={{0,1},{1,0},{2,3},{3,2},{4,5},{5,4},{6,7},{7,6},{8,9},{9,8},{10,11... | collective-permute-start | bytes 589832 | tf_op jit(solution)/shard_map/ppermute | solution.py:740
  42.9 57.4 %copy-start = (f32[3456,128]{1,0:T(8,128)S(1)}, f32[3456,128]{1,0:T(8,128)}, u32[]{:S(2)}) copy-start(f32[3456,128]{1,0:T(8,128)} %get-tuple-element.52.t_ref) | copy-start | bytes 5308420
  42.9 8.3 %all-to-all-start.2 = ((f32[8,8,128]{2,1,0:T(8,128)}), f32[8,8,128]{2,1,0:T(8,128)S(1)}, u32[]{:S(2)}, u32[]{:S(2)}) async-start(f32[8,8,128]{2,1,0:T(8,128)} %get-tuple-element.62), calls=%async_computation.2 | async-start | bytes 65536 | tf_op jit(solution)/shard_map/all_to_all | solution.py:843
  51.8 67.8 %copy-start.6 = (bf16[8,32,96]{2,1,0:T(8,128)(2,1)S(1)}, bf16[8,32,96]{2,1,0:T(8,128)(2,1)}, u32[]{:S(2)}) copy-start(bf16[8,32,96]{2,1,0:T(8,128)(2,1)} %constant.61.clone.back_ref) | copy-start | bytes 147460
  51.8 67.8 %copy-start.8 = (f32[96,128]{1,0:T(8,128)S(1)}, f32[96,128]{1,0:T(8,128)}, u32[]{:S(2)}) copy-start(f32[96,128]{1,0:T(8,128)} %constant.62.clone.diag_rows_ref) | copy-start | bytes 147460
  51.8 67.8 %copy-start.9 = (bf16[96,96]{1,0:T(8,128)(2,1)S(1)}, bf16[96,96]{1,0:T(8,128)(2,1)}, u32[]{:S(2)}) copy-start(bf16[96,96]{1,0:T(8,128)(2,1)} %constant.63.clone.off_rows_ref) | copy-start | bytes 55300
  51.8 67.8 %copy-start.11 = (f32[1,1024]{1,0:T(1,128)S(1)}, f32[1,1024]{1,0:T(1,128)}, u32[]{:S(2)}) copy-start(f32[1,1024]{1,0:T(1,128)} %constant.64.clone.diag_ref) | copy-start | bytes 12292
  57.6 19.6 %all-to-all-start.3 = ((bf16[8,32,384]{2,1,0:T(8,128)(2,1)}), bf16[8,32,384]{2,1,0:T(8,128)(2,1)S(1)}, u32[]{:S(2)}, u32[]{:S(2)}) async-start(bf16[8,32,384]{2,1,0:T(8,128)(2,1)} %get-tuple-element.82), calls=%async_computation.3 | async-start | bytes 393216 | tf_op jit(solution)/shard_map/all_to_all | solution.py:870
  61.4 6.3 %collective-permute-start.1 = (bf16[512,128]{1,0:T(8,128)(2,1)}, bf16[512,128]{1,0:T(8,128)(2,1)S(1)}, u32[]{:S(2)}, u32[]{:S(2)}) collective-permute-start(bf16[512,128]{1,0:T(8,128)(2,1)} %get-tuple-element.71), channel_id=1, source_target_pairs={{0,8},{8,16},{16,24},{24,0},{32,40},{40,48},{48,56},{56,32},{64,72... | collective-permute-start | bytes 393224 | tf_op jit(solution)/shard_map/ppermute | solution.py:723
  61.8 9.7 %collective-permute-start.2 = (bf16[512,128]{1,0:T(8,128)(2,1)}, bf16[512,128]{1,0:T(8,128)(2,1)S(1)}, u32[]{:S(2)}, u32[]{:S(2)}) collective-permute-start(bf16[512,128]{1,0:T(8,128)(2,1)} %get-tuple-element.72), channel_id=1, source_target_pairs={{0,16},{8,24},{16,0},{24,8},{32,48},{40,56},{48,32},{56,40},{64,80... | collective-permute-start | bytes 393224 | tf_op jit(solution)/shard_map/ppermute | solution.py:723
  65.0 6.5 %collective-permute-start.3 = (bf16[512,128]{1,0:T(8,128)(2,1)}, bf16[512,128]{1,0:T(8,128)(2,1)S(1)}, u32[]{:S(2)}, u32[]{:S(2)}) collective-permute-start(bf16[512,128]{1,0:T(8,128)(2,1)} %get-tuple-element.73), channel_id=1, source_target_pairs={{0,24},{8,0},{16,8},{24,16},{32,56},{40,32},{48,40},{56,48},{64,88... | collective-permute-start | bytes 393224 | tf_op jit(solution)/shard_map/ppermute | solution.py:723
  71.6 5.8 %collective-permute-start.4 = (bf16[128,128]{1,0:T(8,128)(2,1)S(1)}, bf16[128,128]{1,0:T(8,128)(2,1)S(1)}, u32[]{:S(2)}, u32[]{:S(2)}) collective-permute-start(bf16[128,128]{1,0:T(8,128)(2,1)S(1)} %get-tuple-element.79), channel_id=1, source_target_pairs={{0,32},{8,40},{16,48},{24,56},{32,64},{40,72},{48,80},{56,88},{64,... | collective-permute-start | bytes 98312 | tf_op jit(solution)/shard_map/ppermute | solution.py:729
  74.7 4.3 %collective-permute-start.5 = (bf16[128,128]{1,0:T(8,128)(2,1)S(1)}, bf16[128,128]{1,0:T(8,128)(2,1)S(1)}, u32[]{:S(2)}, u32[]{:S(2)}) collective-permute-start(bf16[128,128]{1,0:T(8,128)(2,1)S(1)} %get-tuple-element.80), channel_id=1, source_target_pairs={{0,64},{8,72},{16,80},{24,88},{32,96},{40,104},{48,112},{56,120},{... | collective-permute-start | bytes 98312 | tf_op jit(solution)/shard_map/ppermute | solution.py:729
  75.6 3.3 %collective-permute-start.6 = (bf16[128,128]{1,0:T(8,128)(2,1)S(1)}, bf16[128,128]{1,0:T(8,128)(2,1)S(1)}, u32[]{:S(2)}, u32[]{:S(2)}) collective-permute-start(bf16[128,128]{1,0:T(8,128)(2,1)S(1)} %get-tuple-element.81), channel_id=1, source_target_pairs={{0,96},{8,104},{16,112},{24,120},{32,0},{40,8},{48,16},{56,24},{64... | collective-permute-start | bytes 98312 | tf_op jit(solution)/shard_map/ppermute | solution.py:729
  79.0 7.2 %collective-permute-start.7 = (bf16[272,128]{1,0:T(8,128)(2,1)S(1)}, bf16[272,128]{1,0:T(8,128)(2,1)S(1)}, u32[]{:S(2)}, u32[]{:S(2)}) collective-permute-start(bf16[272,128]{1,0:T(8,128)(2,1)S(1)} %get-tuple-element.84), channel_id=1, source_target_pairs={{0,128},{8,136},{16,144},{24,152},{32,160},{40,168},{48,176},{56,1... | collective-permute-start | bytes 208904 | tf_op jit(solution)/shard_map/ppermute | solution.py:899
  86.2 6.3 %collective-permute-start.10 = (bf16[160,128]{1,0:T(8,128)(2,1)S(1)}, bf16[160,128]{1,0:T(8,128)(2,1)S(1)}, u32[]{:S(2)}, u32[]{:S(2)}) collective-permute-start(bf16[160,128]{1,0:T(8,128)(2,1)S(1)} %get-tuple-element.86), channel_id=1, source_target_pairs={{0,24},{8,0},{16,8},{24,16},{32,56},{40,32},{48,40},{56,48},{64,88... | collective-permute-start | bytes 122888 | tf_op jit(solution)/shard_map/ppermute | solution.py:723
  89.5 4.5 %collective-permute-start.8 = (bf16[160,128]{1,0:T(8,128)(2,1)S(1)}, bf16[160,128]{1,0:T(8,128)(2,1)S(1)}, u32[]{:S(2)}, u32[]{:S(2)}) collective-permute-start(bf16[160,128]{1,0:T(8,128)(2,1)S(1)} %get-tuple-element.86), channel_id=1, source_target_pairs={{0,8},{8,16},{16,24},{24,0},{32,40},{40,48},{48,56},{56,32},{64,72... | collective-permute-start | bytes 122888 | tf_op jit(solution)/shard_map/ppermute | solution.py:723
  89.5 4.5 %collective-permute-start.9 = (bf16[160,128]{1,0:T(8,128)(2,1)S(1)}, bf16[160,128]{1,0:T(8,128)(2,1)S(1)}, u32[]{:S(2)}, u32[]{:S(2)}) collective-permute-start(bf16[160,128]{1,0:T(8,128)(2,1)S(1)} %get-tuple-element.86), channel_id=1, source_target_pairs={{0,16},{8,24},{16,0},{24,8},{32,48},{40,56},{48,32},{56,40},{64,80... | collective-permute-start | bytes 122888 | tf_op jit(solution)/shard_map/ppermute | solution.py:723
  94.0 4.1 %collective-permute-start.11 = (bf16[160,128]{1,0:T(8,128)(2,1)S(1)}, bf16[160,128]{1,0:T(8,128)(2,1)S(1)}, u32[]{:S(2)}, u32[]{:S(2)}) collective-permute-start(bf16[160,128]{1,0:T(8,128)(2,1)S(1)} %get-tuple-element.92), channel_id=1, source_target_pairs={{0,32},{8,40},{16,48},{24,56},{32,64},{40,72},{48,80},{56,88},{64,... | collective-permute-start | bytes 122888 | tf_op jit(solution)/shard_map/ppermute | solution.py:729
  94.2 5.1 %collective-permute-start.12 = (bf16[160,128]{1,0:T(8,128)(2,1)S(1)}, bf16[160,128]{1,0:T(8,128)(2,1)S(1)}, u32[]{:S(2)}, u32[]{:S(2)}) collective-permute-start(bf16[160,128]{1,0:T(8,128)(2,1)S(1)} %get-tuple-element.92), channel_id=1, source_target_pairs={{0,64},{8,72},{16,80},{24,88},{32,96},{40,104},{48,112},{56,120},{... | collective-permute-start | bytes 122888 | tf_op jit(solution)/shard_map/ppermute | solution.py:729
  97.5 2.9 %collective-permute-start.13 = (bf16[160,128]{1,0:T(8,128)(2,1)S(1)}, bf16[160,128]{1,0:T(8,128)(2,1)S(1)}, u32[]{:S(2)}, u32[]{:S(2)}) collective-permute-start(bf16[160,128]{1,0:T(8,128)(2,1)S(1)} %get-tuple-element.92), channel_id=1, source_target_pairs={{0,96},{8,104},{16,112},{24,120},{32,0},{40,8},{48,16},{56,24},{64... | collective-permute-start | bytes 122888 | tf_op jit(solution)/shard_map/ppermute | solution.py:729
  109.9 9.7 %collective-permute-start.14 = (f32[4,56,128]{2,1,0:T(8,128)S(1)}, f32[4,56,128]{2,1,0:T(8,128)S(1)}, u32[]{:S(2)}, u32[]{:S(2)}) collective-permute-start(f32[4,56,128]{2,1,0:T(8,128)S(1)} %all_to_all.25.m_ref), channel_id=1, source_target_pairs={{0,1},{1,0},{2,3},{3,2},{4,5},{5,4},{6,7},{7,6},{8,9},{9,8},{10,11... | collective-permute-start | bytes 344072 | tf_op jit(solution)/shard_map/ppermute | solution.py:740
  (12 other events, 292.9 us)
